TPU v7x, 32 devices: a whole 2x2x4 slice. The times are simulated.
32 devices in a mesh: blk: 4 (over x, core), uly: 8 (over z, y).
Axes of the slice: x: 2, y: 2, z: 4, core: 2. Of those that a mesh axis runs over, the one named last changes fastest.
Arguments:
- residual: bfloat16 [2, 2048, 1024], P(None, ('uly', 'blk')), may hold values from -6 to 6
- cotangent: bfloat16 [2, 2048, 1024], P(None, ('uly', 'blk')), may hold values from -6 to 6
- lengths: int32 [2], replicated, may hold values from 512 to 2048, as said below
- positions: int32 [2, 2048], P(None, ('uly', 'blk')), may hold values from 0 to 2047, as said below
- masters: float32 [12596224], P(('blk', 'uly')), may hold values from -2 to 2
- momenta: float32 [12596224], P(('blk', 'uly')), may hold values from -102.4 to 102.4
- averages: float32 [12596224], P(('blk', 'uly')), may hold values from -2 to 2
Outputs:
- block_output: bfloat16 [2, 2048, 1024], P(None, ('uly', 'blk'))
- input_gradient: bfloat16 [2, 2048, 1024], P(None, ('uly', 'blk'))
- gradients: float32 [12596224], P(('blk', 'uly'))
- updated_masters: float32 [12596224], P(('blk', 'uly'))
- updated_momenta: float32 [12596224], P(('blk', 'uly'))
- updated_averages: float32 [12596224], P(('blk', 'uly'))
Inputs may be any that keep to these rules, and one draw needn't show every extreme that they name: `lengths`: in every draw some slot is live over all 2048 positions; tokens at or past a slot's length are padding. Each slot's positions start at 0, restart at 0 at the first token of each packed document, and otherwise rise by one per token; the first slot holds a single document, every other slot two or more.
All inputs are finite; a program needn't handle non-finite values.
Results may differ from a plain program's by a relative error of at most 0.014.
The roundings to bfloat16 on the way count: a program that leaves them out, or rounds other values in their place, can miss the bound.
Values may be sent and summed in bfloat16 or wider, within the bound.
No kernel may reach another device: no remote copies, remote signals or barrier semaphores. Data moves between devices by JAX's collectives and lax.ppermute only.
A program may use at most 256 MiB of HBM per device.

v0:
```python
from functools import partial
import math

import jax
import jax.numpy as jnp
from jax import lax
from jax.sharding import PartitionSpec as P

D = 1024
H = 16
HD = 64
ROT = 16
FF = 4096


EPSILON = 1e-05
NEGATIVE = -1e30
MOMENTUM = 0.5
LEARN_RATE = 0.05
AVERAGE_DECAY = 0.5
ROTARY_BASE = 10000.0


def passed_along(block, axis, distance):
    devices = range(lax.axis_size(axis))
    route = [((i - distance) % len(devices), i) for i in devices]
    return lax.ppermute(block, axis, route)


def unpack(flat_vector):
    layouts = [
        (D,),
        (D,),
        (D,),
        (D,),
        (D, 3 * D),
        (3 * D,),
        (D, D),
        (D,),
        (D, FF),
        (FF,),
        (FF, D),
        (D,),
    ]
    pieces = []
    cursor = 0
    for layout in layouts:
        number = math.prod(layout)
        pieces.append(flat_vector[cursor : cursor + number].reshape(layout))
        cursor += number
    return pieces


def layer_norm(values, gain, shift):
    centered = values - jnp.mean(values, axis=-1, keepdims=True)
    variance = jnp.mean(centered * centered, axis=-1, keepdims=True)
    return centered * lax.rsqrt(variance + EPSILON) * gain + shift


def rotary_tables(positions):
    half_dims = ROT // 2
    inverse = ROTARY_BASE ** (-(jnp.arange(half_dims, dtype=jnp.float32) * 2.0 / ROT))
    angles = positions.astype(jnp.float32)[..., None] * inverse
    return (jnp.cos(angles), jnp.sin(angles))


def rotate(values, cos_table, sin_table):
    half_dims = ROT // 2
    first_half = values[..., :half_dims]
    second_half = values[..., half_dims:ROT]
    return jnp.concatenate(
        [
            first_half * cos_table - second_half * sin_table,
            second_half * cos_table + first_half * sin_table,
            values[..., ROT:],
        ],
        axis=-1,
    )


def group_tokens(source, group_count, uly_count, span_rows):
    spans = jnp.arange(uly_count, dtype=jnp.int32)[:, None] * group_count + source
    return (spans * span_rows + jnp.arange(span_rows, dtype=jnp.int32)[None, :]).reshape(-1)


def block_scores(queries, keys_rows, row_tokens, col_tokens, length):
    scores = jnp.einsum(
        "qhd,khd->hqk", queries, keys_rows, preferred_element_type=jnp.float32
    ) * HD ** (-0.5)
    allowed = (col_tokens[None, :] <= row_tokens[:, None]) & (col_tokens[None, :] < length)
    return jnp.where(allowed[None], scores, NEGATIVE)


def is_live(row_tokens, col_tokens, length):
    return (col_tokens[0] <= row_tokens[-1]) & (col_tokens[0] < length)


def fold_stats(row_max, row_total, queries, key_value, lengths, row_tokens, col_tokens):

    def per_slot(inputs):
        slot_max, slot_total, slot_queries, slot_pairs, length = inputs

        def compute(current):
            prev_max, prev_total = current
            scores = block_scores(slot_queries, slot_pairs[:, :, 0], row_tokens, col_tokens, length)
            next_max = jnp.maximum(prev_max, jnp.max(scores, axis=-1))
            next_total = prev_total * jnp.exp(prev_max - next_max) + jnp.sum(
                jnp.exp(scores - next_max[..., None]), axis=-1
            )
            return (next_max, next_total)

        return lax.cond(
            is_live(row_tokens, col_tokens, length),
            compute,
            lambda current: current,
            (slot_max, slot_total),
        )

    return lax.map(per_slot, (row_max, row_total, queries, key_value, lengths))


def fold_values(attended, queries, key_value, log_total, lengths, row_tokens, col_tokens):

    def per_slot(inputs):
        slot_out, slot_queries, slot_pairs, slot_log, length = inputs

        def compute(current):
            scores = block_scores(slot_queries, slot_pairs[:, :, 0], row_tokens, col_tokens, length)
            prob_low = jnp.exp(scores - slot_log[..., None]).astype(jnp.bfloat16)
            return current + jnp.einsum(
                "hqk,khd->qhd", prob_low, slot_pairs[:, :, 1], preferred_element_type=jnp.float32
            )

        return lax.cond(
            is_live(row_tokens, col_tokens, length), compute, lambda current: current, slot_out
        )

    return lax.map(per_slot, (attended, queries, key_value, log_total, lengths))


def fold_grads(
    query_grad,
    pair_grad,
    queries,
    key_value,
    grad_out,
    log_total,
    row_delta,
    lengths,
    row_tokens,
    col_tokens,
):

    def per_slot(inputs):
        (
            slot_qgrad,
            slot_pgrad,
            slot_queries,
            slot_pairs,
            slot_gout,
            slot_log,
            slot_delta,
            length,
        ) = inputs

        def compute(current):
            cur_qgrad, cur_pgrad = current
            scores = block_scores(slot_queries, slot_pairs[:, :, 0], row_tokens, col_tokens, length)
            attend_prob = jnp.exp(scores - slot_log[..., None])
            prob_low = attend_prob.astype(jnp.bfloat16)
            prob_grad = jnp.einsum(
                "qhd,khd->hqk", slot_gout, slot_pairs[:, :, 1], preferred_element_type=jnp.float32
            )
            score_grad = (attend_prob * (prob_grad - slot_delta[..., None])).astype(jnp.bfloat16)
            cur_qgrad = cur_qgrad + jnp.einsum(
                "hqk,khd->qhd", score_grad, slot_pairs[:, :, 0], preferred_element_type=jnp.float32
            ) * HD ** (-0.5)
            key_grad = jnp.einsum(
                "hqk,qhd->khd", score_grad, slot_queries, preferred_element_type=jnp.float32
            ) * HD ** (-0.5)
            value_grad = jnp.einsum(
                "hqk,qhd->khd", prob_low, slot_gout, preferred_element_type=jnp.float32
            )
            return (cur_qgrad, cur_pgrad + jnp.stack([key_grad, value_grad], axis=2))

        return lax.cond(
            is_live(row_tokens, col_tokens, length),
            compute,
            lambda current: current,
            (slot_qgrad, slot_pgrad),
        )

    return lax.map(
        per_slot,
        (query_grad, pair_grad, queries, key_value, grad_out, log_total, row_delta, lengths),
    )


def local(residual, cotangent, lengths, positions, masters, momenta, averages):
    slot_count, span_rows, model_width = residual.shape
    group_count = lax.axis_size("blk")
    uly_count = lax.axis_size("uly")
    group_index = lax.axis_index("blk")
    uly_index = lax.axis_index("uly")
    block_rows = uly_count * span_rows
    full_rows = group_count * block_rows
    local_heads = H // uly_count
    token_rows = slot_count * span_rows
    row_tokens = group_tokens(group_index, group_count, uly_count, span_rows)

    def tokens_of(source):
        return group_tokens(source, group_count, uly_count, span_rows)

    gathered = lax.all_gather(masters.astype(jnp.bfloat16), ("blk", "uly"), axis=0, tiled=True)
    (
        gain_one,
        shift_one,
        gain_two,
        shift_two,
        project_w,
        project_b,
        dense_w,
        dense_b,
        expand_w,
        expand_b,
        shrink_w,
        shrink_b,
    ) = unpack(gathered)
    values = residual.astype(jnp.float32).reshape(token_rows, model_width)
    normed_one, norm_back_one = jax.vjp(
        layer_norm, values, gain_one.astype(jnp.float32), shift_one.astype(jnp.float32)
    )
    normed_two, norm_back_two = jax.vjp(
        layer_norm, values, gain_two.astype(jnp.float32), shift_two.astype(jnp.float32)
    )
    normed_one = normed_one.astype(jnp.bfloat16)
    normed_two = normed_two.astype(jnp.bfloat16)
    mixed_rows = jnp.dot(
        normed_one, project_w, preferred_element_type=jnp.float32
    ) + project_b.astype(jnp.float32)
    mixed_rows = mixed_rows.reshape(slot_count, span_rows, H, 3, HD)
    cos_table, sin_table = rotary_tables(positions)
    cos_table = cos_table[:, :, None, None, :]
    sin_table = sin_table[:, :, None, None, :]
    turned, turn_back = jax.vjp(
        lambda pair_rows: rotate(pair_rows, cos_table, sin_table), mixed_rows[:, :, :, 0:2]
    )
    packed = jnp.concatenate([turned, mixed_rows[:, :, :, 2:3]], axis=3).astype(jnp.bfloat16)
    packed = packed.reshape(slot_count, span_rows, 3 * model_width)
    heads_rows = lax.all_to_all(packed, "uly", split_axis=2, concat_axis=1, tiled=True).reshape(
        slot_count, block_rows, local_heads, 3, HD
    )
    queries = heads_rows[:, :, :, 0]
    key_value = heads_rows[:, :, :, 1:3]
    row_max = jnp.full((slot_count, local_heads, block_rows), NEGATIVE, jnp.float32)
    row_total = jnp.zeros((slot_count, local_heads, block_rows), jnp.float32)
    attended = jnp.zeros((slot_count, block_rows, local_heads, HD), jnp.float32)
    last_tokens = tokens_of((group_index + 1) % group_count)

    def stats_turn(turn_index, carried):
        pairs_now, cur_max, cur_total = carried
        col_tokens = tokens_of((group_index - turn_index) % group_count)
        cur_max, cur_total = fold_stats(
            cur_max, cur_total, queries, pairs_now, lengths, row_tokens, col_tokens
        )
        pairs_now = passed_along(pairs_now, "blk", 1)
        return (pairs_now, cur_max, cur_total)

    pairs_now, row_max, row_total = lax.fori_loop(
        0, group_count - 1, stats_turn, (key_value, row_max, row_total)
    )
    row_max, row_total = fold_stats(
        row_max, row_total, queries, pairs_now, lengths, row_tokens, last_tokens
    )
    log_total = row_max + jnp.log(row_total)

    def value_turn(turn_index, carried):
        pairs_now, cur_out = carried
        col_tokens = tokens_of((group_index - turn_index) % group_count)
        cur_out = fold_values(
            cur_out, queries, pairs_now, log_total, lengths, row_tokens, col_tokens
        )
        pairs_now = passed_along(pairs_now, "blk", 1)
        return (pairs_now, cur_out)

    pairs_now, attended = lax.fori_loop(0, group_count - 1, value_turn, (key_value, attended))
    attended = fold_values(
        attended, queries, pairs_now, log_total, lengths, row_tokens, last_tokens
    )
    heads_out = attended.astype(jnp.bfloat16).reshape(slot_count, block_rows, local_heads * HD)
    merged = lax.all_to_all(heads_out, "uly", split_axis=1, concat_axis=2, tiled=True).reshape(
        token_rows, model_width
    )
    branch_attn = jnp.dot(merged, dense_w, preferred_element_type=jnp.float32) + dense_b.astype(
        jnp.float32
    )
    hidden_pre = jnp.dot(
        normed_two, expand_w, preferred_element_type=jnp.float32
    ) + expand_b.astype(jnp.float32)
    activated, gelu_back = jax.vjp(partial(jax.nn.gelu, approximate=False), hidden_pre)
    activated_low = activated.astype(jnp.bfloat16)
    branch_feed = jnp.dot(
        activated_low, shrink_w, preferred_element_type=jnp.float32
    ) + shrink_b.astype(jnp.float32)
    outputs = (
        (values + branch_attn + branch_feed)
        .astype(jnp.bfloat16)
        .reshape(slot_count, span_rows, model_width)
    )
    first_token = (uly_index * group_count + group_index) * span_rows
    token_index = first_token + jnp.arange(span_rows, dtype=jnp.int32)
    live_mask = (token_index[None, :] < lengths[:, None]).astype(jnp.float32)
    seed_grad = (cotangent.astype(jnp.float32) * live_mask[:, :, None]).reshape(
        token_rows, model_width
    )
    seed_low = seed_grad.astype(jnp.bfloat16)
    dense_w_grad = jnp.einsum("ra,rb->ab", merged, seed_low, preferred_element_type=jnp.float32)
    bias_grad = jnp.sum(seed_low.astype(jnp.float32), axis=0)
    merged_grad = jnp.einsum(
        "rb,ab->ra", seed_low, dense_w, preferred_element_type=jnp.float32
    ).astype(jnp.bfloat16)
    shrink_w_grad = jnp.einsum(
        "rf,rb->fb", activated_low, seed_low, preferred_element_type=jnp.float32
    )
    activated_grad = jnp.einsum("rb,fb->rf", seed_low, shrink_w, preferred_element_type=jnp.float32)
    hidden_grad = gelu_back(activated_grad)[0].astype(jnp.bfloat16)
    expand_w_grad = jnp.einsum(
        "ra,rf->af", normed_two, hidden_grad, preferred_element_type=jnp.float32
    )
    expand_b_grad = jnp.sum(hidden_grad.astype(jnp.float32), axis=0)
    normed_two_grad = jnp.einsum(
        "rf,af->ra", hidden_grad, expand_w, preferred_element_type=jnp.float32
    )
    grad_heads = lax.all_to_all(
        merged_grad.reshape(slot_count, span_rows, model_width),
        "uly",
        split_axis=2,
        concat_axis=1,
        tiled=True,
    )
    grad_out = grad_heads.reshape(slot_count, block_rows, local_heads, HD)
    row_delta = jnp.sum(grad_out.astype(jnp.float32) * attended, axis=-1).transpose(0, 2, 1)
    query_grad = jnp.zeros((slot_count, block_rows, local_heads, HD), jnp.float32)
    pair_grad = jnp.zeros((slot_count, block_rows, local_heads, 2, HD), jnp.float32)

    def grad_turn(turn_index, carried):
        pairs_now, cur_pgrad, cur_qgrad = carried
        col_tokens = tokens_of((group_index - turn_index) % group_count)
        cur_qgrad, cur_pgrad = fold_grads(
            cur_qgrad,
            cur_pgrad,
            queries,
            pairs_now,
            grad_out,
            log_total,
            row_delta,
            lengths,
            row_tokens,
            col_tokens,
        )
        pairs_now = passed_along(pairs_now, "blk", 1)
        cur_pgrad = passed_along(cur_pgrad.astype(jnp.bfloat16), "blk", 1).astype(cur_pgrad.dtype)
        return (pairs_now, cur_pgrad, cur_qgrad)

    pairs_now, pair_grad, query_grad = lax.fori_loop(
        0, group_count - 1, grad_turn, (key_value, pair_grad, query_grad)
    )
    query_grad, pair_grad = fold_grads(
        query_grad,
        pair_grad,
        queries,
        pairs_now,
        grad_out,
        log_total,
        row_delta,
        lengths,
        row_tokens,
        last_tokens,
    )
    pair_grad = passed_along(pair_grad.astype(jnp.bfloat16), "blk", 1).astype(pair_grad.dtype)
    back_packed = jnp.concatenate(
        [query_grad.astype(jnp.bfloat16)[:, :, :, None], pair_grad.astype(jnp.bfloat16)], axis=3
    )
    back_packed = back_packed.reshape(slot_count, block_rows, local_heads * 3 * HD)
    token_grads = lax.all_to_all(
        back_packed, "uly", split_axis=1, concat_axis=2, tiled=True
    ).reshape(slot_count, span_rows, H, 3, HD)
    turned_grad = turn_back(token_grads[:, :, :, 0:2].astype(jnp.float32))[0]
    mixed_grad = jnp.concatenate(
        [turned_grad, token_grads[:, :, :, 2:3].astype(jnp.float32)], axis=3
    ).astype(jnp.bfloat16)
    mixed_grad = mixed_grad.reshape(token_rows, 3 * model_width)
    project_w_grad = jnp.einsum(
        "ra,rc->ac", normed_one, mixed_grad, preferred_element_type=jnp.float32
    )
    project_b_grad = jnp.sum(mixed_grad.astype(jnp.float32), axis=0)
    normed_one_grad = jnp.einsum(
        "rc,ac->ra", mixed_grad, project_w, preferred_element_type=jnp.float32
    )
    values_one, gain_one_grad, shift_one_grad = norm_back_one(normed_one_grad)
    values_two, gain_two_grad, shift_two_grad = norm_back_two(normed_two_grad)
    input_grad = (
        (seed_grad + values_one + values_two)
        .astype(jnp.bfloat16)
        .reshape(slot_count, span_rows, model_width)
    )
    local_grads = jnp.concatenate(
        [
            gain_one_grad,
            shift_one_grad,
            gain_two_grad,
            shift_two_grad,
            project_w_grad.reshape(-1),
            project_b_grad,
            dense_w_grad.reshape(-1),
            bias_grad,
            expand_w_grad.reshape(-1),
            expand_b_grad,
            shrink_w_grad.reshape(-1),
            bias_grad,
        ]
    )
    gradients = lax.psum_scatter(local_grads, ("blk", "uly"), scatter_dimension=0, tiled=True)
    velocity = MOMENTUM * momenta + gradients
    step_rate = LEARN_RATE / math.sqrt(slot_count * full_rows)
    updated = masters - step_rate * (gradients + MOMENTUM * velocity)
    averaged = AVERAGE_DECAY * averages + (1.0 - AVERAGE_DECAY) * updated
    return (outputs, input_grad, gradients, updated, velocity, averaged)


def solution(mesh):
    return jax.shard_map(
        local,
        mesh=mesh,
        in_specs=(
            P(None, ("uly", "blk"), None),
            P(None, ("uly", "blk"), None),
            P(),
            P(None, ("uly", "blk")),
            P(("blk", "uly")),
            P(("blk", "uly")),
            P(("blk", "uly")),
        ),
        out_specs=(
            P(None, ("uly", "blk"), None),
            P(None, ("uly", "blk"), None),
            P(("blk", "uly")),
            P(("blk", "uly")),
            P(("blk", "uly")),
            P(("blk", "uly")),
        ),
        check_vma=False,
    )
```

profile of v0, /device:TPU:0, one launch (start us, length us, event | category | flops | bytes accessed | tf_op | source)
XLA Modules:
  0.0 1666.7 jit_solution(17894882868313508942)
XLA Ops:
  17.2 13.2 dynamic-update-slice
  38.1 389.4 %all-reduce.8.cloned.1.call-done = bf16[12596224]{0:T(1024)(128)(2,1)} async-done(((bf16[12596224]{0:T(1024)(128)(2,1)}), bf16[12596224]{0:T(1024)(128)(2,1)}) %all-reduce.8.cloned.1.call-update) | async-done | bytes 25192464
  434.0 10.3 reshape.771
  488.2 11.4 fusion.125
  499.5 13.3 reshape.776
  512.9 13.4 slice.252
  537.2 68.6 %while.214 = (s32[]{:T(128)}, bf16[2,512,2,2,64]{1,4,2,3,0:T(8,128)(2,1)S(1)}, f32[2,2,512]{2,1,0:T(2,128)S(1)}, f32[2,2,512]{2,1,0:T(2,128)S(1)}, s32[]{:T(128)...) while((s32[]{:T(128)}, ...), condition=%wide.region_9.10_spmd.clone.clone, body=%wide.region_2.9_spmd.clone.sunk.clone | while | flops 71307304 | bytes 9029437 | solution.py:269
  540.6 18.9 %while.213 = (s32[]{:T(128)}, f32[2,2,512]{2,1,0:T(2,128)S(1)}, f32[2,2,512]{2,1,0:T(2,128)S(1)}, s32[512]{0:T(512)S(1)}, s32[2]{0:T(128)S(1)}, /*index=5*/pred[...) while((s32[]{:T(128)}, f32[2,2,512]{2,1,0:T(2,128)S(1)}, ...), condition=%wide.region_8.8_spmd.clone.clone, body=%wide.region_3.7_spmd.clone.clone.sunk | while | flops 71306240 | bytes 5875002 | solution.py:119
  564.6 18.9 %while.213 = (s32[]{:T(128)}, f32[2,2,512]{2,1,0:T(2,128)S(1)}, f32[2,2,512]{2,1,0:T(2,128)S(1)}, s32[512]{0:T(512)S(1)}, s32[2]{0:T(128)S(1)}, /*index=5*/pred[...) while((s32[]{:T(128)}, f32[2,2,512]{2,1,0:T(2,128)S(1)}, ...), condition=%wide.region_8.8_spmd.clone.clone, body=%wide.region_3.7_spmd.clone.clone.sunk | while | flops 71306240 | bytes 5875002 | solution.py:119
  586.9 18.9 %while.213 = (s32[]{:T(128)}, f32[2,2,512]{2,1,0:T(2,128)S(1)}, f32[2,2,512]{2,1,0:T(2,128)S(1)}, s32[512]{0:T(512)S(1)}, s32[2]{0:T(128)S(1)}, /*index=5*/pred[...) while((s32[]{:T(128)}, f32[2,2,512]{2,1,0:T(2,128)S(1)}, ...), condition=%wide.region_8.8_spmd.clone.clone, body=%wide.region_3.7_spmd.clone.clone.sunk | while | flops 71306240 | bytes 5875002 | solution.py:119
  605.8 17.1 %while.215 = (s32[]{:T(128)}, f32[2,2,512]{2,1,0:T(2,128)S(1)}, f32[2,2,512]{2,1,0:T(2,128)S(1)}, s32[512]{0:T(512)S(1)}, s32[2]{0:T(128)S(1)}, /*index=5*/pred[...) while((s32[]{:T(128)}, f32[2,2,512]{2,1,0:T(2,128)S(1)}, ...), condition=%wide.region_15.16_spmd.clone.clone, body=%wide.region_10.15_spmd.clone.sunk.clone | while | flops 71306752 | bytes 5879146 | solution.py:119
  623.0 47.6 %while.217 = (s32[]{:T(128)}, bf16[2,512,2,2,64]{1,4,2,3,0:T(8,128)(2,1)S(1)}, f32[2,512,2,64]{1,3,2,0:T(8,128)S(1)}, s32[]{:T(128)}, s32[512]{0:T(512)S(1)}, /*...) while((s32[]{:T(128)}, ...), condition=%wide.region_21.22_spmd.clone.clone, body=%wide.region_16.21_spmd.clone.sunk.clone | while | flops 136906784 | bytes 6203165 | solution.py:286
  627.1 11.7 while.216
  642.2 11.7 while.216
  658.9 11.7 while.216
  687.6 95.0 %while.221 = (s32[]{:T(128)}, bf16[2,512,2,2,64]{1,4,2,3,0:T(8,128)(2,1)S(1)}, f32[2,512,2,2,64]{1,4,2,3,0:T(8,128)}, f32[2,512,2,64]{1,3,2,0:T(8,128)S(1)}, s32...) while((s32[]{:T(128)}, ...), condition=%wide.region_32.33_spmd.clone.clone, body=%wide.region_27.32_spmd.clone.sunk.clone | while | flops 340723744 | bytes 26139116 | solution.py:365
  690.4 13.7 while.220
  722.4 13.7 while.220
  754.5 13.7 while.220
  782.6 16.5 while.219
  799.1 10.9 convert_reduce_fusion.1
  848.3 13.2 convert_reduce_fusion
  877.2 12.3 copy.92
  937.3 716.3 %all-reduce.10.cloned.1.call-done = f32[12596224]{0:T(1024)} async-done(((f32[12596224]{0:T(1024)}), f32[12596224]{0:T(1024)}) %all-reduce.10.cloned.1.call-update) | async-done | bytes 50384912
  (761 shorter events, 504.5 us)
Async XLA Ops:
  7.2 420.4 %all-reduce.8.cloned.1.call-start = ((), (), s32[]{:S(2)}) async-start(), calls=%async_computation.4 | async-start | bytes 50384896
  35.8 435.4 %copy-start.33 = (f32[2,64,8]{1,0,2:T(2,128)}, f32[2,64,8]{1,0,2:T(2,128)S(1)}, u32[]{:S(2)}) copy-start(f32[2,64,8]{1,0,2:T(2,128)S(1)} %get-tuple-element.3166) | copy-start | bytes 12292
  35.8 435.4 %copy-start.35 = (f32[2,64,8]{1,0,2:T(2,128)}, f32[2,64,8]{1,0,2:T(2,128)S(1)}, u32[]{:S(2)}) copy-start(f32[2,64,8]{1,0,2:T(2,128)S(1)} %get-tuple-element.3167) | copy-start | bytes 12292
  38.1 425.7 %copy-start.17 = (bf16[128,1024]{1,0:T(8,128)(2,1)}, bf16[128,1024]{1,0:T(8,128)(2,1)S(1)}, u32[]{:S(2)}) copy-start(bf16[128,1024]{1,0:T(8,128)(2,1)S(1)} %bitcast_convert_fusion) | copy-start | bytes 786436
  467.7 14.2 all-to-all-start.2
  482.0 51.9 %all-to-all-start = ((bf16[8,2,24576]{2,1,0:T(2,128)(2,1)}), bf16[8,2,24576]{2,1,0:T(2,128)(2,1)S(1)}, u32[]{:S(2)}, u32[]{:S(2)}) async-start(bf16[8,2,24576]{2,1,0:T(2,128)(2,1)} %reshape.790), calls=%async_computation | async-start | bytes 1572864 | tf_op jit(solution)/shard_map/all_to_all | solution.py:250
  538.0 21.5 %collective-permute-start = (bf16[2,512,2,2,64]{1,4,2,3,0:T(8,128)(2,1)}, bf16[2,512,2,2,64]{1,4,2,3,0:T(8,128)(2,1)S(1)}, u32[]{:S(2)}, u32[]{:S(2)}) collective-permute-start(bf16[2,512,2,2,64]{1,4,2,3,0:T(8,128)(2,1)} %copy.173), channel_id=1, source_target_pairs={{24,0},{0,8},{8,16},{16,24},{25,1},{1,9},{9,17},{17,25},{26,2},{2,... | collective-permute-start | bytes 1572872 | tf_op jit(solution)/shard_map/while/body/eval_jaxpr/ppermute | solution.py:27
  560.3 23.1 %collective-permute-start = (bf16[2,512,2,2,64]{1,4,2,3,0:T(8,128)(2,1)}, bf16[2,512,2,2,64]{1,4,2,3,0:T(8,128)(2,1)S(1)}, u32[]{:S(2)}, u32[]{:S(2)}) collective-permute-start(bf16[2,512,2,2,64]{1,4,2,3,0:T(8,128)(2,1)} %copy.173), channel_id=1, source_target_pairs={{24,0},{0,8},{8,16},{16,24},{25,1},{1,9},{9,17},{17,25},{26,2},{2,... | collective-permute-start | bytes 1572872 | tf_op jit(solution)/shard_map/while/body/eval_jaxpr/ppermute | solution.py:27
  584.3 21.5 %collective-permute-start = (bf16[2,512,2,2,64]{1,4,2,3,0:T(8,128)(2,1)}, bf16[2,512,2,2,64]{1,4,2,3,0:T(8,128)(2,1)S(1)}, u32[]{:S(2)}, u32[]{:S(2)}) collective-permute-start(bf16[2,512,2,2,64]{1,4,2,3,0:T(8,128)(2,1)} %copy.173), channel_id=1, source_target_pairs={{24,0},{0,8},{8,16},{16,24},{25,1},{1,9},{9,17},{17,25},{26,2},{2,... | collective-permute-start | bytes 1572872 | tf_op jit(solution)/shard_map/while/body/eval_jaxpr/ppermute | solution.py:27
  623.8 15.0 collective-permute-start.1
  639.6 14.3 collective-permute-start.1
  654.7 15.9 collective-permute-start.1
  681.1 130.8 %all-to-all-start.1 = ((bf16[2,512,128]{2,0,1:T(2,128)(2,1)}), bf16[2,512,128]{2,0,1:T(2,128)(2,1)}, u32[]{:S(2)}, u32[]{:S(2)}) async-start(bf16[2,512,128]{2,0,1:T(2,128)(2,1)} %copy.54), calls=%async_computation.1 | async-start | bytes 524288 | tf_op jit(solution)/shard_map/all_to_all | solution.py:291
  704.1 8.8 collective-permute-start.3
  704.1 14.4 collective-permute-start.2
  736.1 8.8 collective-permute-start.3
  736.1 14.4 collective-permute-start.2
  768.2 8.8 collective-permute-start.3
  768.2 14.4 collective-permute-start.2
  799.1 10.9 collective-permute-start.4
  811.9 27.9 %all-to-all-start.3 = ((bf16[2,512,384]{2,0,1:T(2,128)(2,1)}), bf16[2,512,384]{2,0,1:T(2,128)(2,1)}, u32[]{:S(2)}, u32[]{:S(2)}) async-start(bf16[2,512,384]{2,0,1:T(2,128)(2,1)} %copy.62), calls=%async_computation.3 | async-start | bytes 1572864 | tf_op jit(solution)/shard_map/all_to_all | solution.py:385
  817.9 835.8 %all-reduce.10.cloned.1.call-start = ((), (), s32[]{:S(2)}) async-start(), calls=%async_computation.5 | async-start | bytes 100769792
  848.3 25.1 %slice-start.2 = ((s8[6291456]{0:T(1024)(128)(4,1)}), s8[2097152]{0:T(1024)(128)(4,1)S(1)}, s32[]{:S(2)}) async-start(s8[6291456]{0:T(1024)(128)(4,1)} %bitcast.393), calls=%async_computation.8 | async-start | bytes 4194304
  936.1 717.6 %copy-start.9 = (f32[393632]{0:T(1024)S(1)}, f32[393632]{0:T(1024)}, u32[]{:S(2)}) copy-start(f32[393632]{0:T(1024)} %param.41) | copy-start | bytes 4723588
  (52 other events, 310.7 us)
Sparse Core Ops, SparseCore 0:
  30.5 397.0 all-reduce.7
  930.7 722.8 all-reduce.9
where the time goes:
time: 1680 us; the launch traced here: 1670 us
  waiting for transfers between devices  1140 us (68%)
  local copies, waits for them, and re-layouts  260 us (15%)
  other arithmetic  94.3 us (6%)
  matrix products  80 us (5%)
  loops' own time  43.7 us (3%)
  starting transfers between devices  28 us (2%)
    unnamed x4, waiting for transfers between devices  1110 us
    unnamed x128, local copies, waits for them, and re-layouts  90.7 us
    ppermute x13, waiting for transfers between devices, passed_along(): return lax.ppermute(block, axis, route)  38 us
    slice x6, local copies, waits for them, and re-layouts, unpack(): pieces.append(flat_vector[cursor:cursor + number].reshape(layout))  35 us
  transfers between devices with their start and end apart: 19, of which 8 were waited for; matrix products, arithmetic and copies ran while one was open for 15% of the time, Pallas kernels for 0%

commit v1 on v0

--- a/solution.py
+++ b/solution.py
@@ -4,7 +4,9 @@
 import jax
 import jax.numpy as jnp
 from jax import lax
-from jax.sharding import PartitionSpec as P
+from jax.experimental import pallas as pl
+from jax.experimental.pallas import tpu as pltpu
+from jax.sharding import Mesh, PartitionSpec as P
 
 D = 1024
 H = 16
@@ -428,26 +430,781 @@
     return (outputs, input_grad, gradients, updated, velocity, averaged)
 
 
+LANES = 128
+BLOCK = 256
+RING = ("core", "z", "y")
+ALL = ("x", "core", "z", "y")
+F32 = jnp.float32
+BF16 = jnp.bfloat16
+
+
+def call(body, grid, in_specs, out_specs, out_shape, scratch=(), prefetch=0, name=None):
+    return pl.pallas_call(
+        body,
+        grid_spec=pltpu.PrefetchScalarGridSpec(
+            num_scalar_prefetch=prefetch,
+            grid=grid,
+            in_specs=in_specs,
+            out_specs=out_specs,
+            scratch_shapes=scratch,
+        ),
+        out_shape=out_shape,
+        name=name,
+        compiler_params=pltpu.CompilerParams(vmem_limit_bytes=56 << 20),
+    )
+
+
+def whole(shape):
+    return pl.BlockSpec(shape, lambda *_: (0,) * len(shape))
+
+
+def shaped(shape, kind):
+    return jax.ShapeDtypeStruct(shape, kind)
+
+
+def mm(a, b, dims=((1,), (0,))):
+    return lax.dot_general(a, b, (dims, ((), ())), preferred_element_type=F32)
+
+
+def low_lanes(shape):
+    return lax.broadcasted_iota(jnp.int32, shape, len(shape) - 1) < LANES // 2
+
+
+def swap(a):
+    return pltpu.roll(a, LANES // 2, 1)
+
+
+def join(a, a_half, b, b_half):
+    first = swap(a) if a_half else a
+    second = b if b_half else swap(b)
+    return jnp.where(low_lanes(a.shape), first, second)
+
+
+OWNERS = 32
+PER = (3 * D + D + FF + FF) // OWNERS
+FLAT = PER * D // LANES
+PIECE = FLAT // 16
+LEAD = 4 * D // LANES
+PROJECT, PLAIN, PLAIN_EXPAND, EXPAND, EXPAND_PLAIN = range(5)
+
+
+def kind_of(c):
+    return (
+        PROJECT
+        if c < 8
+        else PLAIN
+        if c < 10 or c > 21
+        else PLAIN_EXPAND
+        if c == 10
+        else EXPAND_PLAIN
+        if c == 21
+        else EXPAND
+    )
+
+
+def plain_place(row, base, count):
+    local = row - base
+    half = int(local >= count // 2)
+    return local - half * (count // 2), half
+
+
+def dense_place(row):
+    if row < 768:
+        c = 8 + row // 384
+        return (c, 0) + plain_place(row, 384 * (c - 8), 384)
+    return (10, 0) + plain_place(row, 768, 256)
+
+
+def shrink_place(row):
+    if row < 256:
+        return (21, 64) + plain_place(row, 0, 256)
+    c = 22 + (row - 256) // 384
+    return (c, 0) + plain_place(row, 256 + 384 * (c - 22), 384)
+
+
+def expand_places():
+    places = [(10, 128, 0, 32)]
+    places += [(c, 0, 32 + 96 * (c - 11), 96) for c in range(11, 21)]
+    places += [(21, 0, 992, 32)]
+    return places
+
+
+def shifted_rows(source, start, shift, at, rows):
+    turn = (LANES - shift) % LANES
+    first = pltpu.roll(source[pl.ds(start + at, rows), :], turn, 1)
+    second = pltpu.roll(source[pl.ds(start + at + 1, rows), :], turn, 1)
+    lane = lax.broadcasted_iota(jnp.int32, (rows, LANES), 1)
+    return jnp.where(lane < LANES - shift, first, second)
+
+
+SHIFT_ROWS = 3200
+SEND_ROWS = PIECE + 32 + 16
+
+
+def weights_out_body(scalars, source, places, out, flat):
+    start, shift, kind, vector_row = scalars[0], scalars[1], scalars[2], scalars[3]
+
+    def align(step, carry):
+        at = pl.multiple_of(step * 80, 8)
+        flat[pl.ds(at, 80), :] = shifted_rows(source, start, shift, at, 80)
+        return carry
+
+    lax.fori_loop(0, SHIFT_ROWS // 80, align, 0)
+
+    def rows(first, count, stride):
+        return flat[pl.ds(first, count, stride), :]
+
+    def plain(base, count, to):
+        for m in range(8):
+            tile = rows(base + m, count, 8)
+            a, b = tile[: count // 2], tile[count // 2 :]
+            out[2 * m, to : to + count // 2] = join(a, 0, b, 0).astype(BF16)
+            out[2 * m + 1, to : to + count // 2] = join(a, 1, b, 1).astype(BF16)
+
+    def expand(base, count, to):
+        for r in range(16):
+            out[r, to : to + count] = rows(base + 2 * r, count, 32).astype(BF16)
+            out[r, to + count : to + 2 * count] = rows(base + 2 * r + 1, count, 32).astype(BF16)
+
+    def project(base):
+        for m in range(8):
+            first, middle, last = (rows(base + 3 * m + j, 128, 24) for j in range(3))
+            out[2 * m, 0:128] = first.astype(BF16)
+            out[2 * m, 128:192] = join(middle[:64], 0, middle[64:], 0).astype(BF16)
+            out[2 * m + 1, 0:128] = join(middle, 1, last, 0).astype(BF16)
+            out[2 * m + 1, 128:192] = join(last[:64], 1, last[64:], 1).astype(BF16)
+
+    @pl.when(kind == PROJECT)
+    def _():
+        project(LEAD)
+
+    @pl.when(kind == PLAIN)
+    def _():
+        plain(LEAD, 384, 0)
+
+    @pl.when(kind == PLAIN_EXPAND)
+    def _():
+        plain(LEAD, 256, 0)
+        expand(LEAD + 2048 + 8, 32, 128)
+
+    @pl.when(kind == EXPAND)
+    def _():
+        expand(LEAD, 96, 0)
+
+    @pl.when(kind == EXPAND_PLAIN)
+    def _():
+        expand(LEAD, 32, 0)
+        plain(LEAD + 1024 + 32, 256, 64)
+
+    vectors = flat[pl.ds(vector_row, 32), :].astype(BF16)
+    for r in range(16):
+        out[r, PIECE : PIECE + 32] = vectors
+        out[r, PIECE + 32 :] = places[...]
+
+
+def weights_in_body(scalars, got, qkv_w, expand_w, second, vectors, qkv_b, expand_b, project_rows, expand_rows):
+    head = scalars[0]
+    low = low_lanes((64, LANES))
+    for c in range(8):
+        qkv_w[128 * c : 128 * c + 128, 0:128] = got[c, 0:128]
+        packed = got[c, 128:192].astype(F32)
+        qkv_w[128 * c : 128 * c + 64, 128:256] = jnp.where(low, packed, 0.0).astype(BF16)
+        qkv_w[128 * c + 64 : 128 * c + 128, 128:256] = jnp.where(low, swap(packed), 0.0).astype(BF16)
+    for c, at, row, count in expand_places():
+        expand_w[row : row + count, 0:128] = got[c, at : at + count]
+        expand_w[row : row + count, 128:256] = got[c, at + count : at + 2 * count]
+
+    for h in range(16):
+        c, at, row, half = dense_place(64 * h)
+        tile = got[c, at + row : at + row + 64].astype(F32)
+        second[h, 0:32] = join(tile[:32], half, tile[32:], half).astype(BF16)
+        for part in range(2):
+            c, at, row, half = shrink_place(256 * h + 64 * part)
+            tile = got[c, at + row : at + row + 64].astype(F32)
+            c, at, row, other = shrink_place(256 * h + 128 + 64 * part)
+            after = got[c, at + row : at + row + 64].astype(F32)
+            second[h, 32 + 64 * part : 96 + 64 * part] = join(tile, half, after, other).astype(BF16)
+
+    def vector(c, at, to):
+        tile = got[c, PIECE + at : PIECE + at + 8].astype(F32)
+        for j in range(8):
+            vectors[to : to + 1, 128 * j : 128 * j + 128] = tile[j : j + 1]
+
+    vectors[...] = jnp.zeros(vectors.shape, F32)
+    for v in range(4):
+        vector(0, 8 * v, v)
+    vector(10, 0, 4)
+    vector(31, 0, 5)
+    project_rows[...] = got[8, PIECE + 8 : PIECE + 32].astype(F32)
+    expand_rows[...] = got[21, PIECE : PIECE + 32].astype(F32)
+    row = head // 2 * 3
+    first, middle, last = (project_rows[pl.ds(row + j, 1), :] for j in range(3))
+    odd = head % 2 == 1
+    qkv_b[0:1, 0:128] = jnp.where(odd, join(middle, 1, last, 0), first)
+    value = jnp.where(odd, swap(last), middle)
+    qkv_b[0:1, 128:256] = jnp.where(low_lanes((1, LANES)), value, 0.0)
+    expand_b[0:1, 0:128] = expand_rows[pl.ds(2 * head, 1), :]
+    expand_b[0:1, 128:256] = expand_rows[pl.ds(2 * head + 1, 1), :]
+
+
+def rows_in_body(got, dense_w, shrink_w):
+    for m in range(8):
+        even, odd = got[2 * m].astype(F32), got[2 * m + 1].astype(F32)
+        columns = slice(128 * m, 128 * m + 128)
+        for out, at, half in ((dense_w, 0, 32), (shrink_w, 32, 128)):
+            a, b = even[at : at + half], odd[at : at + half]
+            out[0:half, columns] = join(a, 0, b, 0).astype(BF16)
+            out[half : 2 * half, columns] = join(a, 1, b, 1).astype(BF16)
+
+
+def rows_out_body(dense_g, shrink_g, out):
+    for m in range(8):
+        columns = slice(128 * m, 128 * m + 128)
+        for source, at, half in ((dense_g, 0, 32), (shrink_g, 32, 128)):
+            a, b = source[0:half, columns], source[half : 2 * half, columns]
+            out[2 * m, at : at + half] = join(a, 0, b, 0).astype(BF16)
+            out[2 * m + 1, at : at + half] = join(a, 1, b, 1).astype(BF16)
+
+
+BACK_ROWS = PIECE + 32
+
+
+def grads_out_body(scalars, second, qkv_g, expand_g, vector_g, qkv_bg, expand_bg, out, project_rows, expand_rows):
+    head = scalars[0]
+    out[...] = jnp.zeros(out.shape, BF16)
+    for c in range(8):
+        out[c, 0:128] = qkv_g[128 * c : 128 * c + 128, 0:128].astype(BF16)
+        a = qkv_g[128 * c : 128 * c + 64, 128:256]
+        b = qkv_g[128 * c + 64 : 128 * c + 128, 128:256]
+        out[c, 128:192] = join(a, 0, b, 0).astype(BF16)
+    for c, at, row, count in expand_places():
+        out[c, at : at + count] = expand_g[row : row + count, 0:128].astype(BF16)
+        out[c, at + count : at + 2 * count] = expand_g[row : row + count, 128:256].astype(BF16)
+
+    def dense_rows(row):
+        packed = second[row // 64, 0:32].astype(F32)
+        return jnp.concatenate([packed, swap(packed)], axis=0)
+
+    def shrink_rows(row):
+        h, part = row // 256, row % 256 // 64
+        packed = second[h, 32 + part % 2 * 64 : 96 + part % 2 * 64].astype(F32)
+        return swap(packed) if part >= 2 else packed
+
+    def plain(c, to, base, count, take):
+        for i in range(count // 128):
+            a, b = take(base + 64 * i), take(base + count // 2 + 64 * i)
+            out[c, to + 64 * i : to + 64 * i + 64] = join(a, 0, b, 0).astype(BF16)
+
+    plain(8, 0, 0, 384, dense_rows)
+    plain(9, 0, 384, 384, dense_rows)
+    plain(10, 0, 768, 256, dense_rows)
+    plain(21, 64, 0, 256, shrink_rows)
+    for c in range(22, 32):
+        plain(c, 0, 256 + 384 * (c - 22), 384, shrink_rows)
+
+    def rows_of(row):
+        return jnp.concatenate([vector_g[row : row + 1, 128 * j : 128 * j + 128] for j in range(8)], axis=0)
+
+    gains = jnp.concatenate([rows_of(v) for v in range(4)], axis=0)
+    out[0, PIECE : PIECE + 32] = gains.astype(BF16)
+    bias = jnp.concatenate([rows_of(4), jnp.zeros((8, LANES), F32)], axis=0).astype(BF16)
+    out[10, PIECE : PIECE + 16] = bias
+    out[31, PIECE : PIECE + 16] = bias
+    project_rows[...] = jnp.zeros(project_rows.shape, F32)
+    expand_rows[...] = jnp.zeros(expand_rows.shape, F32)
+    pair, value = qkv_bg[0:1, 0:128], qkv_bg[0:1, 128:256]
+    low = low_lanes((1, LANES))
+    row = 8 + head // 2 * 3
+    odd = head % 2 == 1
+    project_rows[pl.ds(row, 1), :] = jnp.where(odd, 0.0, pair)
+    project_rows[pl.ds(row + 1, 1), :] = jnp.where(
+        odd, jnp.where(low, 0.0, swap(pair)), jnp.where(low, value, 0.0)
+    )
+    project_rows[pl.ds(row + 2, 1), :] = jnp.where(odd, join(pair, 1, value, 0), 0.0)
+    out[8, PIECE : PIECE + 32] = project_rows[...].astype(BF16)
+    expand_rows[pl.ds(2 * head, 1), :] = expand_bg[0:1, 0:128]
+    expand_rows[pl.ds(2 * head + 1, 1), :] = expand_bg[0:1, 128:256]
+    out[21, PIECE : PIECE + 32] = expand_rows[...].astype(BF16)
+
+
+TAKE_ROWS = 3120
+
+
+def grads_in_body(scalars, got, out, flat):
+    start, shift, kind, vector_row = scalars[0], scalars[1], scalars[2], scalars[3]
+    lead = LEAD + 8
+
+    def clear(step, carry):
+        flat[pl.ds(pl.multiple_of(step * 80, 8), 80), :] = jnp.zeros((80, LANES), F32)
+        return carry
+
+    lax.fori_loop(0, SHIFT_ROWS // 80, clear, 0)
+
+    def add_vectors(source, total):
+        return total + got[source, PIECE : PIECE + 32].astype(F32)
+
+    flat[pl.ds(vector_row + 8, 32), :] = lax.fori_loop(0, OWNERS, add_vectors, jnp.zeros((32, LANES), F32))
+
+    def taken(r, at, count):
+        return got[r, at : at + count].astype(F32) + got[16 + r, at : at + count].astype(F32)
+
+    def plain(base, count, at):
+        half = count // 2
+        for m in range(8):
+            a, b = taken(2 * m, at, half), taken(2 * m + 1, at, half)
+            flat[pl.ds(base + m, half, 8), :] = join(a, 0, b, 0)
+            flat[pl.ds(base + m + 8 * half, half, 8), :] = join(a, 1, b, 1)
+
+    def expand(base, count, at):
+        for r in range(16):
+            flat[pl.ds(base + 2 * r, count, 32), :] = taken(r, at, count)
+            flat[pl.ds(base + 2 * r + 1, count, 32), :] = taken(r, at + count, count)
+
+    def project(base):
+        for m in range(8):
+            pair, values = taken(2 * m, 0, 128), taken(2 * m, 128, 64)
+            odd_pair, odd_values = taken(2 * m + 1, 0, 128), taken(2 * m + 1, 128, 64)
+            values = jnp.concatenate([values, swap(values)], axis=0)
+            odd_values = jnp.concatenate([odd_values, swap(odd_values)], axis=0)
+            flat[pl.ds(base + 3 * m, 128, 24), :] = pair
+            flat[pl.ds(base + 3 * m + 1, 128, 24), :] = join(values, 0, odd_pair, 0)
+            flat[pl.ds(base + 3 * m + 2, 128, 24), :] = join(odd_pair, 1, odd_values, 0)
+
+    @pl.when(kind == PROJECT)
+    def _():
+        project(lead)
+
+    @pl.when(kind == PLAIN)
+    def _():
+        plain(lead, 384, 0)
+
+    @pl.when(kind == PLAIN_EXPAND)
+    def _():
+        plain(lead, 256, 0)
+        expand(lead + 2048 + 8, 32, 128)
+
+    @pl.when(kind == EXPAND)
+    def _():
+        expand(lead, 96, 0)
+
+    @pl.when(kind == EXPAND_PLAIN)
+    def _():
+        expand(lead, 32, 0)
+        plain(lead + 1024 + 32, 256, 64)
+
+    def align(step, carry):
+        at = pl.multiple_of(step * 80, 8)
+        out[pl.ds(at, 80), :] = shifted_rows(flat, start, shift, at, 80)
+        return carry
+
+    lax.fori_loop(0, TAKE_ROWS // 80, align, 0)
+
+
+def token_rows(ref):
+    return jnp.concatenate([ref[0, 0, 0], ref[1, 0, 0], ref[0, 0, 1], ref[1, 0, 1]], axis=0)
+
+
+def put_rows(ref, rows):
+    step = rows.shape[0] // 4
+    for i, (core, x) in enumerate(((0, 0), (1, 0), (0, 1), (1, 1))):
+        ref[core, 0, x] = rows[step * i : step * i + step].astype(ref.dtype)
+
+
+def normalized(values):
+    centered = values - jnp.mean(values, axis=-1, keepdims=True)
+    variance = jnp.mean(centered * centered, axis=-1, keepdims=True)
+    return centered * lax.rsqrt(variance + EPSILON)
+
+
+def turned(pair, cos, sin):
+    lane = lax.broadcasted_iota(jnp.int32, pair.shape, 1) % HD
+    half = ROT // 2
+    other = jnp.where(
+        lane < half, -pltpu.roll(pair, LANES - half, 1), jnp.where(lane < ROT, pltpu.roll(pair, half, 1), 0.0)
+    )
+    return pair * cos + other * sin
+
+
+def mixed_body(tokens, vectors, qkv_w, qkv_b, cos, sin, one, two, query, key, value):
+    unit = normalized(token_rows(tokens).astype(F32))
+    first = (unit * vectors[0:1] + vectors[1:2]).astype(BF16)
+    one[...] = first
+    two[...] = (unit * vectors[2:3] + vectors[3:4]).astype(BF16)
+    mixed = mm(first, qkv_w[...]) + qkv_b[...]
+    pair = turned(mixed[:, :LANES], cos[...], sin[...])
+    query[...] = pair[:, :HD].astype(BF16) * HD ** (-0.5)
+    key[...] = pair[:, HD:].astype(BF16)
+    value[...] = mixed[:, LANES : LANES + HD].astype(BF16)
+
+
+def masked_scores(key, query_t, at, first_query, length):
+    scores = mm(key, query_t)
+    keys = at * BLOCK + lax.broadcasted_iota(jnp.int32, scores.shape, 0)
+    queries = first_query + lax.broadcasted_iota(jnp.int32, scores.shape, 1)
+    return jnp.where((keys <= queries) & (keys < length), scores, NEGATIVE)
+
+
+def folded(values, op):
+    parts = [values[8 * i : 8 * i + 8] for i in range(values.shape[0] // 8)]
+    while len(parts) > 1:
+        parts = [op(a, b) for a, b in zip(parts[::2], parts[1::2])]
+    return parts[0]
+
+
+def attend_body(lengths, query, key, value, low_out, full_out, log_out, scores, value_t):
+    at = pl.program_id(0)
+    length = lengths[0]
+
+    @pl.when(at == 0)
+    def _():
+        value_t[...] = value[...].astype(F32).T.astype(BF16)
+
+    query_t = query[...].astype(F32).T.astype(BF16)
+    clear = jnp.minimum(at, length // BLOCK)
+    stop = jnp.minimum(at, (length - 1) // BLOCK) + 1
+
+    def rows(j):
+        return pl.ds(pl.multiple_of(j * BLOCK, BLOCK), BLOCK)
+
+    def score(j, top, masked):
+        if masked:
+            tile = masked_scores(key[rows(j), :], query_t, j, at * BLOCK, length)
+        else:
+            tile = mm(key[rows(j), :], query_t)
+        scores[rows(j), :] = tile
+        return jnp.maximum(top, folded(tile, jnp.maximum))
+
+    top = jnp.full((8, BLOCK), NEGATIVE, F32)
+    top = lax.fori_loop(0, clear, lambda j, t: score(j, t, False), top)
+    top = lax.fori_loop(clear, stop, lambda j, t: score(j, t, True), top)
+    top = jnp.max(top, axis=0, keepdims=True)
+
+    def power(j, total):
+        tile = jnp.exp(scores[rows(j), :] - top)
+        scores[rows(j), :] = tile
+        return total + folded(tile, jnp.add)
+
+    total = lax.fori_loop(0, stop, power, jnp.zeros((8, BLOCK), F32))
+    total = jnp.sum(total, axis=0, keepdims=True)
+    inverse = 1.0 / total
+
+    def weigh(j, out):
+        low = (scores[rows(j), :] * inverse).astype(BF16)
+        return out + mm(value_t[:, rows(j)], low)
+
+    out = lax.fori_loop(0, stop, weigh, jnp.zeros((HD, BLOCK), F32))
+    full_out[...] = out
+    low_out[...] = out.T.astype(BF16)
+    log_out[...] = top + jnp.log(total)
+
+
+def attend_back_body(
+    lengths, query, key, value, grad, full_out, log_in, query_g, key_g, value_g, key_t, key_sum, value_sum
+):
+    at = pl.program_id(0)
+    length = lengths[0]
+
+    @pl.when(at == 0)
+    def _():
+        key_t[...] = key[...].astype(F32).T.astype(BF16)
+        key_sum[...] = jnp.zeros(key_sum.shape, F32)
+        value_sum[...] = jnp.zeros(value_sum.shape, F32)
+
+    query_rows, grad_rows = query[...], grad[...]
+    query_t = query_rows.astype(F32).T.astype(BF16)
+    grad_full_t = grad_rows.astype(F32).T
+    grad_t = grad_full_t.astype(BF16)
+    delta = jnp.sum(grad_full_t * full_out[...], axis=0, keepdims=True)
+    log_total = log_in[...]
+    clear = jnp.minimum(at, length // BLOCK)
+    stop = jnp.minimum(at, (length - 1) // BLOCK) + 1
+    clear, stop = (jnp.where(at * BLOCK < length, n, 0) for n in (clear, stop))
+
+    def step(j, query_sum, masked):
+        rows = pl.ds(pl.multiple_of(j * BLOCK, BLOCK), BLOCK)
+        if masked:
+            tile = masked_scores(key[rows, :], query_t, j, at * BLOCK, length)
+        else:
+            tile = mm(key[rows, :], query_t)
+        probs = jnp.exp(tile - log_total)
+        value_sum[rows, :] += mm(probs.astype(BF16), grad_rows)
+        score_g = (probs * (mm(value[rows, :], grad_t) - delta)).astype(BF16)
+        key_sum[rows, :] += mm(score_g, query_rows)
+        return query_sum + mm(key_t[:, rows], score_g)
+
+    query_sum = jnp.zeros((HD, BLOCK), F32)
+    query_sum = lax.fori_loop(0, clear, lambda j, s: step(j, s, False), query_sum)
+    query_sum = lax.fori_loop(clear, stop, lambda j, s: step(j, s, True), query_sum)
+    query_g[...] = (query_sum * HD ** (-0.5)).T.astype(BF16)
+
+    @pl.when(at == pl.num_programs(0) - 1)
+    def _():
+        key_g[...] = key_sum[...].astype(BF16)
+        value_g[...] = value_sum[...].astype(BF16)
+
+
+def feed_body(
+    lengths, two, attended, cotangent, expand_w, expand_b, shrink_w, dense_w,
+    partial_out, attended_g, hidden_g, shrink_g, dense_g, expand_g, expand_bg, bias_g,
+):
+    at = pl.program_id(0)
+
+    @pl.when(at == 0)
+    def _():
+        for total in (shrink_g, dense_g, expand_g, expand_bg, bias_g):
+            total[...] = jnp.zeros(total.shape, F32)
+
+    normed, mixed = two[...], attended[...]
+    hidden = mm(normed, expand_w[...]) + expand_b[...]
+    error = lax.erf(hidden * math.sqrt(0.5))
+    cumulative = 0.5 * (1.0 + error)
+    active = (hidden * cumulative).astype(BF16)
+    put_rows(partial_out, mm(mixed, dense_w[...]) + mm(active, shrink_w[...]))
+    token = at * BLOCK + lax.broadcasted_iota(jnp.int32, (BLOCK, D), 0)
+    seed = jnp.where(token < lengths[0], token_rows(cotangent).astype(F32), 0.0)
+    bias_g[...] += jnp.sum(seed, axis=0, keepdims=True)
+    seed = seed.astype(BF16)
+    attended_g[...] = mm(seed, dense_w[...], ((1,), (1,))).astype(BF16)
+    slope = cumulative + hidden * jnp.exp(-0.5 * hidden * hidden) * (1.0 / math.sqrt(2.0 * math.pi))
+    back = (mm(seed, shrink_w[...], ((1,), (1,))) * slope).astype(BF16)
+    hidden_g[...] = back
+    expand_bg[...] += jnp.sum(back.astype(F32), axis=0, keepdims=True)
+    shrink_g[...] += mm(active, seed, ((0,), (0,)))
+    dense_g[...] += mm(mixed, seed, ((0,), (0,)))
+    expand_g[...] += mm(normed, back, ((0,), (0,)))
+
+
+def mixed_back_body(
+    tokens, one, query_g, key_g, value_g, hidden_g, vectors, qkv_w, expand_w, cos, sin,
+    partial_out, qkv_g, qkv_bg, vector_g,
+):
+    at = pl.program_id(0)
+
+    @pl.when(at == 0)
+    def _():
+        for total in (qkv_g, qkv_bg, vector_g):
+            total[...] = jnp.zeros(total.shape, F32)
+
+    pair = jnp.concatenate([query_g[...].astype(F32), key_g[...].astype(F32)], axis=1)
+    pair = turned(pair, cos[...], -sin[...])
+    values = value_g[...].astype(F32)
+    mixed_g = jnp.concatenate([pair, values, jnp.zeros_like(values)], axis=1)
+    mixed_low = mixed_g.astype(BF16)
+    qkv_bg[...] += jnp.sum(mixed_low.astype(F32), axis=0, keepdims=True)
+    qkv_g[...] += mm(one[...], mixed_low, ((0,), (0,)))
+    one_g = mm(mixed_low, qkv_w[...], ((1,), (1,)))
+    two_g = mm(hidden_g[...], expand_w[...], ((1,), (1,)))
+    unit = normalized(token_rows(tokens).astype(F32))
+    vector_g[0:1] += jnp.sum(one_g * unit, axis=0, keepdims=True)
+    vector_g[1:2] += jnp.sum(one_g, axis=0, keepdims=True)
+    vector_g[2:3] += jnp.sum(two_g * unit, axis=0, keepdims=True)
+    vector_g[3:4] += jnp.sum(two_g, axis=0, keepdims=True)
+    put_rows(partial_out, one_g * vectors[0:1] + two_g * vectors[2:3])
+
+
+def split_mesh(mesh):
+    groups, members = mesh.shape["blk"], mesh.shape["uly"]
+    return Mesh(mesh.devices.reshape(groups // 2, 2, members // 2, 2), ALL)
+
+
+def across_x(block):
+    return lax.ppermute(block, "x", [(0, 1), (1, 0)])
+
+
+def by_head(residual, cotangent, lengths, positions, masters, momenta, averages):
+    slots, span, width = residual.shape
+    x = lax.axis_index("x")
+    head = lax.axis_index("core") * 8 + lax.axis_index("z") * 2 + lax.axis_index("y")
+    owner = x * 16 + head
+    groups = lax.axis_size("z") * lax.axis_size("y")
+    count = groups * 4 * span
+    chunk = masters.shape[0]
+    length = lax.dynamic_slice_in_dim(lengths, x, 1)
+
+    def to_slot(rows):
+        mine = lax.dynamic_index_in_dim(rows, x, 0, keepdims=False)
+        theirs = across_x(lax.dynamic_index_in_dim(rows, 1 - x, 0, keepdims=False))
+        both = jnp.where(x == 0, jnp.stack([mine, theirs]), jnp.stack([theirs, mine]))
+        return lax.all_gather(both, RING, axis=0).reshape(2, groups, 2, span, width)
+
+    def to_tokens(partial_rows):
+        rows = lax.psum_scatter(partial_rows.reshape(16, 2, span, width), RING, scatter_dimension=0, tiled=True)[0]
+        mine = lax.dynamic_index_in_dim(rows, x, 0, keepdims=False)
+        theirs = across_x(lax.dynamic_index_in_dim(rows, 1 - x, 0, keepdims=False))
+        return jnp.where(x == 0, jnp.stack([mine, theirs]), jnp.stack([theirs, mine])).astype(F32)
+
+    onward = [(i, i + 1) for i in range(OWNERS - 1)]
+    backward = [(i + 1, i) for i in range(OWNERS - 1)]
+    before = lax.ppermute(masters[chunk - D :], ALL, onward)
+    after = lax.ppermute(masters[: 4 * D], ALL, backward)
+    total = 410 * D
+    source = jnp.concatenate(
+        [jnp.zeros((7 * D,), F32), before, masters, after, jnp.zeros((total - 12 * D - chunk,), F32)]
+    ).reshape(total // LANES, LANES)
+    skipped = jnp.where(owner < 8, 4, jnp.where(owner < 11, 7, jnp.where(owner < 22, 8, 12)))
+    kind = jnp.where(
+        owner < 8,
+        PROJECT,
+        jnp.where(
+            owner == 10,
+            PLAIN_EXPAND,
+            jnp.where(owner == 21, EXPAND_PLAIN, jnp.where((owner > 10) & (owner < 21), EXPAND, PLAIN)),
+        ),
+    )
+    vector_row = jnp.where(owner == 10, 2080, jnp.where(owner == 21, 1056, jnp.where(owner == 31, 3104, 0)))
+    ahead = skipped * D - (chunk - PER * D) * owner
+    begin = ahead + 4 * D
+    scalars = jnp.stack([begin // LANES, begin % LANES, kind, vector_row]).astype(jnp.int32)
+    high = (positions // 256).astype(BF16).reshape(1, 2 * span)
+    rest = (positions % 256).astype(BF16).reshape(1, 2 * span)
+    places = jnp.concatenate([high, rest, jnp.zeros((14, 2 * span), BF16)])
+    sent = call(
+        weights_out_body, (1,),
+        [whole(source.shape), whole(places.shape)],
+        whole((16, SEND_ROWS, LANES)),
+        shaped((16, SEND_ROWS, LANES), BF16),
+        [pltpu.VMEM((SHIFT_ROWS, LANES), F32)], 1, "weights_out",
+    )(scalars, source, places)
+    got = lax.all_to_all(jnp.concatenate([sent, sent]), ALL, 0, 0, tiled=True)
+    slot_tokens = to_slot(residual)
+    slot_cotangent = to_slot(cotangent)
+    head_scalar = head.astype(jnp.int32).reshape(1)
+    qkv_w, expand_w, second, vectors, qkv_b, expand_b = call(
+        weights_in_body, (1,),
+        [whole(got.shape)],
+        [whole((D, 256)), whole((D, 256)), whole((16, 160, LANES)), whole((8, D)), whole((1, 256)), whole((1, 256))],
+        [shaped((D, 256), BF16), shaped((D, 256), BF16), shaped((16, 160, LANES), BF16), shaped((8, D), F32),
+         shaped((1, 256), F32), shaped((1, 256), F32)],
+        [pltpu.VMEM((24, LANES), F32), pltpu.VMEM((32, LANES), F32)], 1, "weights_in",
+    )(head_scalar, got)
+    second = lax.all_to_all(second, RING, 0, 0, tiled=True)
+    dense_w, shrink_w = call(
+        rows_in_body, (1,), [whole(second.shape)], [whole((HD, D)), whole((256, D))],
+        [shaped((HD, D), BF16), shaped((256, D), BF16)], name="rows_in",
+    )(second)
+
+    halves = got[:, PIECE + 32 : PIECE + 34].astype(F32).reshape(2, 2, groups, 2, slots, span)
+    halves = lax.dynamic_index_in_dim(halves, x, 4, keepdims=False)
+    place = (halves[:, :, :, 0] * 256.0 + halves[:, :, :, 1]).transpose(2, 0, 1, 3).reshape(count)
+    half_dims = ROT // 2
+    inverse = ROTARY_BASE ** (-(jnp.arange(half_dims, dtype=F32) * 2.0 / ROT))
+    angles = place[:, None] * inverse
+    cos, sin = jnp.cos(angles), jnp.sin(angles)
+    flat_part = jnp.ones((count, HD - ROT), F32)
+    cos = jnp.concatenate([cos, cos, flat_part] * 2, axis=1)
+    sin = jnp.concatenate([sin, sin, 0.0 * flat_part] * 2, axis=1)
+
+    steps = (count // BLOCK,)
+    token_spec = pl.BlockSpec((2, 1, 2, span, width), lambda i, *_: (0, i, 0, 0, 0))
+    token_shape = shaped((2, groups, 2, span, width), BF16)
+
+    def rows_spec(columns):
+        return pl.BlockSpec((BLOCK, columns), lambda i, *_: (i, 0))
+
+    def columns_spec(rows):
+        return pl.BlockSpec((rows, BLOCK), lambda i, *_: (0, i))
+
+    narrow = shaped((count, HD), BF16)
+    one, two, query, key, value = call(
+        mixed_body, steps,
+        [token_spec, whole((8, D)), whole((D, 256)), whole((1, 256)), rows_spec(LANES), rows_spec(LANES)],
+        [rows_spec(D), rows_spec(D), rows_spec(HD), rows_spec(HD), rows_spec(HD)],
+        [shaped((count, D), BF16), shaped((count, D), BF16), narrow, narrow, narrow], name="mixed",
+    )(slot_tokens, vectors, qkv_w, qkv_b, cos, sin)
+    attended, attended_full, log_total = call(
+        attend_body, steps,
+        [rows_spec(HD), whole((count, HD)), whole((count, HD))],
+        [rows_spec(HD), columns_spec(HD), columns_spec(1)],
+        [narrow, shaped((HD, count), F32), shaped((1, count), F32)],
+        [pltpu.VMEM((count, BLOCK), F32), pltpu.VMEM((HD, count), BF16)], 1, "attend",
+    )(length, query, key, value)
+    partial_out, attended_g, hidden_g, shrink_g, dense_g, expand_g, expand_bg, bias_g = call(
+        feed_body, steps,
+        [rows_spec(D), rows_spec(HD), token_spec, whole((D, 256)), whole((1, 256)), whole((256, D)), whole((HD, D))],
+        [token_spec, rows_spec(HD), rows_spec(256), whole((256, D)), whole((HD, D)), whole((D, 256)),
+         whole((1, 256)), whole((1, D))],
+        [token_shape, narrow, shaped((count, 256), BF16), shaped((256, D), F32), shaped((HD, D), F32),
+         shaped((D, 256), F32), shaped((1, 256), F32), shaped((1, D), F32)], (), 1, "feed",
+    )(length, two, attended, slot_cotangent, expand_w, expand_b, shrink_w, dense_w)
+    out_rows = to_tokens(partial_out)
+    query_g, key_g, value_g = call(
+        attend_back_body, steps,
+        [rows_spec(HD), whole((count, HD)), whole((count, HD)), rows_spec(HD), columns_spec(HD), columns_spec(1)],
+        [rows_spec(HD), whole((count, HD)), whole((count, HD))],
+        [narrow, narrow, narrow],
+        [pltpu.VMEM((HD, count), BF16), pltpu.VMEM((count, HD), F32), pltpu.VMEM((count, HD), F32)],
+        1, "attend_back",
+    )(length, query, key, value, attended_g, attended_full, log_total)
+    partial_in, qkv_g, qkv_bg, vector_g = call(
+        mixed_back_body, steps,
+        [token_spec, rows_spec(D), rows_spec(HD), rows_spec(HD), rows_spec(HD), rows_spec(256), whole((8, D)),
+         whole((D, 256)), whole((D, 256)), rows_spec(LANES), rows_spec(LANES)],
+        [token_spec, whole((D, 256)), whole((1, 256)), whole((8, D))],
+        [token_shape, shaped((D, 256), F32), shaped((1, 256), F32), shaped((8, D), F32)], name="mixed_back",
+    )(slot_tokens, one, query_g, key_g, value_g, hidden_g, vectors, qkv_w, expand_w, cos, sin)
+    in_rows = to_tokens(partial_in)
+
+    second_g = call(
+        rows_out_body, (1,), [whole((HD, D)), whole((256, D))], whole((16, 160, LANES)),
+        shaped((16, 160, LANES), BF16), name="rows_out",
+    )(dense_g, shrink_g)
+    second_g = lax.all_to_all(second_g, RING, 0, 0, tiled=True)
+    bias_g = jnp.where(head == 0, bias_g, 0.0)
+    vector_g = jnp.concatenate([vector_g[:4], bias_g, jnp.zeros((3, D), F32)])
+    sent_g = call(
+        grads_out_body, (1,),
+        [whole((16, 160, LANES)), whole((D, 256)), whole((D, 256)), whole((8, D)), whole((1, 256)), whole((1, 256))],
+        whole((OWNERS, BACK_ROWS, LANES)),
+        shaped((OWNERS, BACK_ROWS, LANES), BF16),
+        [pltpu.VMEM((32, LANES), F32), pltpu.VMEM((32, LANES), F32)], 1, "grads_out",
+    )(head_scalar, second_g, qkv_g, expand_g, vector_g, qkv_bg, expand_bg)
+    got_g = lax.all_to_all(sent_g, ALL, 0, 0, tiled=True)
+    begin_g = (chunk - PER * D) * owner - skipped * D + 4 * D
+    scalars_g = jnp.stack([begin_g // LANES, begin_g % LANES, kind, vector_row]).astype(jnp.int32)
+    taken = call(
+        grads_in_body, (1,), [whole(got_g.shape)], whole((TAKE_ROWS, LANES)), shaped((TAKE_ROWS, LANES), F32),
+        [pltpu.VMEM((SHIFT_ROWS, LANES), F32)], 1, "grads_in",
+    )(scalars_g, got_g).reshape(-1)
+    from_before = lax.ppermute(taken[D + chunk : 5 * D + chunk], ALL, onward)
+    from_after = lax.ppermute(taken[:D], ALL, backward)
+    gradients = taken[D : D + chunk]
+    gradients = gradients.at[: 4 * D].add(from_before).at[chunk - D :].add(from_after)
+
+    values = residual.astype(F32)
+    outputs = (values + out_rows + (vectors[4] + vectors[5])).astype(BF16)
+    first_token = ((lax.axis_index("z") * 2 + lax.axis_index("y")) * 4 + x * 2 + lax.axis_index("core")) * span
+    token = first_token + jnp.arange(span, dtype=jnp.int32)
+    live = token[None, :] < lengths[:, None]
+    seed = jnp.where(live[:, :, None], cotangent.astype(F32), 0.0)
+    centered = values - jnp.mean(values, axis=-1, keepdims=True)
+    scale = lax.rsqrt(jnp.mean(centered * centered, axis=-1, keepdims=True) + EPSILON)
+    unit = centered * scale
+    back = in_rows - jnp.mean(in_rows, axis=-1, keepdims=True)
+    back = scale * (back - unit * jnp.mean(in_rows * unit, axis=-1, keepdims=True))
+    input_grad = (seed + back).astype(BF16)
+
+    velocity = MOMENTUM * momenta + gradients
+    step_rate = LEARN_RATE / math.sqrt(slots * count)
+    updated = masters - step_rate * (gradients + MOMENTUM * velocity)
+    averaged = AVERAGE_DECAY * averages + (1.0 - AVERAGE_DECAY) * updated
+    return (outputs, input_grad, gradients, updated, velocity, averaged)
+
+
 def solution(mesh):
-    return jax.shard_map(
-        local,
-        mesh=mesh,
-        in_specs=(
-            P(None, ("uly", "blk"), None),
-            P(None, ("uly", "blk"), None),
-            P(),
-            P(None, ("uly", "blk")),
-            P(("blk", "uly")),
-            P(("blk", "uly")),
-            P(("blk", "uly")),
-        ),
-        out_specs=(
-            P(None, ("uly", "blk"), None),
-            P(None, ("uly", "blk"), None),
-            P(("blk", "uly")),
-            P(("blk", "uly")),
-            P(("blk", "uly")),
-            P(("blk", "uly")),
-        ),
-        check_vma=False,
-    )
+    def step(*args):
+        slots, tokens = args[0].shape[:2]
+        if mesh.size == OWNERS == slots * H and mesh.shape["blk"] == 4 and tokens == 64 * OWNERS:
+            tokens_in, flat, used, body = P(None, ("z", "y", "x", "core"), None), P(ALL), split_mesh(mesh), by_head
+            places = P(None, ("z", "y", "x", "core"))
+        else:
+            tokens_in, flat, used, body = P(None, ("uly", "blk"), None), P(("blk", "uly")), mesh, local
+            places = P(None, ("uly", "blk"))
+        return jax.shard_map(
+            body,
+            mesh=used,
+            in_specs=(tokens_in, tokens_in, P(), places, flat, flat, flat),
+            out_specs=(tokens_in, tokens_in, flat, flat, flat, flat),
+            check_vma=False,
+        )(*args)
+
+    return step

time: 1680 us -> 418 us (0.25)
  waiting for transfers between devices: 1140 us -> 139 us
  local copies, waits for them, and re-layouts: 260 us -> 30.1 us
  Pallas kernels: 0 us -> 106 us
  matrix products: 80 us -> 0 us
  blocking collectives: 0 us -> 71.3 us
  other arithmetic: 94.3 us -> 23.2 us
  loops' own time: 43.7 us -> 0 us
    unnamed x4, waiting for transfers between devices: 1110 us -> 0.07 us
    pallas_call x0 -> x11, Pallas kernels: none -> 106 us  [the longest x1 19.3 us: by_head(): call(attend_back_body, steps, [rows_spec(HD), whole((count, HD)), whole((...]
    unnamed x128 -> x20, local copies, waits for them, and re-layouts: 90.7 us -> 2.13 us
    all_to_all x4 -> x3, waiting for transfers between devices: 0.01 us -> 83.7 us  [the longest x1 59.5 us: by_head(): got_g = lax.all_to_all(sent_g, ALL, 0, 0, tiled=True)]
    dot_general x68 -> x0, matrix products: 80 us -> none  [the longest x16 11 us: block_scores(): jnp.einsum('qhd,khd->hqk', queries, keys_rows, preferred_element_type=jnp...]
    all_to_all x0 -> x1, blocking collectives: none -> 71.3 us  [by_head(): got = lax.all_to_all(jnp.concatenate([sent, sent]), ALL, 0, 0, tiled=True)]
    slice x54 -> x6, local copies, waits for them, and re-layouts: 61 us -> 4.46 us  [the longest x1 2.9 us: by_head(): gradients = taken[D:D + chunk]]
    another operation x39 -> x0, loops' own time: 43.7 us -> none  [the longest x4 10.9 us: fold_values(): return lax.map(per_slot, (attended, queries, key_value, log_total, lengths))]
  transfers between devices with their start and end apart: 19 -> 15, of which waited for: 8 -> 9; matrix products, arithmetic and copies ran while one was open for 15% -> 11% of each run, Pallas kernels for 0% -> 14%
where the time goes in v1:
time: 418 us; the launch traced here: 416 us
  waiting for transfers between devices  139 us (33%)
  Pallas kernels  106 us (25%)
  blocking collectives  71.3 us (17%)
  starting transfers between devices  31.1 us (7%)
  local copies, waits for them, and re-layouts  30.1 us (7%)
  other arithmetic  23.2 us (6%)
  between operations  14.2 us (3%)
    all_to_all x1, blocking collectives, by_head(): got = lax.all_to_all(jnp.concatenate([sent, sent]), ALL, 0, 0, tiled=True)  71.3 us
    all_to_all x1, waiting for transfers between devices, by_head(): got_g = lax.all_to_all(sent_g, ALL, 0, 0, tiled=True)  59.5 us
    reduce_scatter x2, waiting for transfers between devices, to_tokens(): lax.psum_scatter(partial_rows.reshape(16, 2, span, width), RING, scatter_...  41.2 us
    pallas_call x1, Pallas kernels, by_head(): call(attend_back_body, steps, [rows_spec(HD), whole((count, HD)), whole((...  19.3 us
    pallas_call x1, Pallas kernels, by_head(): call(attend_body, steps, [rows_spec(HD), whole((count, HD)), whole((count...  18.1 us
    all_to_all x1, waiting for transfers between devices, by_head(): second_g = lax.all_to_all(second_g, RING, 0, 0, tiled=True)  17.4 us
    pallas_call x1, Pallas kernels, by_head(): call(feed_body, steps, [rows_spec(D), rows_spec(HD), token_spec, whole((D...  16.8 us
    pallas_call x1, Pallas kernels, by_head(): call(mixed_back_body, steps, [token_spec, rows_spec(D), rows_spec(HD), ro...  13.3 us
  transfers between devices with their start and end apart: 15, of which 9 were waited for; matrix products, arithmetic and copies ran while one was open for 11% of the time, Pallas kernels for 14%

profile of v1, /device:TPU:0, one launch (start us, length us, event | category | flops | bytes accessed | tf_op | source)
XLA Modules:
  0.0 415.8 jit_solution(15175207134590643940)
XLA Ops:
  8.3 3.0 collective-permute-start
  11.4 3.5 collective-permute-done
  18.5 3.2 collective-permute-done.3
  22.5 3.7 collective-permute-start.1
  31.9 11.6 %concatenate.50 = f32[419840]{0:T(1024)} concatenate(f32[7168]{0:T(1024)S(1)} %broadcast_in_dim.40, f32[1024]{0:T(1024)S(1)} %collective-permute-done.1, f32[393632]{0:T(1024)S(1)} %copy-done.2, f32[4096]{0:T(1024)S(1)} %collective-permute-done.2, f32[13920]{0:T(1024)S(1)} %broadcast_in_dim.41), dimensions={0} | concatenate | bytes 3358720 | tf_op jit(solution)/shard_map/concatenate | solution.py:1041
  43.4 7.2 %weights_out.1 = bf16[16,240,128]{2,1,0:T(8,128)(2,1)} custom-call(s32[4]{0:T(128)} %add_add_fusion.scalars, f32[3280,128]{1,0:T(8,128)} %bitcast.51, bf16[16,128]{1,0:T(8,128)(2,1)} %maximum_maximum_fusion.1.places), custom_call_target="tpu_custom_call" | custom-call | tf_op jit(solution)/shard_map/weights_out/pallas_call | solution.py:1061
  52.3 71.3 %all_to_all.20.got = bf16[32,240,128]{2,1,0:T(8,128)(2,1)} all-to-all(bf16[32,240,128]{2,1,0:T(8,128)(2,1)S(1)} %pad_maximum_fusion), channel_id=1, replica_groups=mesh['x'=2,'core'=2,'z'=4,'y'=2] {'x','core','z','y'}, dimensions={0} | all-to-all | bytes 3932160 | tf_op jit(solution)/shard_map/all_to_all | solution.py:1068
  123.6 3.0 weights_in.1
  126.7 5.1 %all-to-all-start.1 = ((bf16[16,160,128]{2,1,0:T(8,128)(2,1)}), bf16[16,160,128]{2,1,0:T(8,128)(2,1)}, u32[]{:S(2)}, u32[]{:S(2)}) async-start(bf16[16,160,128]{2,1,0:T(8,128)(2,1)} %get-tuple-element.71), calls=%async_computation.1 | async-start | bytes 1310720 | tf_op jit(solution)/shard_map/all_to_all | solution.py:1080
  133.8 3.7 multiply_sine_fusion
  143.5 6.8 %all-to-all-done.1.got = bf16[16,160,128]{2,1,0:T(8,128)(2,1)} async-done(((bf16[16,160,128]{2,1,0:T(8,128)(2,1)}), bf16[16,160,128]{2,1,0:T(8,128)(2,1)}, u32[]{:S(2)}, u32[]{:S(2)}) %all-to-all-start.1) | async-done | bytes 655392 | tf_op jit(solution)/shard_map/all_to_all | solution.py:1080
  152.5 10.6 %mixed.1 = (bf16[2048,1024]{1,0:T(8,128)(2,1)}, bf16[2048,1024]{1,0:T(8,128)(2,1)}, bf16[2048,64]{1,0:T(8,128)(2,1)}, bf16[2048,64]{1,0:T(8,128)(2,1)}, bf16[2048,64]{1,0:T(8,128)(2,1)}) custom-call(bf16[2,8,2,64,1024]{4,3,2,1,0:T(8,128)(2,1)} %bitcast.49, f32[8,1024]{1,0:T(8,128)} %get-tuple-element.61.vectors, bf16[1024,256]{1,0:T(8,128)(2,1)} %get-tuple-element.62.qkv_w, ...), custom_call_target="tpu_custom_call" | custom-call | tf_op jit(solution)/shard_map/mixed/pallas_call | solution.py:1108
  163.1 18.1 %attend.1 = (bf16[2048,64]{1,0:T(8,128)(2,1)}, f32[64,2048]{1,0:T(8,128)}, f32[1,2048]{1,0:T(1,128)}) custom-call(s32[1]{0:T(128)} %dynamic_slice.36.lengths, bf16[2048,64]{1,0:T(8,128)(2,1)} %get-tuple-element.65.query, bf16[2048,64]{1,0:T(8,128)(2,1)} %get-tuple-element.66.key, bf16[2048,64]{1,0:T(8,128)(2,1)} %get-tuple-element.67.value), custom_call_target="tpu_custom_call" | custom-call | tf_op jit(solution)/shard_map/attend/pallas_call | solution.py:1114
  181.2 16.8 %feed.1 = (bf16[2,8,2,64,1024]{4,3,2,1,0:T(8,128)(2,1)}, bf16[2048,64]{1,0:T(8,128)(2,1)}, bf16[2048,256]{1,0:T(8,128)(2,1)}, f32[256,1024]{1,0:T(8,128)}, f32[6...) custom-call(s32[1]{0:T(128)} %dynamic_slice.36.lengths, ...), custom_call_target="tpu_custom_call" | custom-call | tf_op jit(solution)/shard_map/feed/pallas_call | solution.py:1121
  198.0 19.3 %attend_back.1 = (bf16[2048,64]{1,0:T(8,128)(2,1)}, bf16[2048,64]{1,0:T(8,128)(2,1)}, bf16[2048,64]{1,0:T(8,128)(2,1)}) custom-call(s32[1]{0:T(128)} %dynamic_slice.36.lengths, bf16[2048,64]{1,0:T(8,128)(2,1)} %get-tuple-element.65.query, bf16[2048,64]{1,0:T(8,128)(2,1)} %get-tuple-element.66.key, bf16[2048,64]{1,0:T(8,128)(2,1)} %get-tuple-element.67.value, ...), custom_call_target="tpu_custom_call" | custom-call | tf_op jit(solution)/shard_map/attend_back/pallas_call | solution.py:1130
  217.4 13.3 %mixed_back.1 = (bf16[2,8,2,64,1024]{4,3,2,1,0:T(8,128)(2,1)}, f32[1024,256]{1,0:T(8,128)}, f32[1,256]{1,0:T(1,128)}, f32[8,1024]{1,0:T(8,128)}) custom-call(bf16[2,8,2,64,1024]{4,3,2,1,0:T(8,128)(2,1)} %bitcast.50, bf16[2048,1024]{1,0:T(8,128)(2,1)} %get-tuple-element.75.one, bf16[2048,64]{1,0:T(8,128)(2,1)} %get-tuple-element.79.query_g, ...), custom_call_target="tpu_custom_call" | custom-call | tf_op jit(solution)/shard_map/mixed_back/pallas_call | solution.py:1138
  233.1 3.8 all-to-all-start.2
  237.8 17.4 %all-to-all-done.2.second = bf16[16,160,128]{2,1,0:T(8,128)(2,1)S(1)} async-done(((bf16[16,160,128]{2,1,0:T(8,128)(2,1)}), bf16[16,160,128]{2,1,0:T(8,128)(2,1)S(1)}, u32[]{:S(2)}, u32[]{:S(2)}) %all-to-all-start.2) | async-done | bytes 655392 | tf_op jit(solution)/shard_map/all_to_all | solution.py:1151
  256.0 5.3 %grads_out.1 = bf16[32,224,128]{2,1,0:T(8,128)(2,1)} custom-call(s32[1]{0:T(128)} %bitcast.4.scalars, bf16[16,160,128]{2,1,0:T(8,128)(2,1)} %copy-done.4, f32[1024,256]{1,0:T(8,128)} %get-tuple-element.86.qkv_g, f32[1024,256]{1,0:T(8,128)} %get-tuple-element.87.expand_g, f32[8,1024]{1,0:T(8,128)} %maximum_maximum_fusion.vector_g, ...), custom_call_target="tpu_custom_call" | custom-call | tf_op jit(solution)/shard_map/grads_out/pallas_call | solution.py:1154
  267.3 59.5 %all-to-all-done.3.got = bf16[32,224,128]{2,1,0:T(8,128)(2,1)S(1)} async-done(((bf16[32,224,128]{2,1,0:T(8,128)(2,1)}), bf16[32,224,128]{2,1,0:T(8,128)(2,1)S(1)}, u32[]{:S(2)}, u32[]{:S(2)}) %all-to-all-start.3) | async-done | bytes 1835040 | tf_op jit(solution)/shard_map/all_to_all | solution.py:1161
  328.1 8.1 %grads_in.1 = f32[3120,128]{1,0:T(8,128)} custom-call(s32[4]{0:T(128)} %add_add_fusion.1.scalars, bf16[32,224,128]{2,1,0:T(8,128)(2,1)} %copy-done), custom_call_target="tpu_custom_call" | custom-call | tf_op jit(solution)/shard_map/grads_in/pallas_call | solution.py:1164
  351.0 4.5 %collective-permute-start.5 = (bf16[64,1024]{1,0:T(8,128)(2,1)}, bf16[64,1024]{1,0:T(8,128)(2,1)}, u32[]{:S(2)}, u32[]{:S(2)}) collective-permute-start(bf16[64,1024]{1,0:T(8,128)(2,1)} %get-tuple-element.99), channel_id=1, source_target_pairs={{0,16},{16,0},{1,17},{17,1},{2,18},{18,2},{3,19},{19,3},{4,20},{20... | collective-permute-start | bytes 393224 | tf_op jit(solution)/shard_map/ppermute | solution.py:1011
  355.6 4.4 %add_multiply_fusion = (f32[393632]{0:T(1024)}, f32[393632]{0:T(1024)}, f32[393632]{0:T(1024)}) fusion(f32[393632]{0:T(1024)S(1)} %copy-done.5, f32[393632]{0:T(1024)S(1)} %copy-done.3, f32[393632]{0:T(1024)} %fusion.14, f32[393632]{0:T(1024)} %param.16), kind=kLoop, calls=%fused_computation.1 | loop fusion | flops 3149056 | bytes 11021696 | tf_op jit(solution)/shard_map/add | solution.py:1189
  360.0 41.2 %reduce-scatter.3.cloned.1.call-done = bf16[1,2,64,1024]{3,2,1,0:T(8,128)(2,1)} async-done(((bf16[16,2,64,1024]{3,2,1,0:T(8,128)(2,1)}), bf16[1,2,64,1024]{3,2,1,0:T(8,128)(2,1)}) %reduce-scatter.3.cloned.1.call-update) | async-done | bytes 262160 | tf_op jit(solution)/shard_map/reduce_scatter | solution.py:1031
  (96 shorter events, 57.1 us)
Async XLA Ops:
  7.2 15.3 %copy-start.2 = (f32[393632]{0:T(1024)S(1)}, f32[393632]{0:T(1024)}, u32[]{:S(2)}) copy-start(f32[393632]{0:T(1024)} %param.15) | copy-start | bytes 4723588
  7.2 20.4 %copy-start.8 = (s32[2,64]{1,0:T(2,128)S(1)}, s32[2,64]{1,0:T(2,128)}, u32[]{:S(2)}) copy-start(s32[2,64]{1,0:T(2,128)} %param.14) | copy-start | bytes 1540
  7.2 145.4 %all-gather.3.cloned.1.call-start = ((), (), s32[]{:S(2)}) async-start(), calls=%async_computation.6 | async-start | bytes 4456448 | tf_op jit(solution)/shard_map/all_gather | solution.py:1028
  8.3 6.5 %collective-permute-start = (bf16[64,1024]{1,0:T(8,128)(2,1)S(1)}, bf16[64,1024]{1,0:T(8,128)(2,1)S(1)}, u32[]{:S(2)}, u32[]{:S(2)}) collective-permute-start(bf16[64,1024]{1,0:T(8,128)(2,1)S(1)} %get-tuple-element.106), channel_id=1, source_target_pairs={{0,16},{16,0},{1,17},{17,1},{2,18},{18,2},{3,19},{19,3},{4,20},{20... | collective-permute-start | bytes 393224 | tf_op jit(solution)/shard_map/ppermute | solution.py:1011
  15.6 165.6 %all-gather.5.cloned.1.call-start = ((), (), s32[]{:S(2)}) async-start(), calls=%async_computation.7 | async-start | bytes 4456448 | tf_op jit(solution)/shard_map/all_gather | solution.py:1028
  16.7 5.0 %collective-permute-start.3 = (bf16[64,1024]{1,0:T(8,128)(2,1)S(1)}, bf16[64,1024]{1,0:T(8,128)(2,1)S(1)}, u32[]{:S(2)}, u32[]{:S(2)}) collective-permute-start(bf16[64,1024]{1,0:T(8,128)(2,1)S(1)} %get-tuple-element.104), channel_id=1, source_target_pairs={{0,16},{16,0},{1,17},{17,1},{2,18},{18,2},{3,19},{19,3},{4,20},{20... | collective-permute-start | bytes 393224 | tf_op jit(solution)/shard_map/ppermute | solution.py:1011
  22.5 6.6 %collective-permute-start.1 = (f32[1024]{0:T(1024)S(1)}, f32[1024]{0:T(1024)S(1)}, u32[]{:S(2)}, u32[]{:S(2)}) collective-permute-start(f32[1024]{0:T(1024)S(1)} %slice.66), channel_id=1, source_target_pairs={{0,1},{1,2},{2,3},{3,4},{4,5},{5,6},{6,7},{7,8},{8,9},{9,10},{10,1... | collective-permute-start | bytes 12296 | tf_op jit(solution)/shard_map/ppermute | solution.py:1038
  26.2 5.6 %collective-permute-start.2 = (f32[4096]{0:T(1024)S(1)}, f32[4096]{0:T(1024)S(1)}, u32[]{:S(2)}, u32[]{:S(2)}) collective-permute-start(f32[4096]{0:T(1024)S(1)} %slice.67), channel_id=1, source_target_pairs={{1,0},{2,1},{3,2},{4,3},{5,4},{6,5},{7,6},{8,7},{9,8},{10,9},{11,1... | collective-permute-start | bytes 49160 | tf_op jit(solution)/shard_map/ppermute | solution.py:1039
  123.6 8.4 %copy-start.9 = (s32[2]{0:T(128)S(1)}, s32[2]{0:T(128)}, u32[]{:S(2)}) copy-start(s32[2]{0:T(128)} %param.13) | copy-start | bytes 28
  126.7 23.7 %all-to-all-start.1 = ((bf16[16,160,128]{2,1,0:T(8,128)(2,1)}), bf16[16,160,128]{2,1,0:T(8,128)(2,1)}, u32[]{:S(2)}, u32[]{:S(2)}) async-start(bf16[16,160,128]{2,1,0:T(8,128)(2,1)} %get-tuple-element.71), calls=%async_computation.1 | async-start | bytes 1310720 | tf_op jit(solution)/shard_map/all_to_all | solution.py:1080
  131.8 217.6 %reduce-scatter.5.cloned.1.call-start = ((), (), s32[]{:S(2)}) async-start(), calls=%async_computation.9 | async-start | bytes 4456448 | tf_op jit(solution)/shard_map/reduce_scatter | solution.py:1031
  230.7 6.3 %copy-start.6 = (f32[8,1024]{1,0:T(8,128)S(1)}, f32[8,1024]{1,0:T(8,128)}, u32[]{:S(2)}) copy-start(f32[8,1024]{1,0:T(8,128)} %get-tuple-element.88) | copy-start | bytes 98308
  230.7 6.3 %copy-start.7 = (f32[1,1024]{1,0:T(1,128)S(1)}, f32[1,1024]{1,0:T(1,128)}, u32[]{:S(2)}) copy-start(f32[1,1024]{1,0:T(1,128)} %get-tuple-element.89) | copy-start | bytes 12292
  233.1 22.1 %all-to-all-start.2 = ((bf16[16,160,128]{2,1,0:T(8,128)(2,1)}), bf16[16,160,128]{2,1,0:T(8,128)(2,1)S(1)}, u32[]{:S(2)}, u32[]{:S(2)}) async-start(bf16[16,160,128]{2,1,0:T(8,128)(2,1)} %rows_out.1), calls=%async_computation.4 | async-start | bytes 1310720 | tf_op jit(solution)/shard_map/all_to_all | solution.py:1151
  261.4 3.5 copy-start.1
  261.4 65.4 %all-to-all-start.3 = ((bf16[32,224,128]{2,1,0:T(8,128)(2,1)}), bf16[32,224,128]{2,1,0:T(8,128)(2,1)S(1)}, u32[]{:S(2)}, u32[]{:S(2)}) async-start(bf16[32,224,128]{2,1,0:T(8,128)(2,1)} %grads_out.1), calls=%async_computation.5 | async-start | bytes 3670016 | tf_op jit(solution)/shard_map/all_to_all | solution.py:1161
  264.2 136.9 %reduce-scatter.3.cloned.1.call-start = ((), (), s32[]{:S(2)}) async-start(), calls=%async_computation.8 | async-start | bytes 4456448 | tf_op jit(solution)/shard_map/reduce_scatter | solution.py:1031
  326.8 1.3 copy-start
  336.9 6.7 %collective-permute-start.6 = (f32[4096]{0:T(1024)S(1)}, f32[4096]{0:T(1024)S(1)}, u32[]{:S(2)}, u32[]{:S(2)}) collective-permute-start(f32[4096]{0:T(1024)S(1)} %slice.85), channel_id=1, source_target_pairs={{0,1},{1,2},{2,3},{3,4},{4,5},{5,6},{6,7},{7,8},{8,9},{9,10},{10,1... | collective-permute-start | bytes 49160 | tf_op jit(solution)/shard_map/ppermute | solution.py:1168
  339.4 16.1 %copy-start.3 = (f32[393632]{0:T(1024)S(1)}, f32[393632]{0:T(1024)}, u32[]{:S(2)}) copy-start(f32[393632]{0:T(1024)} %param.15) | copy-start | bytes 4723588
  339.4 16.1 %copy-start.5 = (f32[393632]{0:T(1024)S(1)}, f32[393632]{0:T(1024)}, u32[]{:S(2)}) copy-start(f32[393632]{0:T(1024)} %param.17) | copy-start | bytes 4723588
  342.3 5.5 %collective-permute-start.7 = (f32[1024]{0:T(1024)S(1)}, f32[1024]{0:T(1024)S(1)}, u32[]{:S(2)}, u32[]{:S(2)}) collective-permute-start(f32[1024]{0:T(1024)S(1)} %slice_bitcast_fusion.1), channel_id=1, source_target_pairs={{1,0},{2,1},{3,2},{4,3},{5,4},{6,5},{7,6},{8,7},{9,8},{10,9},{11,1... | collective-permute-start | bytes 12296 | tf_op jit(solution)/shard_map/ppermute | solution.py:1169
  351.0 52.7 %collective-permute-start.5 = (bf16[64,1024]{1,0:T(8,128)(2,1)}, bf16[64,1024]{1,0:T(8,128)(2,1)}, u32[]{:S(2)}, u32[]{:S(2)}) collective-permute-start(bf16[64,1024]{1,0:T(8,128)(2,1)} %get-tuple-element.99), channel_id=1, source_target_pairs={{0,16},{16,0},{1,17},{17,1},{2,18},{18,2},{3,19},{19,3},{4,20},{20... | collective-permute-start | bytes 393224 | tf_op jit(solution)/shard_map/ppermute | solution.py:1011
  402.1 5.0 %collective-permute-start.4 = (bf16[64,1024]{1,0:T(8,128)(2,1)S(1)}, bf16[64,1024]{1,0:T(8,128)(2,1)S(1)}, u32[]{:S(2)}, u32[]{:S(2)}) collective-permute-start(bf16[64,1024]{1,0:T(8,128)(2,1)S(1)} %get-tuple-element.102), channel_id=1, source_target_pairs={{0,16},{16,0},{1,17},{17,1},{2,18},{18,2},{3,19},{19,3},{4,20},{20... | collective-permute-start | bytes 393224 | tf_op jit(solution)/shard_map/ppermute | solution.py:1011
  (1 other events, 0.8 us)
Sparse Core Ops, SparseCore 0:
  15.7 56.4 all-gather.2
  75.0 60.8 all-gather.4
  230.8 94.8 reduce-scatter.4
  329.4 71.6 reduce-scatter.2

commit v2 on v1

--- a/solution.py
+++ b/solution.py
@@ -438,7 +438,7 @@
 BF16 = jnp.bfloat16
 
 
-def call(body, grid, in_specs, out_specs, out_shape, scratch=(), prefetch=0, name=None):
+def call(body, grid, in_specs, out_specs, out_shape, scratch=(), prefetch=0, name=None, aliases=None):
     return pl.pallas_call(
         body,
         grid_spec=pltpu.PrefetchScalarGridSpec(
@@ -450,6 +450,7 @@
         ),
         out_shape=out_shape,
         name=name,
+        input_output_aliases=aliases or {},
         compiler_params=pltpu.CompilerParams(vmem_limit_bytes=56 << 20),
     )
 
@@ -485,6 +486,7 @@
 FLAT = PER * D // LANES
 PIECE = FLAT // 16
 LEAD = 4 * D // LANES
+EDGE = PER * D + 13 * D // OWNERS
 PROJECT, PLAIN, PLAIN_EXPAND, EXPAND, EXPAND_PLAIN = range(5)
 
 
@@ -538,11 +540,30 @@
 
 
 SHIFT_ROWS = 3200
-SEND_ROWS = PIECE + 32 + 16
-
-
-def weights_out_body(scalars, source, places, out, flat):
+SEND_ROWS = PIECE + 32
+OWN_ROW = 64
+
+
+def weights_out_body(scalars, before, own, after, out, source, flat, tail):
     start, shift, kind, vector_row = scalars[0], scalars[1], scalars[2], scalars[3]
+    count = own.shape[0]
+    source[0 : OWN_ROW - 8] = jnp.zeros((OWN_ROW - 8, LANES), F32)
+    source[OWN_ROW - 8 : OWN_ROW] = before[...]
+
+    def copy(step, carry):
+        at = pl.multiple_of(step * 88, 8)
+        source[pl.ds(at + OWN_ROW, 88), :] = own[pl.ds(at, 88), :]
+        return carry
+
+    lax.fori_loop(0, count // 88, copy, 0)
+    last = OWN_ROW + EDGE // LANES
+    source[OWN_ROW + count :] = jnp.zeros((source.shape[0] - OWN_ROW - count, LANES), F32)
+    edge = EDGE % LANES
+    tail[...] = jnp.zeros(tail.shape, F32)
+    tail[7:8] = source[last : last + 1]
+    tail[8:40] = pltpu.roll(after[...], edge, 1)
+    lane = lax.broadcasted_iota(jnp.int32, (40, LANES), 1)
+    source[last : last + 40] = jnp.where(lane < edge, tail[7:47], tail[8:48])
 
     def align(step, carry):
         at = pl.multiple_of(step * 80, 8)
@@ -599,7 +620,6 @@
     vectors = flat[pl.ds(vector_row, 32), :].astype(BF16)
     for r in range(16):
         out[r, PIECE : PIECE + 32] = vectors
-        out[r, PIECE + 32 :] = places[...]
 
 
 def weights_in_body(scalars, got, qkv_w, expand_w, second, vectors, qkv_b, expand_b, project_rows, expand_rows):
@@ -975,7 +995,7 @@
 
 
 def mixed_back_body(
-    tokens, one, query_g, key_g, value_g, hidden_g, vectors, qkv_w, expand_w, cos, sin,
+    partials, tokens, one, query_g, key_g, value_g, hidden_g, vectors, qkv_w, expand_w, cos, sin,
     partial_out, qkv_g, qkv_bg, vector_g,
 ):
     at = pl.program_id(0)
@@ -1021,26 +1041,34 @@
     chunk = masters.shape[0]
     length = lax.dynamic_slice_in_dim(lengths, x, 1)
 
-    def to_slot(rows):
-        mine = lax.dynamic_index_in_dim(rows, x, 0, keepdims=False)
-        theirs = across_x(lax.dynamic_index_in_dim(rows, 1 - x, 0, keepdims=False))
-        both = jnp.where(x == 0, jnp.stack([mine, theirs]), jnp.stack([theirs, mine]))
-        return lax.all_gather(both, RING, axis=0).reshape(2, groups, 2, span, width)
-
-    def to_tokens(partial_rows):
-        rows = lax.psum_scatter(partial_rows.reshape(16, 2, span, width), RING, scatter_dimension=0, tiled=True)[0]
-        mine = lax.dynamic_index_in_dim(rows, x, 0, keepdims=False)
-        theirs = across_x(lax.dynamic_index_in_dim(rows, 1 - x, 0, keepdims=False))
-        return jnp.where(x == 0, jnp.stack([mine, theirs]), jnp.stack([theirs, mine])).astype(F32)
+    def paired(mine, theirs):
+        return jnp.where(x == 0, jnp.stack([mine, theirs]), jnp.stack([theirs, mine]))
+
+    def at_x(rows, index):
+        return lax.dynamic_index_in_dim(rows, index, 0, keepdims=False)
+
+    rows = jnp.stack([residual, cotangent], axis=1)
+    rows = paired(at_x(rows, x), across_x(at_x(rows, 1 - x)))
+    gathered = lax.all_gather(rows, RING, axis=0).reshape(2, groups, 2, 2, span, width)
+
+    place = jnp.broadcast_to(positions.reshape(1, slots * span), (OWNERS, slots * span))
+    place = lax.all_to_all(place, ALL, 0, 0, tiled=True).reshape(2, 2, groups, slots, span)
+    place = lax.dynamic_index_in_dim(place, x, 3, keepdims=False).transpose(2, 0, 1, 3).reshape(count)
+    half_dims = ROT // 2
+    inverse = ROTARY_BASE ** (-(jnp.arange(half_dims, dtype=F32) * 2.0 / ROT))
+    angles = place.astype(F32)[:, None] * inverse
+    cos, sin = jnp.cos(angles), jnp.sin(angles)
+    flat_part = jnp.ones((count, HD - ROT), F32)
+    cos = jnp.concatenate([cos, cos, flat_part] * 2, axis=1)
+    sin = jnp.concatenate([sin, sin, 0.0 * flat_part] * 2, axis=1)
 
     onward = [(i, i + 1) for i in range(OWNERS - 1)]
     backward = [(i + 1, i) for i in range(OWNERS - 1)]
     before = lax.ppermute(masters[chunk - D :], ALL, onward)
     after = lax.ppermute(masters[: 4 * D], ALL, backward)
-    total = 410 * D
-    source = jnp.concatenate(
-        [jnp.zeros((7 * D,), F32), before, masters, after, jnp.zeros((total - 12 * D - chunk,), F32)]
-    ).reshape(total // LANES, LANES)
+    own_rows = -(-chunk // D) * 8
+    own = jnp.pad(masters, (0, own_rows * LANES - chunk)).reshape(own_rows, LANES)
+    before, after = before.reshape(8, LANES), after.reshape(32, LANES)
     skipped = jnp.where(owner < 8, 4, jnp.where(owner < 11, 7, jnp.where(owner < 22, 8, 12)))
     kind = jnp.where(
         owner < 8,
@@ -1055,19 +1083,15 @@
     ahead = skipped * D - (chunk - PER * D) * owner
     begin = ahead + 4 * D
     scalars = jnp.stack([begin // LANES, begin % LANES, kind, vector_row]).astype(jnp.int32)
-    high = (positions // 256).astype(BF16).reshape(1, 2 * span)
-    rest = (positions % 256).astype(BF16).reshape(1, 2 * span)
-    places = jnp.concatenate([high, rest, jnp.zeros((14, 2 * span), BF16)])
     sent = call(
         weights_out_body, (1,),
-        [whole(source.shape), whole(places.shape)],
+        [whole(before.shape), whole(own.shape), whole(after.shape)],
         whole((16, SEND_ROWS, LANES)),
         shaped((16, SEND_ROWS, LANES), BF16),
-        [pltpu.VMEM((SHIFT_ROWS, LANES), F32)], 1, "weights_out",
-    )(scalars, source, places)
+        [pltpu.VMEM((3280, LANES), F32), pltpu.VMEM((SHIFT_ROWS, LANES), F32), pltpu.VMEM((48, LANES), F32)],
+        1, "weights_out",
+    )(scalars, before, own, after)
     got = lax.all_to_all(jnp.concatenate([sent, sent]), ALL, 0, 0, tiled=True)
-    slot_tokens = to_slot(residual)
-    slot_cotangent = to_slot(cotangent)
     head_scalar = head.astype(jnp.int32).reshape(1)
     qkv_w, expand_w, second, vectors, qkv_b, expand_b = call(
         weights_in_body, (1,),
@@ -1083,20 +1107,12 @@
         [shaped((HD, D), BF16), shaped((256, D), BF16)], name="rows_in",
     )(second)
 
-    halves = got[:, PIECE + 32 : PIECE + 34].astype(F32).reshape(2, 2, groups, 2, slots, span)
-    halves = lax.dynamic_index_in_dim(halves, x, 4, keepdims=False)
-    place = (halves[:, :, :, 0] * 256.0 + halves[:, :, :, 1]).transpose(2, 0, 1, 3).reshape(count)
-    half_dims = ROT // 2
-    inverse = ROTARY_BASE ** (-(jnp.arange(half_dims, dtype=F32) * 2.0 / ROT))
-    angles = place[:, None] * inverse
-    cos, sin = jnp.cos(angles), jnp.sin(angles)
-    flat_part = jnp.ones((count, HD - ROT), F32)
-    cos = jnp.concatenate([cos, cos, flat_part] * 2, axis=1)
-    sin = jnp.concatenate([sin, sin, 0.0 * flat_part] * 2, axis=1)
-
     steps = (count // BLOCK,)
-    token_spec = pl.BlockSpec((2, 1, 2, span, width), lambda i, *_: (0, i, 0, 0, 0))
-    token_shape = shaped((2, groups, 2, span, width), BF16)
+    first_spec, second_spec = (
+        pl.BlockSpec((2, 1, 2, None, span, width), lambda i, *_, which=which: (0, i, 0, which, 0, 0))
+        for which in range(2)
+    )
+    token_shape = shaped(gathered.shape, BF16)
 
     def rows_spec(columns):
         return pl.BlockSpec((BLOCK, columns), lambda i, *_: (i, 0))
@@ -1107,10 +1123,10 @@
     narrow = shaped((count, HD), BF16)
     one, two, query, key, value = call(
         mixed_body, steps,
-        [token_spec, whole((8, D)), whole((D, 256)), whole((1, 256)), rows_spec(LANES), rows_spec(LANES)],
+        [first_spec, whole((8, D)), whole((D, 256)), whole((1, 256)), rows_spec(LANES), rows_spec(LANES)],
         [rows_spec(D), rows_spec(D), rows_spec(HD), rows_spec(HD), rows_spec(HD)],
         [shaped((count, D), BF16), shaped((count, D), BF16), narrow, narrow, narrow], name="mixed",
-    )(slot_tokens, vectors, qkv_w, qkv_b, cos, sin)
+    )(gathered, vectors, qkv_w, qkv_b, cos, sin)
     attended, attended_full, log_total = call(
         attend_body, steps,
         [rows_spec(HD), whole((count, HD)), whole((count, HD))],
@@ -1118,15 +1134,14 @@
         [narrow, shaped((HD, count), F32), shaped((1, count), F32)],
         [pltpu.VMEM((count, BLOCK), F32), pltpu.VMEM((HD, count), BF16)], 1, "attend",
     )(length, query, key, value)
-    partial_out, attended_g, hidden_g, shrink_g, dense_g, expand_g, expand_bg, bias_g = call(
+    partials, attended_g, hidden_g, shrink_g, dense_g, expand_g, expand_bg, bias_g = call(
         feed_body, steps,
-        [rows_spec(D), rows_spec(HD), token_spec, whole((D, 256)), whole((1, 256)), whole((256, D)), whole((HD, D))],
-        [token_spec, rows_spec(HD), rows_spec(256), whole((256, D)), whole((HD, D)), whole((D, 256)),
+        [rows_spec(D), rows_spec(HD), second_spec, whole((D, 256)), whole((1, 256)), whole((256, D)), whole((HD, D))],
+        [first_spec, rows_spec(HD), rows_spec(256), whole((256, D)), whole((HD, D)), whole((D, 256)),
          whole((1, 256)), whole((1, D))],
         [token_shape, narrow, shaped((count, 256), BF16), shaped((256, D), F32), shaped((HD, D), F32),
          shaped((D, 256), F32), shaped((1, 256), F32), shaped((1, D), F32)], (), 1, "feed",
-    )(length, two, attended, slot_cotangent, expand_w, expand_b, shrink_w, dense_w)
-    out_rows = to_tokens(partial_out)
+    )(length, two, attended, gathered, expand_w, expand_b, shrink_w, dense_w)
     query_g, key_g, value_g = call(
         attend_back_body, steps,
         [rows_spec(HD), whole((count, HD)), whole((count, HD)), rows_spec(HD), columns_spec(HD), columns_spec(1)],
@@ -1135,14 +1150,16 @@
         [pltpu.VMEM((HD, count), BF16), pltpu.VMEM((count, HD), F32), pltpu.VMEM((count, HD), F32)],
         1, "attend_back",
     )(length, query, key, value, attended_g, attended_full, log_total)
-    partial_in, qkv_g, qkv_bg, vector_g = call(
+    partials, qkv_g, qkv_bg, vector_g = call(
         mixed_back_body, steps,
-        [token_spec, rows_spec(D), rows_spec(HD), rows_spec(HD), rows_spec(HD), rows_spec(256), whole((8, D)),
-         whole((D, 256)), whole((D, 256)), rows_spec(LANES), rows_spec(LANES)],
-        [token_spec, whole((D, 256)), whole((1, 256)), whole((8, D))],
-        [token_shape, shaped((D, 256), F32), shaped((1, 256), F32), shaped((8, D), F32)], name="mixed_back",
-    )(slot_tokens, one, query_g, key_g, value_g, hidden_g, vectors, qkv_w, expand_w, cos, sin)
-    in_rows = to_tokens(partial_in)
+        [pl.BlockSpec(memory_space=pl.ANY), first_spec, rows_spec(D), rows_spec(HD), rows_spec(HD), rows_spec(HD),
+         rows_spec(256), whole((8, D)), whole((D, 256)), whole((D, 256)), rows_spec(LANES), rows_spec(LANES)],
+        [second_spec, whole((D, 256)), whole((1, 256)), whole((8, D))],
+        [token_shape, shaped((D, 256), F32), shaped((1, 256), F32), shaped((8, D), F32)], name="mixed_back", aliases={0: 0},
+    )(partials, gathered, one, query_g, key_g, value_g, hidden_g, vectors, qkv_w, expand_w, cos, sin)
+    rows = lax.psum_scatter(partials.reshape(16, 2, 2, span, width), RING, scatter_dimension=0, tiled=True)[0]
+    rows = paired(at_x(rows, x), across_x(at_x(rows, 1 - x))).astype(F32)
+    out_rows, in_rows = rows[:, 0], rows[:, 1]
 
     second_g = call(
         rows_out_body, (1,), [whole((HD, D)), whole((256, D))], whole((16, 160, LANES)),

time: 418 us -> 394 us (0.943)
  blocking collectives: 71.3 us -> 0 us
  waiting for transfers between devices: 139 us -> 195 us
  local copies, waits for them, and re-layouts: 30.1 us -> 17.6 us
  starting transfers between devices: 31.1 us -> 37.5 us
    all_to_all x0 -> x2, waiting for transfers between devices: none -> 80.5 us  [the longest x1 76.4 us: by_head(): got = lax.all_to_all(jnp.concatenate([sent, sent]), ALL, 0, 0, tiled=True)]
    all_to_all x1 -> x0, blocking collectives: 71.3 us -> none  [by_head(): got = lax.all_to_all(jnp.concatenate([sent, sent]), ALL, 0, 0, tiled=True)]
    reduce_scatter x2 -> x1, waiting for transfers between devices: 41.2 us -> 8.56 us  [by_head(): lax.psum_scatter(partials.reshape(16, 2, 2, span, width), RING, scatter_d...]
    all_to_all x0 -> x2, starting transfers between devices: none -> 12.5 us  [the longest x1 8.66 us: by_head(): got = lax.all_to_all(jnp.concatenate([sent, sent]), ALL, 0, 0, tiled=True)]
    concatenate x2 -> x0, local copies, waits for them, and re-layouts: 11.7 us -> none  [the longest x1 11.6 us: by_head(): jnp.concatenate([jnp.zeros((7 * D,), F32), before, masters, after, jnp.ze...]
    all_to_all x1, waiting for transfers between devices: 59.5 us -> 71.1 us  [by_head(): got_g = lax.all_to_all(sent_g, ALL, 0, 0, tiled=True)]
    ppermute x4 -> x2, starting transfers between devices: 11 us -> 4.55 us  [across_x(): return lax.ppermute(block, 'x', [(0, 1), (1, 0)])]
    ppermute x4 -> x2, waiting for transfers between devices: 8.93 us -> 8.11 us  [across_x(): return lax.ppermute(block, 'x', [(0, 1), (1, 0)])]
  transfers between devices with their start and end apart: 15 -> 13, of which waited for: 9 -> 9; matrix products, arithmetic and copies ran while one was open for 11% -> 8% of each run, Pallas kernels for 14% -> 7%
where the time goes in v2:
time: 394 us; the launch traced here: 392 us
  waiting for transfers between devices  195 us (49%)
  Pallas kernels  106 us (27%)
  starting transfers between devices  37.5 us (10%)
  other arithmetic  21.2 us (5%)
  local copies, waits for them, and re-layouts  17.6 us (4%)
  between operations  14.5 us (4%)
    all_to_all x1, waiting for transfers between devices, by_head(): got = lax.all_to_all(jnp.concatenate([sent, sent]), ALL, 0, 0, tiled=True)  76.4 us
    all_to_all x1, waiting for transfers between devices, by_head(): got_g = lax.all_to_all(sent_g, ALL, 0, 0, tiled=True)  71.1 us
    pallas_call x1, Pallas kernels, by_head(): call(attend_back_body, steps, [rows_spec(HD), whole((count, HD)), whole((...  19.4 us
    pallas_call x1, Pallas kernels, by_head(): call(attend_body, steps, [rows_spec(HD), whole((count, HD)), whole((count...  18.1 us
    all_to_all x1, waiting for transfers between devices, by_head(): second_g = lax.all_to_all(second_g, RING, 0, 0, tiled=True)  17.4 us
    pallas_call x1, Pallas kernels, by_head(): call(feed_body, steps, [rows_spec(D), rows_spec(HD), second_spec, whole((...  16.9 us
    pallas_call x1, Pallas kernels, by_head(): call(mixed_back_body, steps, [pl.BlockSpec(memory_space=pl.ANY), first_sp...  13.4 us
    pallas_call x1, Pallas kernels, by_head(): call(mixed_body, steps, [first_spec, whole((8, D)), whole((D, 256)), whol...  10.7 us
  transfers between devices with their start and end apart: 13, of which 9 were waited for; matrix products, arithmetic and copies ran while one was open for 8% of the time, Pallas kernels for 7%

profile of v2, /device:TPU:0, one launch (start us, length us, event | category | flops | bytes accessed | tf_op | source)
XLA Modules:
  0.0 392.1 jit_solution(17797546892341480764)
XLA Ops:
  8.5 3.0 collective-permute-start
  11.5 6.3 %collective-permute-done = bf16[2,64,1024]{2,1,0:T(8,128)(2,1)S(1)} collective-permute-done((bf16[2,64,1024]{2,1,0:T(8,128)(2,1)S(1)}, bf16[2,64,1024]{2,1,0:T(8,128)(2,1)S(1)}, u32[]{:S(2)}, u32[]{:S(2)}) %collective-permute-start) | collective-permute-done | bytes 262176 | tf_op jit(solution)/shard_map/ppermute | solution.py:1031
  20.1 4.5 %collective-permute-start.1 = (f32[1024]{0:T(1024)S(1)}, f32[1024]{0:T(1024)S(1)}, u32[]{:S(2)}, u32[]{:S(2)}) collective-permute-start(f32[1024]{0:T(1024)S(1)} %slice.63), channel_id=1, source_target_pairs={{0,1},{1,2},{2,3},{3,4},{4,5},{5,6},{6,7},{7,8},{8,9},{9,10},{10,1... | collective-permute-start | bytes 12296 | tf_op jit(solution)/shard_map/ppermute | solution.py:1067
  27.2 7.3 %weights_out.1 = bf16[16,224,128]{2,1,0:T(8,128)(2,1)} custom-call(s32[4]{0:T(128)} %add_add_fusion.scalars, f32[8,128]{1,0:T(8,128)} %bitcast.60, f32[3080,128]{1,0:T(8,128)} %pad_bitcast_fusion.own, f32[32,128]{1,0:T(8,128)} %bitcast.58), custom_call_target="tpu_custom_call" | custom-call | tf_op jit(solution)/shard_map/weights_out/pallas_call | solution.py:1086
  37.4 8.7 %all-to-all-start = ((bf16[32,224,128]{2,1,0:T(8,128)(2,1)}), bf16[32,224,128]{2,1,0:T(8,128)(2,1)S(1)}, u32[]{:S(2)}, u32[]{:S(2)}) async-start(bf16[32,224,128]{2,1,0:T(8,128)(2,1)} %pad_maximum_fusion), calls=%async_computation | async-start | bytes 3670016 | tf_op jit(solution)/shard_map/all_to_all | solution.py:1094
  46.1 76.4 %all-to-all-done.got = bf16[32,224,128]{2,1,0:T(8,128)(2,1)S(1)} async-done(((bf16[32,224,128]{2,1,0:T(8,128)(2,1)}), bf16[32,224,128]{2,1,0:T(8,128)(2,1)S(1)}, u32[]{:S(2)}, u32[]{:S(2)}) %all-to-all-start) | async-done | bytes 1835040 | tf_op jit(solution)/shard_map/all_to_all | solution.py:1094
  123.2 3.9 all-to-all-start.1
  127.1 3.0 weights_in.1
  130.1 4.1 %all-to-all-done.1 = s32[32,1,128]{2,1,0:T(1,128)S(1)} async-done(((s32[32,1,128]{2,1,0:T(1,128)}), s32[32,1,128]{2,1,0:T(1,128)S(1)}, u32[]{:S(2)}, u32[]{:S(2)}) %all-to-all-start.1) | async-done | bytes 16416 | tf_op jit(solution)/shard_map/all_to_all | solution.py:1055
  134.2 4.3 %all-to-all-start.2 = ((bf16[16,160,128]{2,1,0:T(8,128)(2,1)}), bf16[16,160,128]{2,1,0:T(8,128)(2,1)}, u32[]{:S(2)}, u32[]{:S(2)}) async-start(bf16[16,160,128]{2,1,0:T(8,128)(2,1)} %get-tuple-element.71), calls=%async_computation.2 | async-start | bytes 1310720 | tf_op jit(solution)/shard_map/all_to_all | solution.py:1104
  140.8 3.7 multiply_sine_fusion
  150.5 6.5 %all-to-all-done.2.got = bf16[16,160,128]{2,1,0:T(8,128)(2,1)} async-done(((bf16[16,160,128]{2,1,0:T(8,128)(2,1)}), bf16[16,160,128]{2,1,0:T(8,128)(2,1)}, u32[]{:S(2)}, u32[]{:S(2)}) %all-to-all-start.2) | async-done | bytes 655392 | tf_op jit(solution)/shard_map/all_to_all | solution.py:1104
  159.2 10.7 %mixed.1 = (bf16[2048,1024]{1,0:T(8,128)(2,1)}, bf16[2048,1024]{1,0:T(8,128)(2,1)}, bf16[2048,64]{1,0:T(8,128)(2,1)}, bf16[2048,64]{1,0:T(8,128)(2,1)}, bf16[2048,64]{1,0:T(8,128)(2,1)}) custom-call(bf16[2,8,2,2,64,1024]{5,4,3,2,1,0:T(8,128)(2,1)} %bitcast.47, f32[8,1024]{1,0:T(8,128)} %get-tuple-element.61.vectors, ...), custom_call_target="tpu_custom_call" | custom-call | tf_op jit(solution)/shard_map/mixed/pallas_call | solution.py:1124
  169.8 18.1 %attend.1 = (bf16[2048,64]{1,0:T(8,128)(2,1)}, f32[64,2048]{1,0:T(8,128)}, f32[1,2048]{1,0:T(1,128)}) custom-call(s32[1]{0:T(128)} %dynamic_slice.22.lengths, bf16[2048,64]{1,0:T(8,128)(2,1)} %get-tuple-element.65.query, bf16[2048,64]{1,0:T(8,128)(2,1)} %get-tuple-element.66.key, bf16[2048,64]{1,0:T(8,128)(2,1)} %get-tuple-element.67.value), custom_call_target="tpu_custom_call" | custom-call | tf_op jit(solution)/shard_map/attend/pallas_call | solution.py:1130
  188.0 16.9 %feed.1 = (bf16[2,8,2,2,64,1024]{5,4,3,2,1,0:T(8,128)(2,1)}, bf16[2048,64]{1,0:T(8,128)(2,1)}, bf16[2048,256]{1,0:T(8,128)(2,1)}, f32[256,1024]{1,0:T(8,128)}, f...) custom-call(s32[1]{0:T(128)} %dynamic_slice.22.lengths, ...), custom_call_target="tpu_custom_call" | custom-call | tf_op jit(solution)/shard_map/feed/pallas_call | solution.py:1137
  204.9 19.4 %attend_back.1 = (bf16[2048,64]{1,0:T(8,128)(2,1)}, bf16[2048,64]{1,0:T(8,128)(2,1)}, bf16[2048,64]{1,0:T(8,128)(2,1)}) custom-call(s32[1]{0:T(128)} %dynamic_slice.22.lengths, bf16[2048,64]{1,0:T(8,128)(2,1)} %get-tuple-element.65.query, bf16[2048,64]{1,0:T(8,128)(2,1)} %get-tuple-element.66.key, bf16[2048,64]{1,0:T(8,128)(2,1)} %get-tuple-element.67.value, ...), custom_call_target="tpu_custom_call" | custom-call | tf_op jit(solution)/shard_map/attend_back/pallas_call | solution.py:1145
  224.2 13.4 %mixed_back.1 = (bf16[2,8,2,2,64,1024]{5,4,3,2,1,0:T(8,128)(2,1)}, f32[1024,256]{1,0:T(8,128)}, f32[1,256]{1,0:T(1,128)}, f32[8,1024]{1,0:T(8,128)}) custom-call(bf16[2,8,2,2,64,1024]{5,4,3,2,1,0:T(8,128)(2,1)} %get-tuple-element.74.partials, bf16[2,8,2,2,64,1024]{5,4,3,2,1,0:T(8,128)(2,1)} %bitcast.49, ...), custom_call_target="tpu_custom_call", output_to_operand_aliasing={{0}: (0, {})} | custom-call | tf_op jit(solution)/shard_map/mixed_back/pallas_call | solution.py:1153
  240.0 3.8 all-to-all-start.3
  244.7 17.4 %all-to-all-done.3.second = bf16[16,160,128]{2,1,0:T(8,128)(2,1)S(1)} async-done(((bf16[16,160,128]{2,1,0:T(8,128)(2,1)}), bf16[16,160,128]{2,1,0:T(8,128)(2,1)S(1)}, u32[]{:S(2)}, u32[]{:S(2)}) %all-to-all-start.3) | async-done | bytes 655392 | tf_op jit(solution)/shard_map/all_to_all | solution.py:1168
  263.0 4.8 %grads_out.1 = bf16[32,224,128]{2,1,0:T(8,128)(2,1)} custom-call(s32[1]{0:T(128)} %bitcast.6.scalars, bf16[16,160,128]{2,1,0:T(8,128)(2,1)} %copy-done.5, f32[1024,256]{1,0:T(8,128)} %get-tuple-element.86.qkv_g, f32[1024,256]{1,0:T(8,128)} %get-tuple-element.87.expand_g, f32[8,1024]{1,0:T(8,128)} %maximum_maximum_fusion.vector_g, ...), custom_call_target="tpu_custom_call" | custom-call | tf_op jit(solution)/shard_map/grads_out/pallas_call | solution.py:1171
  272.6 71.1 %all-to-all-done.4.got = bf16[32,224,128]{2,1,0:T(8,128)(2,1)S(1)} async-done(((bf16[32,224,128]{2,1,0:T(8,128)(2,1)}), bf16[32,224,128]{2,1,0:T(8,128)(2,1)S(1)}, u32[]{:S(2)}, u32[]{:S(2)}) %all-to-all-start.4) | async-done | bytes 1835040 | tf_op jit(solution)/shard_map/all_to_all | solution.py:1178
  344.9 8.1 %grads_in.1 = f32[3120,128]{1,0:T(8,128)} custom-call(s32[4]{0:T(128)} %add_add_fusion.1.scalars, bf16[32,224,128]{2,1,0:T(8,128)(2,1)} %copy-done), custom_call_target="tpu_custom_call" | custom-call | tf_op jit(solution)/shard_map/grads_in/pallas_call | solution.py:1181
  366.4 8.6 %reduce-scatter.2.cloned.1.call-done = bf16[1,2,2,64,1024]{4,3,2,1,0:T(8,128)(2,1)} async-done(((bf16[16,2,2,64,1024]{4,3,2,1,0:T(8,128)(2,1)}), bf16[1,2,2,64,1024]{4,3,2,1,0:T(8,128)(2,1)}) %reduce-scatter.2.cloned.1.call-update) | async-done | bytes 524304 | tf_op jit(solution)/shard_map/reduce_scatter | solution.py:1160
  377.6 4.4 %add_multiply_fusion = (f32[393632]{0:T(1024)}, f32[393632]{0:T(1024)}, f32[393632]{0:T(1024)}) fusion(f32[393632]{0:T(1024)S(1)} %copy-done.6, f32[393632]{0:T(1024)S(1)} %copy-done.4, f32[393632]{0:T(1024)} %fusion.19, f32[393632]{0:T(1024)} %param.16), kind=kLoop, calls=%fused_computation.1 | loop fusion | flops 3149056 | bytes 11021696 | tf_op jit(solution)/shard_map/add | solution.py:1206
  (90 shorter events, 49.4 us)
Async XLA Ops:
  7.2 11.6 %copy-start.3 = (f32[393632]{0:T(1024)S(1)}, f32[393632]{0:T(1024)}, u32[]{:S(2)}) copy-start(f32[393632]{0:T(1024)} %param.15) | copy-start | bytes 4723588
  7.2 152.0 %all-gather.2.cloned.1.call-start = ((), (), s32[]{:S(2)}) async-start(), calls=%async_computation.6 | async-start | bytes 8912896 | tf_op jit(solution)/shard_map/all_gather | solution.py:1052
  8.5 9.3 %collective-permute-start = (bf16[2,64,1024]{2,1,0:T(8,128)(2,1)S(1)}, bf16[2,64,1024]{2,1,0:T(8,128)(2,1)S(1)}, u32[]{:S(2)}, u32[]{:S(2)}) collective-permute-start(bf16[2,64,1024]{2,1,0:T(8,128)(2,1)S(1)} %get-tuple-element.100), channel_id=1, source_target_pairs={{0,16},{16,0},{1,17},{17,1},{2,18},{18,2},{3,19},{19,3},{4,20},{20... | collective-permute-start | bytes 786440 | tf_op jit(solution)/shard_map/ppermute | solution.py:1031
  18.7 7.8 %collective-permute-start.2 = (f32[4096]{0:T(1024)S(1)}, f32[4096]{0:T(1024)S(1)}, u32[]{:S(2)}, u32[]{:S(2)}) collective-permute-start(f32[4096]{0:T(1024)S(1)} %slice.64), channel_id=1, source_target_pairs={{1,0},{2,1},{3,2},{4,3},{5,4},{6,5},{7,6},{8,7},{9,8},{10,9},{11,1... | collective-permute-start | bytes 49160 | tf_op jit(solution)/shard_map/ppermute | solution.py:1068
  20.1 6.5 %collective-permute-start.1 = (f32[1024]{0:T(1024)S(1)}, f32[1024]{0:T(1024)S(1)}, u32[]{:S(2)}, u32[]{:S(2)}) collective-permute-start(f32[1024]{0:T(1024)S(1)} %slice.63), channel_id=1, source_target_pairs={{0,1},{1,2},{2,3},{3,4},{4,5},{5,6},{6,7},{7,8},{8,9},{9,10},{10,1... | collective-permute-start | bytes 12296 | tf_op jit(solution)/shard_map/ppermute | solution.py:1067
  37.4 8.7 %copy-start.12 = (s32[2,64]{1,0:T(2,128)S(1)}, s32[2,64]{1,0:T(2,128)}, u32[]{:S(2)}) copy-start(s32[2,64]{1,0:T(2,128)} %param.14) | copy-start | bytes 1540
  37.4 85.2 %all-to-all-start = ((bf16[32,224,128]{2,1,0:T(8,128)(2,1)}), bf16[32,224,128]{2,1,0:T(8,128)(2,1)S(1)}, u32[]{:S(2)}, u32[]{:S(2)}) async-start(bf16[32,224,128]{2,1,0:T(8,128)(2,1)} %pad_maximum_fusion), calls=%async_computation | async-start | bytes 3670016 | tf_op jit(solution)/shard_map/all_to_all | solution.py:1094
  122.6 4.6 %copy-start.1 = (bf16[32,224,128]{2,1,0:T(8,128)(2,1)}, bf16[32,224,128]{2,1,0:T(8,128)(2,1)S(1)}, u32[]{:S(2)}) copy-start(bf16[32,224,128]{2,1,0:T(8,128)(2,1)S(1)} %all-to-all-done.got) | copy-start | bytes 5505028
  123.2 10.9 %all-to-all-start.1 = ((s32[32,1,128]{2,1,0:T(1,128)}), s32[32,1,128]{2,1,0:T(1,128)S(1)}, u32[]{:S(2)}, u32[]{:S(2)}) async-start(s32[32,1,128]{2,1,0:T(1,128)} %broadcast_in_dim.40), calls=%async_computation.1 | async-start | bytes 32768 | tf_op jit(solution)/shard_map/all_to_all | solution.py:1055
  127.1 11.6 %copy-start.13 = (s32[2]{0:T(128)S(1)}, s32[2]{0:T(128)}, u32[]{:S(2)}) copy-start(s32[2]{0:T(128)} %param.13) | copy-start | bytes 28
  134.2 22.8 %all-to-all-start.2 = ((bf16[16,160,128]{2,1,0:T(8,128)(2,1)}), bf16[16,160,128]{2,1,0:T(8,128)(2,1)}, u32[]{:S(2)}, u32[]{:S(2)}) async-start(bf16[16,160,128]{2,1,0:T(8,128)(2,1)} %get-tuple-element.71), calls=%async_computation.2 | async-start | bytes 1310720 | tf_op jit(solution)/shard_map/all_to_all | solution.py:1104
  138.5 236.5 %reduce-scatter.2.cloned.1.call-start = ((), (), s32[]{:S(2)}) async-start(), calls=%async_computation.7 | async-start | bytes 8912896 | tf_op jit(solution)/shard_map/reduce_scatter | solution.py:1160
  237.6 6.3 %copy-start.9 = (f32[8,1024]{1,0:T(8,128)S(1)}, f32[8,1024]{1,0:T(8,128)}, u32[]{:S(2)}) copy-start(f32[8,1024]{1,0:T(8,128)} %get-tuple-element.88) | copy-start | bytes 98308
  237.6 6.3 %copy-start.11 = (f32[1,1024]{1,0:T(1,128)S(1)}, f32[1,1024]{1,0:T(1,128)}, u32[]{:S(2)}) copy-start(f32[1,1024]{1,0:T(1,128)} %get-tuple-element.89) | copy-start | bytes 12292
  240.0 22.1 %all-to-all-start.3 = ((bf16[16,160,128]{2,1,0:T(8,128)(2,1)}), bf16[16,160,128]{2,1,0:T(8,128)(2,1)S(1)}, u32[]{:S(2)}, u32[]{:S(2)}) async-start(bf16[16,160,128]{2,1,0:T(8,128)(2,1)} %rows_out.1), calls=%async_computation.4 | async-start | bytes 1310720 | tf_op jit(solution)/shard_map/all_to_all | solution.py:1168
  267.8 3.5 copy-start.2
  267.8 75.8 %all-to-all-start.4 = ((bf16[32,224,128]{2,1,0:T(8,128)(2,1)}), bf16[32,224,128]{2,1,0:T(8,128)(2,1)S(1)}, u32[]{:S(2)}, u32[]{:S(2)}) async-start(bf16[32,224,128]{2,1,0:T(8,128)(2,1)} %grads_out.1), calls=%async_computation.5 | async-start | bytes 3670016 | tf_op jit(solution)/shard_map/all_to_all | solution.py:1178
  343.6 1.3 copy-start
  353.8 6.9 %collective-permute-start.4 = (f32[4096]{0:T(1024)S(1)}, f32[4096]{0:T(1024)S(1)}, u32[]{:S(2)}, u32[]{:S(2)}) collective-permute-start(f32[4096]{0:T(1024)S(1)} %slice.80), channel_id=1, source_target_pairs={{0,1},{1,2},{2,3},{3,4},{4,5},{5,6},{6,7},{7,8},{8,9},{9,10},{10,1... | collective-permute-start | bytes 49160 | tf_op jit(solution)/shard_map/ppermute | solution.py:1185
  356.6 21.0 %copy-start.4 = (f32[393632]{0:T(1024)S(1)}, f32[393632]{0:T(1024)}, u32[]{:S(2)}) copy-start(f32[393632]{0:T(1024)} %param.15) | copy-start | bytes 4723588
  356.6 21.0 %copy-start.6 = (f32[393632]{0:T(1024)S(1)}, f32[393632]{0:T(1024)}, u32[]{:S(2)}) copy-start(f32[393632]{0:T(1024)} %param.17) | copy-start | bytes 4723588
  359.4 5.5 %collective-permute-start.5 = (f32[1024]{0:T(1024)S(1)}, f32[1024]{0:T(1024)S(1)}, u32[]{:S(2)}, u32[]{:S(2)}) collective-permute-start(f32[1024]{0:T(1024)S(1)} %slice_bitcast_fusion.2), channel_id=1, source_target_pairs={{1,0},{2,1},{3,2},{4,3},{5,4},{6,5},{7,6},{8,7},{9,8},{10,9},{11,1... | collective-permute-start | bytes 12296 | tf_op jit(solution)/shard_map/ppermute | solution.py:1186
  376.0 7.7 %collective-permute-start.3 = (bf16[2,64,1024]{2,1,0:T(8,128)(2,1)S(1)}, bf16[2,64,1024]{2,1,0:T(8,128)(2,1)S(1)}, u32[]{:S(2)}, u32[]{:S(2)}) collective-permute-start(bf16[2,64,1024]{2,1,0:T(8,128)(2,1)S(1)} %get-tuple-element.98), channel_id=1, source_target_pairs={{0,16},{16,0},{1,17},{17,1},{2,18},{18,2},{3,19},{19,3},{4,20},{20... | collective-permute-start | bytes 786440 | tf_op jit(solution)/shard_map/ppermute | solution.py:1031
  382.0 2.2 copy-start.7
  (3 other events, 2.0 us)
Sparse Core Ops, SparseCore 0:
  18.8 105.7 all-gather.1
  237.8 137.1 reduce-scatter.1

commit v3 on v2

--- a/solution.py
+++ b/solution.py
@@ -438,7 +438,7 @@
 BF16 = jnp.bfloat16
 
 
-def call(body, grid, in_specs, out_specs, out_shape, scratch=(), prefetch=0, name=None, aliases=None):
+def call(body, grid, in_specs, out_specs, out_shape, scratch=(), prefetch=0, name=None):
     return pl.pallas_call(
         body,
         grid_spec=pltpu.PrefetchScalarGridSpec(
@@ -450,7 +450,6 @@
         ),
         out_shape=out_shape,
         name=name,
-        input_output_aliases=aliases or {},
         compiler_params=pltpu.CompilerParams(vmem_limit_bytes=56 << 20),
     )
 
@@ -824,10 +823,18 @@
     return jnp.concatenate([ref[0, 0, 0], ref[1, 0, 0], ref[0, 0, 1], ref[1, 0, 1]], axis=0)
 
 
-def put_rows(ref, rows):
+def put_rows(kept, sent, rows, core):
     step = rows.shape[0] // 4
-    for i, (core, x) in enumerate(((0, 0), (1, 0), (0, 1), (1, 1))):
-        ref[core, 0, x] = rows[step * i : step * i + step].astype(ref.dtype)
+    for x in range(2):
+        first, second = (rows[step * i : step * i + step].astype(kept.dtype) for i in (2 * x, 2 * x + 1))
+        kept[0, x] = jnp.where(core == 0, first, second)
+        sent[0, x] = jnp.where(core == 0, second, first)
+
+
+def relative_place(i, here):
+    y = (i & 1) ^ here[2]
+    z = (i >> 1) ^ here[3]
+    return y * 4 + (z & 1) * 2 + (z >> 1)
 
 
 def normalized(values):
@@ -964,8 +971,8 @@
 
 
 def feed_body(
-    lengths, two, attended, cotangent, expand_w, expand_b, shrink_w, dense_w,
-    partial_out, attended_g, hidden_g, shrink_g, dense_g, expand_g, expand_bg, bias_g,
+    here, two, attended, cotangent, expand_w, expand_b, shrink_w, dense_w,
+    kept, sent, attended_g, hidden_g, shrink_g, dense_g, expand_g, expand_bg, bias_g,
 ):
     at = pl.program_id(0)
 
@@ -979,9 +986,9 @@
     error = lax.erf(hidden * math.sqrt(0.5))
     cumulative = 0.5 * (1.0 + error)
     active = (hidden * cumulative).astype(BF16)
-    put_rows(partial_out, mm(mixed, dense_w[...]) + mm(active, shrink_w[...]))
+    put_rows(kept, sent, mm(mixed, dense_w[...]) + mm(active, shrink_w[...]), here[1])
     token = at * BLOCK + lax.broadcasted_iota(jnp.int32, (BLOCK, D), 0)
-    seed = jnp.where(token < lengths[0], token_rows(cotangent).astype(F32), 0.0)
+    seed = jnp.where(token < here[0], token_rows(cotangent).astype(F32), 0.0)
     bias_g[...] += jnp.sum(seed, axis=0, keepdims=True)
     seed = seed.astype(BF16)
     attended_g[...] = mm(seed, dense_w[...], ((1,), (1,))).astype(BF16)
@@ -995,8 +1002,8 @@
 
 
 def mixed_back_body(
-    partials, tokens, one, query_g, key_g, value_g, hidden_g, vectors, qkv_w, expand_w, cos, sin,
-    partial_out, qkv_g, qkv_bg, vector_g,
+    here, tokens, one, query_g, key_g, value_g, hidden_g, vectors, qkv_w, expand_w, cos, sin,
+    kept, sent, qkv_g, qkv_bg, vector_g,
 ):
     at = pl.program_id(0)
 
@@ -1019,7 +1026,7 @@
     vector_g[1:2] += jnp.sum(one_g, axis=0, keepdims=True)
     vector_g[2:3] += jnp.sum(two_g * unit, axis=0, keepdims=True)
     vector_g[3:4] += jnp.sum(two_g, axis=0, keepdims=True)
-    put_rows(partial_out, one_g * vectors[0:1] + two_g * vectors[2:3])
+    put_rows(kept, sent, one_g * vectors[0:1] + two_g * vectors[2:3], here[1])
 
 
 def split_mesh(mesh):
@@ -1049,10 +1056,15 @@
 
     rows = jnp.stack([residual, cotangent], axis=1)
     rows = paired(at_x(rows, x), across_x(at_x(rows, 1 - x)))
-    gathered = lax.all_gather(rows, RING, axis=0).reshape(2, groups, 2, 2, span, width)
+    tokens_shape = (2, groups, 2, span, width)
+    slot_tokens = lax.all_gather(rows[:, 0], RING, axis=0).reshape(tokens_shape)
+    later, slot_tokens = lax.optimization_barrier((rows[:, 1], slot_tokens))
+    slot_cotangent = lax.all_gather(later, RING, axis=0).reshape(tokens_shape)
 
     place = jnp.broadcast_to(positions.reshape(1, slots * span), (OWNERS, slots * span))
-    place = lax.all_to_all(place, ALL, 0, 0, tiled=True).reshape(2, 2, groups, slots, span)
+    place = lax.all_to_all(place, ALL, 0, 0, tiled=True)
+    known = place
+    place = place.reshape(2, 2, groups, slots, span)
     place = lax.dynamic_index_in_dim(place, x, 3, keepdims=False).transpose(2, 0, 1, 3).reshape(count)
     half_dims = ROT // 2
     inverse = ROTARY_BASE ** (-(jnp.arange(half_dims, dtype=F32) * 2.0 / ROT))
@@ -1091,7 +1103,8 @@
         [pltpu.VMEM((3280, LANES), F32), pltpu.VMEM((SHIFT_ROWS, LANES), F32), pltpu.VMEM((48, LANES), F32)],
         1, "weights_out",
     )(scalars, before, own, after)
-    got = lax.all_to_all(jnp.concatenate([sent, sent]), ALL, 0, 0, tiled=True)
+    sent, _ = lax.optimization_barrier((jnp.concatenate([sent, sent]), known))
+    got = lax.all_to_all(sent, ALL, 0, 0, tiled=True)
     head_scalar = head.astype(jnp.int32).reshape(1)
     qkv_w, expand_w, second, vectors, qkv_b, expand_b = call(
         weights_in_body, (1,),
@@ -1102,17 +1115,29 @@
         [pltpu.VMEM((24, LANES), F32), pltpu.VMEM((32, LANES), F32)], 1, "weights_in",
     )(head_scalar, got)
     second = lax.all_to_all(second, RING, 0, 0, tiled=True)
-    dense_w, shrink_w = call(
-        rows_in_body, (1,), [whole(second.shape)], [whole((HD, D)), whole((256, D))],
-        [shaped((HD, D), BF16), shaped((256, D), BF16)], name="rows_in",
-    )(second)
-
     steps = (count // BLOCK,)
-    first_spec, second_spec = (
-        pl.BlockSpec((2, 1, 2, None, span, width), lambda i, *_, which=which: (0, i, 0, which, 0, 0))
-        for which in range(2)
-    )
-    token_shape = shaped(gathered.shape, BF16)
+    token_spec = pl.BlockSpec((2, 1, 2, span, width), lambda i, *_: (0, i, 0, 0, 0))
+    part_spec = pl.BlockSpec((1, 2, span, width), lambda i, here: (relative_place(i, here), 0, 0, 0))
+    part_shape = shaped((groups, 2, span, width), BF16)
+    y, z, core = lax.axis_index("y"), lax.axis_index("z"), lax.axis_index("core")
+    here = jnp.stack([length[0], core, y, z]).astype(jnp.int32)
+
+    def summed(kept, sent):
+        groups_left = kept.shape[0]
+        for axis, route in (
+            ("core", [(0, 1), (1, 0)]),
+            ("y", [(0, 1), (1, 0)]),
+            ("z", [(0, 1), (1, 0), (2, 3), (3, 2)]),
+            ("z", [(0, 2), (2, 0), (1, 3), (3, 1)]),
+        ):
+            came = lax.ppermute(sent, axis, route)
+            if groups_left == 1:
+                return kept[0].astype(F32) + came[0].astype(F32)
+            groups_left //= 2
+            kept, sent = (
+                (kept[half].astype(F32) + came[half].astype(F32)).astype(BF16)
+                for half in (slice(0, groups_left), slice(groups_left, None))
+            )
 
     def rows_spec(columns):
         return pl.BlockSpec((BLOCK, columns), lambda i, *_: (i, 0))
@@ -1123,10 +1148,10 @@
     narrow = shaped((count, HD), BF16)
     one, two, query, key, value = call(
         mixed_body, steps,
-        [first_spec, whole((8, D)), whole((D, 256)), whole((1, 256)), rows_spec(LANES), rows_spec(LANES)],
+        [token_spec, whole((8, D)), whole((D, 256)), whole((1, 256)), rows_spec(LANES), rows_spec(LANES)],
         [rows_spec(D), rows_spec(D), rows_spec(HD), rows_spec(HD), rows_spec(HD)],
         [shaped((count, D), BF16), shaped((count, D), BF16), narrow, narrow, narrow], name="mixed",
-    )(gathered, vectors, qkv_w, qkv_b, cos, sin)
+    )(slot_tokens, vectors, qkv_w, qkv_b, cos, sin)
     attended, attended_full, log_total = call(
         attend_body, steps,
         [rows_spec(HD), whole((count, HD)), whole((count, HD))],
@@ -1134,14 +1159,27 @@
         [narrow, shaped((HD, count), F32), shaped((1, count), F32)],
         [pltpu.VMEM((count, BLOCK), F32), pltpu.VMEM((HD, count), BF16)], 1, "attend",
     )(length, query, key, value)
-    partials, attended_g, hidden_g, shrink_g, dense_g, expand_g, expand_bg, bias_g = call(
+    second, attended = lax.optimization_barrier((second, attended))
+    dense_w, shrink_w = call(
+        rows_in_body, (1,), [whole(second.shape)], [whole((HD, D)), whole((256, D))],
+        [shaped((HD, D), BF16), shaped((256, D), BF16)], name="rows_in",
+    )(second)
+
+    kept, sent, attended_g, hidden_g, shrink_g, dense_g, expand_g, expand_bg, bias_g = call(
         feed_body, steps,
-        [rows_spec(D), rows_spec(HD), second_spec, whole((D, 256)), whole((1, 256)), whole((256, D)), whole((HD, D))],
-        [first_spec, rows_spec(HD), rows_spec(256), whole((256, D)), whole((HD, D)), whole((D, 256)),
+        [rows_spec(D), rows_spec(HD), token_spec, whole((D, 256)), whole((1, 256)), whole((256, D)), whole((HD, D))],
+        [part_spec, part_spec, rows_spec(HD), rows_spec(256), whole((256, D)), whole((HD, D)), whole((D, 256)),
          whole((1, 256)), whole((1, D))],
-        [token_shape, narrow, shaped((count, 256), BF16), shaped((256, D), F32), shaped((HD, D), F32),
+        [part_shape, part_shape, narrow, shaped((count, 256), BF16), shaped((256, D), F32), shaped((HD, D), F32),
          shaped((D, 256), F32), shaped((1, 256), F32), shaped((1, D), F32)], (), 1, "feed",
-    )(length, two, attended, gathered, expand_w, expand_b, shrink_w, dense_w)
+    )(here, two, attended, slot_cotangent, expand_w, expand_b, shrink_w, dense_w)
+    second_g = call(
+        rows_out_body, (1,), [whole((HD, D)), whole((256, D))], whole((16, 160, LANES)),
+        shaped((16, 160, LANES), BF16), name="rows_out",
+    )(dense_g, shrink_g)
+    attended_g, second_g = lax.optimization_barrier((attended_g, second_g))
+    second_g = lax.all_to_all(second_g, RING, 0, 0, tiled=True)
+    out_rows = summed(kept, sent)
     query_g, key_g, value_g = call(
         attend_back_body, steps,
         [rows_spec(HD), whole((count, HD)), whole((count, HD)), rows_spec(HD), columns_spec(HD), columns_spec(1)],
@@ -1150,22 +1188,18 @@
         [pltpu.VMEM((HD, count), BF16), pltpu.VMEM((count, HD), F32), pltpu.VMEM((count, HD), F32)],
         1, "attend_back",
     )(length, query, key, value, attended_g, attended_full, log_total)
-    partials, qkv_g, qkv_bg, vector_g = call(
+    kept, sent, qkv_g, qkv_bg, vector_g = call(
         mixed_back_body, steps,
-        [pl.BlockSpec(memory_space=pl.ANY), first_spec, rows_spec(D), rows_spec(HD), rows_spec(HD), rows_spec(HD),
+        [token_spec, rows_spec(D), rows_spec(HD), rows_spec(HD), rows_spec(HD),
          rows_spec(256), whole((8, D)), whole((D, 256)), whole((D, 256)), rows_spec(LANES), rows_spec(LANES)],
-        [second_spec, whole((D, 256)), whole((1, 256)), whole((8, D))],
-        [token_shape, shaped((D, 256), F32), shaped((1, 256), F32), shaped((8, D), F32)], name="mixed_back", aliases={0: 0},
-    )(partials, gathered, one, query_g, key_g, value_g, hidden_g, vectors, qkv_w, expand_w, cos, sin)
-    rows = lax.psum_scatter(partials.reshape(16, 2, 2, span, width), RING, scatter_dimension=0, tiled=True)[0]
+        [part_spec, part_spec, whole((D, 256)), whole((1, 256)), whole((8, D))],
+        [part_shape, part_shape, shaped((D, 256), F32), shaped((1, 256), F32), shaped((8, D), F32)], (), 1, "mixed_back",
+    )(here, slot_tokens, one, query_g, key_g, value_g, hidden_g, vectors, qkv_w, expand_w, cos, sin)
+    in_rows = summed(kept, sent)
+    rows = jnp.stack([out_rows, in_rows], axis=1).astype(BF16)
     rows = paired(at_x(rows, x), across_x(at_x(rows, 1 - x))).astype(F32)
     out_rows, in_rows = rows[:, 0], rows[:, 1]
 
-    second_g = call(
-        rows_out_body, (1,), [whole((HD, D)), whole((256, D))], whole((16, 160, LANES)),
-        shaped((16, 160, LANES), BF16), name="rows_out",
-    )(dense_g, shrink_g)
-    second_g = lax.all_to_all(second_g, RING, 0, 0, tiled=True)
     bias_g = jnp.where(head == 0, bias_g, 0.0)
     vector_g = jnp.concatenate([vector_g[:4], bias_g, jnp.zeros((3, D), F32)])
     sent_g = call(

time: 394 us -> 430 us (1.091)
  waiting for transfers between devices: 195 us -> 213 us
  other arithmetic: 21.2 us -> 32.1 us
  starting transfers between devices: 37.5 us -> 42.6 us
    ppermute x0 -> x8, waiting for transfers between devices: none -> 72.9 us  [summed(): came = lax.ppermute(sent, axis, route)]
    all_to_all x1, waiting for transfers between devices: 71.1 us -> 0.01 us  [by_head(): got_g = lax.all_to_all(sent_g, ALL, 0, 0, tiled=True)]
    all_gather x1 -> x2, waiting for transfers between devices: 0.01 us -> 52 us  [the longest x1 52 us: by_head(): slot_tokens = lax.all_gather(rows[:, 0], RING, axis=0).reshape(tokens_shape)]
    all_to_all x2, waiting for transfers between devices: 80.5 us -> 65.3 us  [the longest x1 61.2 us: by_head(): got = lax.all_to_all(sent, ALL, 0, 0, tiled=True)]
    convert_element_type x0 -> x6, other arithmetic: none -> 11.8 us  [summed(): (kept[half].astype(F32) + came[half].astype(F32)).astype(BF16)]
    all_to_all x1, waiting for transfers between devices: 17.4 us -> 6.21 us  [by_head(): second_g = lax.all_to_all(second_g, RING, 0, 0, tiled=True)]
    reduce_scatter x1 -> x0, waiting for transfers between devices: 8.56 us -> none  [by_head(): lax.psum_scatter(partials.reshape(16, 2, 2, span, width), RING, scatter_d...]
    ppermute x0 -> x8, starting transfers between devices: none -> 6.84 us  [summed(): came = lax.ppermute(sent, axis, route)]
  transfers between devices with their start and end apart: 13 -> 21, of which waited for: 9 -> 11; matrix products, arithmetic and copies ran while one was open for 8% -> 9% of each run, Pallas kernels for 7% -> 11%
where the time goes in v3:
time: 430 us; the launch traced here: 426 us
  waiting for transfers between devices  213 us (50%)
  Pallas kernels  106 us (25%)
  starting transfers between devices  42.6 us (10%)
  other arithmetic  32.1 us (7%)
  local copies, waits for them, and re-layouts  17.6 us (4%)
  between operations  14.6 us (3%)
    ppermute x8, waiting for transfers between devices, summed(): came = lax.ppermute(sent, axis, route)  72.9 us
    all_to_all x1, waiting for transfers between devices, by_head(): got = lax.all_to_all(sent, ALL, 0, 0, tiled=True)  61.2 us
    all_gather x1, waiting for transfers between devices, by_head(): slot_tokens = lax.all_gather(rows[:, 0], RING, axis=0).reshape(tokens_shape)  52 us
    pallas_call x1, Pallas kernels, by_head(): call(attend_back_body, steps, [rows_spec(HD), whole((count, HD)), whole((...  19.4 us
    pallas_call x1, Pallas kernels, by_head(): call(attend_body, steps, [rows_spec(HD), whole((count, HD)), whole((count...  18.2 us
    pallas_call x1, Pallas kernels, by_head(): call(feed_body, steps, [rows_spec(D), rows_spec(HD), token_spec, whole((D...  16.4 us
    pallas_call x1, Pallas kernels, by_head(): call(mixed_back_body, steps, [token_spec, rows_spec(D), rows_spec(HD), ro...  13.9 us
    ppermute x2, waiting for transfers between devices, across_x(): return lax.ppermute(block, 'x', [(0, 1), (1, 0)])  13.1 us
  transfers between devices with their start and end apart: 21, of which 11 were waited for; matrix products, arithmetic and copies ran while one was open for 9% of the time, Pallas kernels for 11%

profile of v3, /device:TPU:0, one launch (start us, length us, event | category | flops | bytes accessed | tf_op | source)
XLA Modules:
  0.0 426.3 jit_solution(8586389826791769455)
XLA Ops:
  11.5 6.3 %collective-permute-done = bf16[2,64,1024]{2,1,0:T(8,128)(2,1)S(1)} collective-permute-done((bf16[2,64,1024]{2,1,0:T(8,128)(2,1)S(1)}, bf16[2,64,1024]{2,1,0:T(8,128)(2,1)S(1)}, u32[]{:S(2)}, u32[]{:S(2)}) %collective-permute-start) | collective-permute-done | bytes 262176 | tf_op jit(solution)/shard_map/ppermute | solution.py:1038
  18.8 52.0 %all-gather.5.cloned.1.call-done = bf16[32,1,64,1024]{3,2,1,0:T(8,128)(2,1)} async-done(((bf16[2,1,64,1024]{3,2,1,0:T(8,128)(2,1)}), bf16[32,1,64,1024]{3,2,1,0:T(8,128)(2,1)}) %all-gather.5.cloned.1.call-update) | async-done | bytes 4194320 | tf_op jit(solution)/shard_map/all_gather | solution.py:1060
  72.2 4.5 %collective-permute-start.1 = (f32[1024]{0:T(1024)S(1)}, f32[1024]{0:T(1024)S(1)}, u32[]{:S(2)}, u32[]{:S(2)}) collective-permute-start(f32[1024]{0:T(1024)S(1)} %slice.143), channel_id=1, source_target_pairs={{0,1},{1,2},{2,3},{3,4},{4,5},{5,6},{6,7},{7,8},{8,9},{9,10},{10,1... | collective-permute-start | bytes 12296 | tf_op jit(solution)/shard_map/ppermute | solution.py:1079
  79.3 7.3 %weights_out.1 = bf16[16,224,128]{2,1,0:T(8,128)(2,1)} custom-call(s32[4]{0:T(128)} %add_add_fusion.scalars, f32[8,128]{1,0:T(8,128)} %bitcast.66, f32[3080,128]{1,0:T(8,128)} %pad_bitcast_fusion.own, f32[32,128]{1,0:T(8,128)} %bitcast.64), custom_call_target="tpu_custom_call" | custom-call | tf_op jit(solution)/shard_map/weights_out/pallas_call | solution.py:1098
  89.5 7.0 %all-to-all-start = ((bf16[32,224,128]{2,1,0:T(8,128)(2,1)}), bf16[32,224,128]{2,1,0:T(8,128)(2,1)S(1)}, u32[]{:S(2)}, u32[]{:S(2)}) async-start(bf16[32,224,128]{2,1,0:T(8,128)(2,1)} %pad_maximum_fusion), calls=%async_computation | async-start | bytes 3670016 | tf_op jit(solution)/shard_map/all_to_all | solution.py:1107
  96.5 61.2 %all-to-all-done.got = bf16[32,224,128]{2,1,0:T(8,128)(2,1)S(1)} async-done(((bf16[32,224,128]{2,1,0:T(8,128)(2,1)}), bf16[32,224,128]{2,1,0:T(8,128)(2,1)S(1)}, u32[]{:S(2)}, u32[]{:S(2)}) %all-to-all-start) | async-done | bytes 1835040 | tf_op jit(solution)/shard_map/all_to_all | solution.py:1107
  163.9 4.1 all-to-all-done.1
  168.0 4.4 %all-to-all-start.2 = ((bf16[16,160,128]{2,1,0:T(8,128)(2,1)}), bf16[16,160,128]{2,1,0:T(8,128)(2,1)}, u32[]{:S(2)}, u32[]{:S(2)}) async-start(bf16[16,160,128]{2,1,0:T(8,128)(2,1)} %get-tuple-element.74), calls=%async_computation.2 | async-start | bytes 1310720 | tf_op jit(solution)/shard_map/all_to_all | solution.py:1117
  175.8 3.7 multiply_sine_fusion
  185.5 10.6 %mixed.1 = (bf16[2048,1024]{1,0:T(8,128)(2,1)}, bf16[2048,1024]{1,0:T(8,128)(2,1)}, bf16[2048,64]{1,0:T(8,128)(2,1)}, bf16[2048,64]{1,0:T(8,128)(2,1)}, bf16[2048,64]{1,0:T(8,128)(2,1)}) custom-call(bf16[2,8,2,64,1024]{4,3,2,1,0:T(8,128)(2,1)} %bitcast.54, f32[8,1024]{1,0:T(8,128)} %get-tuple-element.70.vectors, bf16[1024,256]{1,0:T(8,128)(2,1)} %get-tuple-element.71.qkv_w, ...), custom_call_target="tpu_custom_call" | custom-call | tf_op jit(solution)/shard_map/mixed/pallas_call | solution.py:1149
  196.1 18.2 %attend.1 = (bf16[2048,64]{1,0:T(8,128)(2,1)}, f32[64,2048]{1,0:T(8,128)}, f32[1,2048]{1,0:T(1,128)}) custom-call(s32[1]{0:T(128)} %dynamic_slice.20.lengths, bf16[2048,64]{1,0:T(8,128)(2,1)} %get-tuple-element.75.query, bf16[2048,64]{1,0:T(8,128)(2,1)} %get-tuple-element.76.key, bf16[2048,64]{1,0:T(8,128)(2,1)} %get-tuple-element.77.value), custom_call_target="tpu_custom_call" | custom-call | tf_op jit(solution)/shard_map/attend/pallas_call | solution.py:1155
  216.5 16.4 %feed.1 = (bf16[8,2,64,1024]{3,2,1,0:T(8,128)(2,1)}, bf16[8,2,64,1024]{3,2,1,0:T(8,128)(2,1)}, bf16[2048,64]{1,0:T(8,128)(2,1)}, bf16[2048,256]{1,0:T(8,128)(2,1...) custom-call(s32[4]{0:T(128)} %pad_add_fusion.here, ...), custom_call_target="tpu_custom_call" | custom-call | tf_op jit(solution)/shard_map/feed/pallas_call | solution.py:1168
  235.4 19.4 %attend_back.1 = (bf16[2048,64]{1,0:T(8,128)(2,1)}, bf16[2048,64]{1,0:T(8,128)(2,1)}, bf16[2048,64]{1,0:T(8,128)(2,1)}) custom-call(s32[1]{0:T(128)} %dynamic_slice.20.lengths, bf16[2048,64]{1,0:T(8,128)(2,1)} %get-tuple-element.75.query, bf16[2048,64]{1,0:T(8,128)(2,1)} %get-tuple-element.76.key, bf16[2048,64]{1,0:T(8,128)(2,1)} %get-tuple-element.77.value, ...), custom_call_target="tpu_custom_call" | custom-call | tf_op jit(solution)/shard_map/attend_back/pallas_call | solution.py:1183
  254.8 13.9 %mixed_back.1 = (bf16[8,2,64,1024]{3,2,1,0:T(8,128)(2,1)}, bf16[8,2,64,1024]{3,2,1,0:T(8,128)(2,1)}, f32[1024,256]{1,0:T(8,128)}, f32[1,256]{1,0:T(1,128)}, f32[8,1024]{1,0:T(8,128)}) custom-call(s32[4]{0:T(128)} %pad_add_fusion.here, bf16[2,8,2,64,1024]{4,3,2,1,0:T(8,128)(2,1)} %bitcast.55, bf16[2048,1024]{1,0:T(8,128)(2,1)} %get-tuple-element.88.one, ...), custom_call_target="tpu_custom_call" | custom-call | tf_op jit(solution)/shard_map/mixed_back/pallas_call | solution.py:1191
  269.4 5.7 %all-to-all-start.3 = ((bf16[16,160,128]{2,1,0:T(8,128)(2,1)}), bf16[16,160,128]{2,1,0:T(8,128)(2,1)S(1)}, u32[]{:S(2)}, u32[]{:S(2)}) async-start(bf16[16,160,128]{2,1,0:T(8,128)(2,1)} %rows_out.1), calls=%async_computation.3 | async-start | bytes 1310720 | tf_op jit(solution)/shard_map/all_to_all | solution.py:1181
  275.2 4.6 %add_convert_fusion.1 = (bf16[4,2,64,1024]{3,2,1,0:T(8,128)(2,1)}, bf16[4,2,64,1024]{3,2,1,0:T(8,128)(2,1)}) fusion(bf16[8,2,64,1024]{3,2,1,0:T(8,128)(2,1)} %collective-permute-done.7, bf16[8,2,64,1024]{3,2,1,0:T(8,128)(2,1)} %get-tuple-element.99), kind=kLoop, calls=%fused_computation.1 | loop fusion | flops 4194304 | bytes 6291456 | tf_op jit(solution)/shard_map/convert_element_type | solution.py:1138
  287.4 6.2 %all-to-all-done.3.second = bf16[16,160,128]{2,1,0:T(8,128)(2,1)S(1)} async-done(((bf16[16,160,128]{2,1,0:T(8,128)(2,1)}), bf16[16,160,128]{2,1,0:T(8,128)(2,1)S(1)}, u32[]{:S(2)}, u32[]{:S(2)}) %all-to-all-start.3) | async-done | bytes 655392 | tf_op jit(solution)/shard_map/all_to_all | solution.py:1181
  294.5 4.9 %grads_out.1 = bf16[32,224,128]{2,1,0:T(8,128)(2,1)} custom-call(s32[1]{0:T(128)} %bitcast.10.scalars, bf16[16,160,128]{2,1,0:T(8,128)(2,1)} %copy-done.6, f32[1024,256]{1,0:T(8,128)} %get-tuple-element.102.qkv_g, f32[1024,256]{1,0:T(8,128)} %get-tuple-element.103.expand_g, f32[8,1024]{1,0:T(8,128)} %maximum_maximum_fusion.vector_g, ...), custom_call_target="tpu_custom_call" | custom-call | tf_op jit(solution)/shard_map/grads_out/pallas_call | solution.py:1205
  302.3 23.8 %collective-permute-done.8 = bf16[4,2,64,1024]{3,2,1,0:T(8,128)(2,1)} collective-permute-done((bf16[4,2,64,1024]{3,2,1,0:T(8,128)(2,1)}, bf16[4,2,64,1024]{3,2,1,0:T(8,128)(2,1)}, u32[]{:S(2)}, u32[]{:S(2)}) %collective-permute-start.8) | collective-permute-done | bytes 1048608 | tf_op jit(solution)/shard_map/ppermute | solution.py:1133
  328.1 22.1 %collective-permute-done.4 = bf16[4,2,64,1024]{3,2,1,0:T(8,128)(2,1)} collective-permute-done((bf16[4,2,64,1024]{3,2,1,0:T(8,128)(2,1)}, bf16[4,2,64,1024]{3,2,1,0:T(8,128)(2,1)}, u32[]{:S(2)}, u32[]{:S(2)}) %collective-permute-start.4) | collective-permute-done | bytes 1048608 | tf_op jit(solution)/shard_map/ppermute | solution.py:1133
  355.4 15.5 %collective-permute-done.5 = bf16[2,2,64,1024]{3,2,1,0:T(8,128)(2,1)S(1)} collective-permute-done((bf16[2,2,64,1024]{3,2,1,0:T(8,128)(2,1)S(1)}, bf16[2,2,64,1024]{3,2,1,0:T(8,128)(2,1)S(1)}, u32[]{:S(2)}, u32[]{:S(2)}) %collective-permute-start.5) | collective-permute-done | bytes 524320 | tf_op jit(solution)/shard_map/ppermute | solution.py:1133
  372.9 11.5 %collective-permute-done.6 = bf16[1,2,64,1024]{3,2,1,0:T(8,128)(2,1)} collective-permute-done((bf16[1,2,64,1024]{3,2,1,0:T(8,128)(2,1)S(1)}, bf16[1,2,64,1024]{3,2,1,0:T(8,128)(2,1)}, u32[]{:S(2)}, u32[]{:S(2)}) %collective-permute-start.6) | collective-permute-done | bytes 262176 | tf_op jit(solution)/shard_map/ppermute | solution.py:1133
  387.1 6.8 %collective-permute-done.11 = bf16[2,64,1024]{2,1,0:T(8,128)(2,1)S(1)} collective-permute-done((bf16[2,64,1024]{2,1,0:T(8,128)(2,1)S(1)}, bf16[2,64,1024]{2,1,0:T(8,128)(2,1)S(1)}, u32[]{:S(2)}, u32[]{:S(2)}) %collective-permute-start.11) | collective-permute-done | bytes 262176 | tf_op jit(solution)/shard_map/ppermute | solution.py:1038
  396.7 8.2 %grads_in.1 = f32[3120,128]{1,0:T(8,128)} custom-call(s32[4]{0:T(128)} %add_add_fusion.1.scalars, bf16[32,224,128]{2,1,0:T(8,128)(2,1)} %copy-done), custom_call_target="tpu_custom_call" | custom-call | tf_op jit(solution)/shard_map/grads_in/pallas_call | solution.py:1215
  (130 shorter events, 73.5 us)
Async XLA Ops:
  7.2 63.6 %all-gather.5.cloned.1.call-start = ((), (), s32[]{:S(2)}) async-start(), calls=%async_computation.5 | async-start | bytes 4456448 | tf_op jit(solution)/shard_map/all_gather | solution.py:1060
  7.2 63.6 %copy-start.3 = (f32[393632]{0:T(1024)S(1)}, f32[393632]{0:T(1024)}, u32[]{:S(2)}) copy-start(f32[393632]{0:T(1024)} %param.15) | copy-start | bytes 4723588
  8.5 9.3 %collective-permute-start = (bf16[2,64,1024]{2,1,0:T(8,128)(2,1)S(1)}, bf16[2,64,1024]{2,1,0:T(8,128)(2,1)S(1)}, u32[]{:S(2)}, u32[]{:S(2)}) collective-permute-start(bf16[2,64,1024]{2,1,0:T(8,128)(2,1)S(1)} %get-tuple-element.126), channel_id=1, source_target_pairs={{0,16},{16,0},{1,17},{17,1},{2,18},{18,2},{3,19},{19,3},{4,20},{20... | collective-permute-start | bytes 786440 | tf_op jit(solution)/shard_map/ppermute | solution.py:1038
  18.7 197.8 %all-gather.7.cloned.1.call-start = ((), (), s32[]{:S(2)}) async-start(), calls=%async_computation.6 | async-start | bytes 4456448 | tf_op jit(solution)/shard_map/all_gather | solution.py:1062
  70.8 7.8 %collective-permute-start.2 = (f32[4096]{0:T(1024)S(1)}, f32[4096]{0:T(1024)S(1)}, u32[]{:S(2)}, u32[]{:S(2)}) collective-permute-start(f32[4096]{0:T(1024)S(1)} %slice.144), channel_id=1, source_target_pairs={{1,0},{2,1},{3,2},{4,3},{5,4},{6,5},{7,6},{8,7},{9,8},{10,9},{11,1... | collective-permute-start | bytes 49160 | tf_op jit(solution)/shard_map/ppermute | solution.py:1080
  72.2 6.5 %collective-permute-start.1 = (f32[1024]{0:T(1024)S(1)}, f32[1024]{0:T(1024)S(1)}, u32[]{:S(2)}, u32[]{:S(2)}) collective-permute-start(f32[1024]{0:T(1024)S(1)} %slice.143), channel_id=1, source_target_pairs={{0,1},{1,2},{2,3},{3,4},{4,5},{5,6},{6,7},{7,8},{8,9},{9,10},{10,1... | collective-permute-start | bytes 12296 | tf_op jit(solution)/shard_map/ppermute | solution.py:1079
  89.5 68.3 %all-to-all-start = ((bf16[32,224,128]{2,1,0:T(8,128)(2,1)}), bf16[32,224,128]{2,1,0:T(8,128)(2,1)S(1)}, u32[]{:S(2)}, u32[]{:S(2)}) async-start(bf16[32,224,128]{2,1,0:T(8,128)(2,1)} %pad_maximum_fusion), calls=%async_computation | async-start | bytes 3670016 | tf_op jit(solution)/shard_map/all_to_all | solution.py:1107
  96.4 76.0 %copy-start.20 = (s32[2]{0:T(128)S(1)}, s32[2]{0:T(128)}, u32[]{:S(2)}) copy-start(s32[2]{0:T(128)} %param.13) | copy-start | bytes 28
  158.4 9.6 %all-to-all-start.1 = ((s32[32,1,128]{2,1,0:T(1,128)}), s32[32,1,128]{2,1,0:T(1,128)S(1)}, u32[]{:S(2)}, u32[]{:S(2)}) async-start(s32[32,1,128]{2,1,0:T(1,128)} %broadcast_in_dim.40), calls=%async_computation.1 | async-start | bytes 32768 | tf_op jit(solution)/shard_map/all_to_all | solution.py:1065
  168.0 46.3 %all-to-all-start.2 = ((bf16[16,160,128]{2,1,0:T(8,128)(2,1)}), bf16[16,160,128]{2,1,0:T(8,128)(2,1)}, u32[]{:S(2)}, u32[]{:S(2)}) async-start(bf16[16,160,128]{2,1,0:T(8,128)(2,1)} %get-tuple-element.74), calls=%async_computation.2 | async-start | bytes 1310720 | tf_op jit(solution)/shard_map/all_to_all | solution.py:1117
  268.7 6.5 %collective-permute-start.7 = (bf16[8,2,64,1024]{3,2,1,0:T(8,128)(2,1)}, bf16[8,2,64,1024]{3,2,1,0:T(8,128)(2,1)}, u32[]{:S(2)}, u32[]{:S(2)}) collective-permute-start(bf16[8,2,64,1024]{3,2,1,0:T(8,128)(2,1)} %get-tuple-element.100), channel_id=1, source_target_pairs={{0,8},{8,0},{1,9},{9,1},{2,10},{10,2},{3,11},{11,3},{4,12},{12,4},... | collective-permute-start | bytes 6291464 | tf_op jit(solution)/shard_map/ppermute | solution.py:1133
  268.8 12.9 %collective-permute-start.3 = (bf16[8,2,64,1024]{3,2,1,0:T(8,128)(2,1)}, bf16[8,2,64,1024]{3,2,1,0:T(8,128)(2,1)S(1)}, u32[]{:S(2)}, u32[]{:S(2)}) collective-permute-start(bf16[8,2,64,1024]{3,2,1,0:T(8,128)(2,1)} %get-tuple-element.87), channel_id=1, source_target_pairs={{0,8},{8,0},{1,9},{9,1},{2,10},{10,2},{3,11},{11,3},{4,12},{12,4},... | collective-permute-start | bytes 6291464 | tf_op jit(solution)/shard_map/ppermute | solution.py:1133
  269.4 24.2 %all-to-all-start.3 = ((bf16[16,160,128]{2,1,0:T(8,128)(2,1)}), bf16[16,160,128]{2,1,0:T(8,128)(2,1)S(1)}, u32[]{:S(2)}, u32[]{:S(2)}) async-start(bf16[16,160,128]{2,1,0:T(8,128)(2,1)} %rows_out.1), calls=%async_computation.3 | async-start | bytes 1310720 | tf_op jit(solution)/shard_map/all_to_all | solution.py:1181
  279.8 46.3 %collective-permute-start.8 = (bf16[4,2,64,1024]{3,2,1,0:T(8,128)(2,1)}, bf16[4,2,64,1024]{3,2,1,0:T(8,128)(2,1)}, u32[]{:S(2)}, u32[]{:S(2)}) collective-permute-start(bf16[4,2,64,1024]{3,2,1,0:T(8,128)(2,1)} %get-tuple-element.112), channel_id=1, source_target_pairs={{0,1},{1,0},{2,3},{3,2},{4,5},{5,4},{6,7},{7,6},{8,9},{9,8},{10,11... | collective-permute-start | bytes 3145736 | tf_op jit(solution)/shard_map/ppermute | solution.py:1133
  286.6 63.6 %collective-permute-start.4 = (bf16[4,2,64,1024]{3,2,1,0:T(8,128)(2,1)}, bf16[4,2,64,1024]{3,2,1,0:T(8,128)(2,1)}, u32[]{:S(2)}, u32[]{:S(2)}) collective-permute-start(bf16[4,2,64,1024]{3,2,1,0:T(8,128)(2,1)} %get-tuple-element.114), channel_id=1, source_target_pairs={{0,1},{1,0},{2,3},{3,2},{4,5},{5,4},{6,7},{7,6},{8,9},{9,8},{10,11... | collective-permute-start | bytes 3145736 | tf_op jit(solution)/shard_map/ppermute | solution.py:1133
  299.4 96.0 %all-to-all-start.4 = ((bf16[32,224,128]{2,1,0:T(8,128)(2,1)}), bf16[32,224,128]{2,1,0:T(8,128)(2,1)S(1)}, u32[]{:S(2)}, u32[]{:S(2)}) async-start(bf16[32,224,128]{2,1,0:T(8,128)(2,1)} %grads_out.1), calls=%async_computation.4 | async-start | bytes 3670016 | tf_op jit(solution)/shard_map/all_to_all | solution.py:1212
  328.0 25.9 %copy-start.9 = (bf16[2,2,64,1024]{3,2,1,0:T(8,128)(2,1)}, bf16[2,2,64,1024]{3,2,1,0:T(8,128)(2,1)S(1)}, u32[]{:S(2)}) copy-start(bf16[2,2,64,1024]{3,2,1,0:T(8,128)(2,1)S(1)} %get-tuple-element.115) | copy-start | bytes 1572868
  328.0 25.8 %collective-permute-start.9 = (bf16[2,2,64,1024]{3,2,1,0:T(8,128)(2,1)S(1)}, bf16[2,2,64,1024]{3,2,1,0:T(8,128)(2,1)S(1)}, u32[]{:S(2)}, u32[]{:S(2)}) collective-permute-start(bf16[2,2,64,1024]{3,2,1,0:T(8,128)(2,1)S(1)} %get-tuple-element.116), channel_id=1, source_target_pairs={{0,2},{2,0},{4,6},{6,4},{1,3},{3,1},{5,7},{7,5},{8,10},{10,8},{12,... | collective-permute-start | bytes 1572872 | tf_op jit(solution)/shard_map/ppermute | solution.py:1133
  351.8 19.2 %collective-permute-start.5 = (bf16[2,2,64,1024]{3,2,1,0:T(8,128)(2,1)S(1)}, bf16[2,2,64,1024]{3,2,1,0:T(8,128)(2,1)S(1)}, u32[]{:S(2)}, u32[]{:S(2)}) collective-permute-start(bf16[2,2,64,1024]{3,2,1,0:T(8,128)(2,1)S(1)} %get-tuple-element.118), channel_id=1, source_target_pairs={{0,2},{2,0},{4,6},{6,4},{1,3},{3,1},{5,7},{7,5},{8,10},{10,8},{12,... | collective-permute-start | bytes 1572872 | tf_op jit(solution)/shard_map/ppermute | solution.py:1133
  353.9 17.8 %collective-permute-start.10 = (bf16[1,2,64,1024]{3,2,1,0:T(8,128)(2,1)S(1)}, bf16[1,2,64,1024]{3,2,1,0:T(8,128)(2,1)S(1)}, u32[]{:S(2)}, u32[]{:S(2)}) collective-permute-start(bf16[1,2,64,1024]{3,2,1,0:T(8,128)(2,1)S(1)} %add_convert_fusion.9), channel_id=1, source_target_pairs={{0,4},{4,0},{2,6},{6,2},{1,5},{5,1},{3,7},{7,3},{8,12},{12,8},{10,... | collective-permute-start | bytes 786440 | tf_op jit(solution)/shard_map/ppermute | solution.py:1133
  371.1 13.3 %collective-permute-start.6 = (bf16[1,2,64,1024]{3,2,1,0:T(8,128)(2,1)S(1)}, bf16[1,2,64,1024]{3,2,1,0:T(8,128)(2,1)}, u32[]{:S(2)}, u32[]{:S(2)}) collective-permute-start(bf16[1,2,64,1024]{3,2,1,0:T(8,128)(2,1)S(1)} %add_convert_fusion.12), channel_id=1, source_target_pairs={{0,4},{4,0},{2,6},{6,2},{1,5},{5,1},{3,7},{7,3},{8,12},{12,8},{10,... | collective-permute-start | bytes 786440 | tf_op jit(solution)/shard_map/ppermute | solution.py:1133
  385.6 8.3 %collective-permute-start.11 = (bf16[2,64,1024]{2,1,0:T(8,128)(2,1)S(1)}, bf16[2,64,1024]{2,1,0:T(8,128)(2,1)S(1)}, u32[]{:S(2)}, u32[]{:S(2)}) collective-permute-start(bf16[2,64,1024]{2,1,0:T(8,128)(2,1)S(1)} %get-tuple-element.122), channel_id=1, source_target_pairs={{0,16},{16,0},{1,17},{17,1},{2,18},{18,2},{3,19},{19,3},{4,20},{20... | collective-permute-start | bytes 786440 | tf_op jit(solution)/shard_map/ppermute | solution.py:1038
  405.8 6.6 %collective-permute-start.12 = (f32[4096]{0:T(1024)S(1)}, f32[4096]{0:T(1024)S(1)}, u32[]{:S(2)}, u32[]{:S(2)}) collective-permute-start(f32[4096]{0:T(1024)S(1)} %slice.206), channel_id=1, source_target_pairs={{0,1},{1,2},{2,3},{3,4},{4,5},{5,6},{6,7},{7,8},{8,9},{9,10},{10,1... | collective-permute-start | bytes 49160 | tf_op jit(solution)/shard_map/ppermute | solution.py:1219
  411.1 5.5 %collective-permute-start.13 = (f32[1024]{0:T(1024)S(1)}, f32[1024]{0:T(1024)S(1)}, u32[]{:S(2)}, u32[]{:S(2)}) collective-permute-start(f32[1024]{0:T(1024)S(1)} %slice_bitcast_fusion.4), channel_id=1, source_target_pairs={{1,0},{2,1},{3,2},{4,3},{5,4},{6,5},{7,6},{8,7},{9,8},{10,9},{11,1... | collective-permute-start | bytes 12296 | tf_op jit(solution)/shard_map/ppermute | solution.py:1220
  (18 other events, 136.3 us)
Sparse Core Ops, SparseCore 0:
  18.9 51.8 all-gather.4
  73.5 68.7 all-gather.6

commit v4 on v3

--- a/solution.py
+++ b/solution.py
@@ -438,7 +438,7 @@
 BF16 = jnp.bfloat16
 
 
-def call(body, grid, in_specs, out_specs, out_shape, scratch=(), prefetch=0, name=None):
+def call(body, grid, in_specs, out_specs, out_shape, scratch=(), prefetch=0):
     return pl.pallas_call(
         body,
         grid_spec=pltpu.PrefetchScalarGridSpec(
@@ -449,7 +449,6 @@
             scratch_shapes=scratch,
         ),
         out_shape=out_shape,
-        name=name,
         compiler_params=pltpu.CompilerParams(vmem_limit_bytes=56 << 20),
     )
 
@@ -487,20 +486,6 @@
 LEAD = 4 * D // LANES
 EDGE = PER * D + 13 * D // OWNERS
 PROJECT, PLAIN, PLAIN_EXPAND, EXPAND, EXPAND_PLAIN = range(5)
-
-
-def kind_of(c):
-    return (
-        PROJECT
-        if c < 8
-        else PLAIN
-        if c < 10 or c > 21
-        else PLAIN_EXPAND
-        if c == 10
-        else EXPAND_PLAIN
-        if c == 21
-        else EXPAND
-    )
 
 
 def plain_place(row, base, count):
@@ -1058,12 +1043,9 @@
     rows = paired(at_x(rows, x), across_x(at_x(rows, 1 - x)))
     tokens_shape = (2, groups, 2, span, width)
     slot_tokens = lax.all_gather(rows[:, 0], RING, axis=0).reshape(tokens_shape)
-    later, slot_tokens = lax.optimization_barrier((rows[:, 1], slot_tokens))
-    slot_cotangent = lax.all_gather(later, RING, axis=0).reshape(tokens_shape)
 
     place = jnp.broadcast_to(positions.reshape(1, slots * span), (OWNERS, slots * span))
     place = lax.all_to_all(place, ALL, 0, 0, tiled=True)
-    known = place
     place = place.reshape(2, 2, groups, slots, span)
     place = lax.dynamic_index_in_dim(place, x, 3, keepdims=False).transpose(2, 0, 1, 3).reshape(count)
     half_dims = ROT // 2
@@ -1101,10 +1083,12 @@
         whole((16, SEND_ROWS, LANES)),
         shaped((16, SEND_ROWS, LANES), BF16),
         [pltpu.VMEM((3280, LANES), F32), pltpu.VMEM((SHIFT_ROWS, LANES), F32), pltpu.VMEM((48, LANES), F32)],
-        1, "weights_out",
+        1,
     )(scalars, before, own, after)
-    sent, _ = lax.optimization_barrier((jnp.concatenate([sent, sent]), known))
+    sent = jnp.concatenate([sent, sent])
     got = lax.all_to_all(sent, ALL, 0, 0, tiled=True)
+    later, got = lax.optimization_barrier((rows[:, 1], got))
+    slot_cotangent = lax.all_gather(later, RING, axis=0).reshape(tokens_shape)
     head_scalar = head.astype(jnp.int32).reshape(1)
     qkv_w, expand_w, second, vectors, qkv_b, expand_b = call(
         weights_in_body, (1,),
@@ -1112,7 +1096,7 @@
         [whole((D, 256)), whole((D, 256)), whole((16, 160, LANES)), whole((8, D)), whole((1, 256)), whole((1, 256))],
         [shaped((D, 256), BF16), shaped((D, 256), BF16), shaped((16, 160, LANES), BF16), shaped((8, D), F32),
          shaped((1, 256), F32), shaped((1, 256), F32)],
-        [pltpu.VMEM((24, LANES), F32), pltpu.VMEM((32, LANES), F32)], 1, "weights_in",
+        [pltpu.VMEM((24, LANES), F32), pltpu.VMEM((32, LANES), F32)], 1,
     )(head_scalar, got)
     second = lax.all_to_all(second, RING, 0, 0, tiled=True)
     steps = (count // BLOCK,)
@@ -1150,19 +1134,19 @@
         mixed_body, steps,
         [token_spec, whole((8, D)), whole((D, 256)), whole((1, 256)), rows_spec(LANES), rows_spec(LANES)],
         [rows_spec(D), rows_spec(D), rows_spec(HD), rows_spec(HD), rows_spec(HD)],
-        [shaped((count, D), BF16), shaped((count, D), BF16), narrow, narrow, narrow], name="mixed",
+        [shaped((count, D), BF16), shaped((count, D), BF16), narrow, narrow, narrow],
     )(slot_tokens, vectors, qkv_w, qkv_b, cos, sin)
     attended, attended_full, log_total = call(
         attend_body, steps,
         [rows_spec(HD), whole((count, HD)), whole((count, HD))],
         [rows_spec(HD), columns_spec(HD), columns_spec(1)],
         [narrow, shaped((HD, count), F32), shaped((1, count), F32)],
-        [pltpu.VMEM((count, BLOCK), F32), pltpu.VMEM((HD, count), BF16)], 1, "attend",
+        [pltpu.VMEM((count, BLOCK), F32), pltpu.VMEM((HD, count), BF16)], 1,
     )(length, query, key, value)
     second, attended = lax.optimization_barrier((second, attended))
     dense_w, shrink_w = call(
         rows_in_body, (1,), [whole(second.shape)], [whole((HD, D)), whole((256, D))],
-        [shaped((HD, D), BF16), shaped((256, D), BF16)], name="rows_in",
+        [shaped((HD, D), BF16), shaped((256, D), BF16)],
     )(second)
 
     kept, sent, attended_g, hidden_g, shrink_g, dense_g, expand_g, expand_bg, bias_g = call(
@@ -1171,11 +1155,11 @@
         [part_spec, part_spec, rows_spec(HD), rows_spec(256), whole((256, D)), whole((HD, D)), whole((D, 256)),
          whole((1, 256)), whole((1, D))],
         [part_shape, part_shape, narrow, shaped((count, 256), BF16), shaped((256, D), F32), shaped((HD, D), F32),
-         shaped((D, 256), F32), shaped((1, 256), F32), shaped((1, D), F32)], (), 1, "feed",
+         shaped((D, 256), F32), shaped((1, 256), F32), shaped((1, D), F32)], (), 1,
     )(here, two, attended, slot_cotangent, expand_w, expand_b, shrink_w, dense_w)
     second_g = call(
         rows_out_body, (1,), [whole((HD, D)), whole((256, D))], whole((16, 160, LANES)),
-        shaped((16, 160, LANES), BF16), name="rows_out",
+        shaped((16, 160, LANES), BF16),
     )(dense_g, shrink_g)
     attended_g, second_g = lax.optimization_barrier((attended_g, second_g))
     second_g = lax.all_to_all(second_g, RING, 0, 0, tiled=True)
@@ -1186,14 +1170,14 @@
         [rows_spec(HD), whole((count, HD)), whole((count, HD))],
         [narrow, narrow, narrow],
         [pltpu.VMEM((HD, count), BF16), pltpu.VMEM((count, HD), F32), pltpu.VMEM((count, HD), F32)],
-        1, "attend_back",
+        1,
     )(length, query, key, value, attended_g, attended_full, log_total)
     kept, sent, qkv_g, qkv_bg, vector_g = call(
         mixed_back_body, steps,
         [token_spec, rows_spec(D), rows_spec(HD), rows_spec(HD), rows_spec(HD),
          rows_spec(256), whole((8, D)), whole((D, 256)), whole((D, 256)), rows_spec(LANES), rows_spec(LANES)],
         [part_spec, part_spec, whole((D, 256)), whole((1, 256)), whole((8, D))],
-        [part_shape, part_shape, shaped((D, 256), F32), shaped((1, 256), F32), shaped((8, D), F32)], (), 1, "mixed_back",
+        [part_shape, part_shape, shaped((D, 256), F32), shaped((1, 256), F32), shaped((8, D), F32)], (), 1,
     )(here, slot_tokens, one, query_g, key_g, value_g, hidden_g, vectors, qkv_w, expand_w, cos, sin)
     in_rows = summed(kept, sent)
     rows = jnp.stack([out_rows, in_rows], axis=1).astype(BF16)
@@ -1207,14 +1191,14 @@
         [whole((16, 160, LANES)), whole((D, 256)), whole((D, 256)), whole((8, D)), whole((1, 256)), whole((1, 256))],
         whole((OWNERS, BACK_ROWS, LANES)),
         shaped((OWNERS, BACK_ROWS, LANES), BF16),
-        [pltpu.VMEM((32, LANES), F32), pltpu.VMEM((32, LANES), F32)], 1, "grads_out",
+        [pltpu.VMEM((32, LANES), F32), pltpu.VMEM((32, LANES), F32)], 1,
     )(head_scalar, second_g, qkv_g, expand_g, vector_g, qkv_bg, expand_bg)
     got_g = lax.all_to_all(sent_g, ALL, 0, 0, tiled=True)
     begin_g = (chunk - PER * D) * owner - skipped * D + 4 * D
     scalars_g = jnp.stack([begin_g // LANES, begin_g % LANES, kind, vector_row]).astype(jnp.int32)
     taken = call(
         grads_in_body, (1,), [whole(got_g.shape)], whole((TAKE_ROWS, LANES)), shaped((TAKE_ROWS, LANES), F32),
-        [pltpu.VMEM((SHIFT_ROWS, LANES), F32)], 1, "grads_in",
+        [pltpu.VMEM((SHIFT_ROWS, LANES), F32)], 1,
     )(scalars_g, got_g).reshape(-1)
     from_before = lax.ppermute(taken[D + chunk : 5 * D + chunk], ALL, onward)
     from_after = lax.ppermute(taken[:D], ALL, backward)
@@ -1242,9 +1226,11 @@
 
 
 def solution(mesh):
+    fits = mesh.size == OWNERS and mesh.shape["blk"] == 4
+
     def step(*args):
         slots, tokens = args[0].shape[:2]
-        if mesh.size == OWNERS == slots * H and mesh.shape["blk"] == 4 and tokens == 64 * OWNERS:
+        if fits and slots * H == OWNERS and tokens == 64 * OWNERS:
             tokens_in, flat, used, body = P(None, ("z", "y", "x", "core"), None), P(ALL), split_mesh(mesh), by_head
             places = P(None, ("z", "y", "x", "core"))
         else:

time: 430 us -> 378 us (0.88)
  waiting for transfers between devices: 213 us -> 87.8 us
  blocking collectives: 0 us -> 69.8 us
  starting transfers between devices: 42.6 us -> 55.9 us
  Pallas kernels: 106 us -> 97 us
    all_to_all x0 -> x1, blocking collectives: none -> 69.8 us  [by_head(): got = lax.all_to_all(sent, ALL, 0, 0, tiled=True)]
    all_to_all x1 -> x0, waiting for transfers between devices: 61.2 us -> none  [by_head(): got = lax.all_to_all(sent, ALL, 0, 0, tiled=True)]
    all_gather x1, waiting for transfers between devices: 52 us -> 0.01 us  [by_head(): slot_tokens = lax.all_gather(rows[:, 0], RING, axis=0).reshape(tokens_shape)]
    ppermute x8, waiting for transfers between devices: 72.9 us -> 62.7 us  [summed(): came = lax.ppermute(sent, axis, route)]
    ppermute x2, starting transfers between devices: 3.1 us -> 13.2 us  [across_x(): return lax.ppermute(block, 'x', [(0, 1), (1, 0)])]
    all_to_all x1, starting transfers between devices: 2.71 us -> 11 us  [by_head(): got_g = lax.all_to_all(sent_g, ALL, 0, 0, tiled=True)]
    pallas_call x1, Pallas kernels: 19.4 us -> 12.2 us  [by_head(): call(attend_back_body, steps, [rows_spec(HD), whole((count, HD)), whole((...]
    all_to_all x1 -> x0, starting transfers between devices: 6.97 us -> none  [by_head(): got = lax.all_to_all(sent, ALL, 0, 0, tiled=True)]
  transfers between devices with their start and end apart: 21 -> 20, of which waited for: 11 -> 9; matrix products, arithmetic and copies ran while one was open for 9% -> 10% of each run, Pallas kernels for 11% -> 12%
where the time goes in v4:
time: 378 us; the launch traced here: 374 us
  Pallas kernels  97 us (26%)
  waiting for transfers between devices  87.8 us (23%)
  blocking collectives  69.8 us (18%)
  starting transfers between devices  55.9 us (15%)
  other arithmetic  30.9 us (8%)
  local copies, waits for them, and re-layouts  17.5 us (5%)
  between operations  14.5 us (4%)
    all_to_all x1, blocking collectives, by_head(): got = lax.all_to_all(sent, ALL, 0, 0, tiled=True)  69.8 us
    ppermute x8, waiting for transfers between devices, summed(): came = lax.ppermute(sent, axis, route)  62.7 us
    pallas_call x1, Pallas kernels, by_head(): call(feed_body, steps, [rows_spec(D), rows_spec(HD), token_spec, whole((D...  16.5 us
    pallas_call x1, Pallas kernels, by_head(): call(attend_body, steps, [rows_spec(HD), whole((count, HD)), whole((count...  15.9 us
    pallas_call x1, Pallas kernels, by_head(): call(mixed_back_body, steps, [token_spec, rows_spec(D), rows_spec(HD), ro...  13.9 us
    ppermute x2, starting transfers between devices, across_x(): return lax.ppermute(block, 'x', [(0, 1), (1, 0)])  13.2 us
    pallas_call x1, Pallas kernels, by_head(): call(attend_back_body, steps, [rows_spec(HD), whole((count, HD)), whole((...  12.2 us
    convert_element_type x6, other arithmetic, summed(): (kept[half].astype(F32) + came[half].astype(F32)).astype(BF16)  11.8 us
  transfers between devices with their start and end apart: 20, of which 9 were waited for; matrix products, arithmetic and copies ran while one was open for 10% of the time, Pallas kernels for 12%

profile of v4, /device:TPU:0, one launch (start us, length us, event | category | flops | bytes accessed | tf_op | source)
XLA Modules:
  0.0 373.6 jit_solution(12465296450016793450)
XLA Ops:
  11.5 6.3 %collective-permute-done = bf16[2,64,1024]{2,1,0:T(8,128)(2,1)S(1)} collective-permute-done((bf16[2,64,1024]{2,1,0:T(8,128)(2,1)S(1)}, bf16[2,64,1024]{2,1,0:T(8,128)(2,1)S(1)}, u32[]{:S(2)}, u32[]{:S(2)}) %collective-permute-start) | collective-permute-done | bytes 262176 | tf_op jit(solution)/shard_map/ppermute | solution.py:1023
  20.2 4.5 %collective-permute-start.1 = (f32[1024]{0:T(1024)S(1)}, f32[1024]{0:T(1024)S(1)}, u32[]{:S(2)}, u32[]{:S(2)}) collective-permute-start(f32[1024]{0:T(1024)S(1)} %slice.143), channel_id=1, source_target_pairs={{0,1},{1,2},{2,3},{3,4},{4,5},{5,6},{6,7},{7,8},{8,9},{9,10},{10,1... | collective-permute-start | bytes 12296 | tf_op jit(solution)/shard_map/ppermute | solution.py:1061
  27.3 7.2 %shard_map.118 = bf16[16,224,128]{2,1,0:T(8,128)(2,1)} custom-call(s32[4]{0:T(128)} %add_add_fusion.scalars, f32[8,128]{1,0:T(8,128)} %bitcast.66, f32[3080,128]{1,0:T(8,128)} %pad_bitcast_fusion.own, f32[32,128]{1,0:T(8,128)} %bitcast.64), custom_call_target="tpu_custom_call" | custom-call | tf_op jit(solution)/shard_map/pallas_call | solution.py:1080
  36.2 69.8 %all_to_all.26.got = bf16[32,224,128]{2,1,0:T(8,128)(2,1)} all-to-all(bf16[32,224,128]{2,1,0:T(8,128)(2,1)S(1)} %pad_maximum_fusion), channel_id=1, replica_groups=mesh['x'=2,'core'=2,'z'=4,'y'=2] {'x','core','z','y'}, dimensions={0} | all-to-all | bytes 3670016 | tf_op jit(solution)/shard_map/all_to_all | solution.py:1089
  112.2 4.1 %all-to-all-done.1 = s32[32,1,128]{2,1,0:T(1,128)S(1)} async-done(((s32[32,1,128]{2,1,0:T(1,128)}), s32[32,1,128]{2,1,0:T(1,128)S(1)}, u32[]{:S(2)}, u32[]{:S(2)}) %all-to-all-start.1) | async-done | bytes 16416 | tf_op jit(solution)/shard_map/all_to_all | solution.py:1048
  116.3 4.4 %all-to-all-start.2 = ((bf16[16,160,128]{2,1,0:T(8,128)(2,1)}), bf16[16,160,128]{2,1,0:T(8,128)(2,1)}, u32[]{:S(2)}, u32[]{:S(2)}) async-start(bf16[16,160,128]{2,1,0:T(8,128)(2,1)} %get-tuple-element.74), calls=%async_computation.2 | async-start | bytes 1310720 | tf_op jit(solution)/shard_map/all_to_all | solution.py:1101
  124.1 3.7 multiply_sine_fusion
  133.8 10.7 %shard_map.120 = (bf16[2048,1024]{1,0:T(8,128)(2,1)}, bf16[2048,1024]{1,0:T(8,128)(2,1)}, bf16[2048,64]{1,0:T(8,128)(2,1)}, bf16[2048,64]{1,0:T(8,128)(2,1)}, bf16[2048,64]{1,0:T(8,128)(2,1)}) custom-call(bf16[2,8,2,64,1024]{4,3,2,1,0:T(8,128)(2,1)} %bitcast.54, f32[8,1024]{1,0:T(8,128)} %get-tuple-element.70.vectors, ...), custom_call_target="tpu_custom_call" | custom-call | tf_op jit(solution)/shard_map/pallas_call | solution.py:1133
  144.5 15.9 %shard_map.121 = (bf16[2048,64]{1,0:T(8,128)(2,1)}, f32[64,2048]{1,0:T(8,128)}, f32[1,2048]{1,0:T(1,128)}) custom-call(s32[1]{0:T(128)} %dynamic_slice.20.lengths, bf16[2048,64]{1,0:T(8,128)(2,1)} %get-tuple-element.75.query, bf16[2048,64]{1,0:T(8,128)(2,1)} %get-tuple-element.76.key, bf16[2048,64]{1,0:T(8,128)(2,1)} %get-tuple-element.77.value), custom_call_target="tpu_custom_call" | custom-call | tf_op jit(solution)/shard_map/pallas_call | solution.py:1139
  162.6 16.5 %shard_map.123 = (bf16[8,2,64,1024]{3,2,1,0:T(8,128)(2,1)}, bf16[8,2,64,1024]{3,2,1,0:T(8,128)(2,1)}, bf16[2048,64]{1,0:T(8,128)(2,1)}, bf16[2048,256]{1,0:T(8,1...) custom-call(s32[4]{0:T(128)} %pad_add_fusion.here, ...), custom_call_target="tpu_custom_call" | custom-call | tf_op jit(solution)/shard_map/pallas_call | solution.py:1152
  181.5 12.2 %shard_map.125 = (bf16[2048,64]{1,0:T(8,128)(2,1)}, bf16[2048,64]{1,0:T(8,128)(2,1)}, bf16[2048,64]{1,0:T(8,128)(2,1)}) custom-call(s32[1]{0:T(128)} %dynamic_slice.20.lengths, bf16[2048,64]{1,0:T(8,128)(2,1)} %get-tuple-element.75.query, bf16[2048,64]{1,0:T(8,128)(2,1)} %get-tuple-element.76.key, bf16[2048,64]{1,0:T(8,128)(2,1)} %get-tuple-element.77.value, ...), custom_call_target="tpu_custom_call" | custom-call | tf_op jit(solution)/shard_map/pallas_call | solution.py:1167
  193.7 13.9 %shard_map.126 = (bf16[8,2,64,1024]{3,2,1,0:T(8,128)(2,1)}, bf16[8,2,64,1024]{3,2,1,0:T(8,128)(2,1)}, f32[1024,256]{1,0:T(8,128)}, f32[1,256]{1,0:T(1,128)}, f32[8,1024]{1,0:T(8,128)}) custom-call(s32[4]{0:T(128)} %pad_add_fusion.here, bf16[2,8,2,64,1024]{4,3,2,1,0:T(8,128)(2,1)} %bitcast.55, bf16[2048,1024]{1,0:T(8,128)(2,1)} %get-tuple-element.88.one, ...), custom_call_target="tpu_custom_call" | custom-call | tf_op jit(solution)/shard_map/pallas_call | solution.py:1175
  208.4 5.6 %all-to-all-start.3 = ((bf16[16,160,128]{2,1,0:T(8,128)(2,1)}), bf16[16,160,128]{2,1,0:T(8,128)(2,1)S(1)}, u32[]{:S(2)}, u32[]{:S(2)}) async-start(bf16[16,160,128]{2,1,0:T(8,128)(2,1)} %shard_map.124), calls=%async_computation.3 | async-start | bytes 1310720 | tf_op jit(solution)/shard_map/all_to_all | solution.py:1165
  214.1 4.6 %add_convert_fusion.1 = (bf16[4,2,64,1024]{3,2,1,0:T(8,128)(2,1)}, bf16[4,2,64,1024]{3,2,1,0:T(8,128)(2,1)}) fusion(bf16[8,2,64,1024]{3,2,1,0:T(8,128)(2,1)} %collective-permute-done.7, bf16[8,2,64,1024]{3,2,1,0:T(8,128)(2,1)} %get-tuple-element.99), kind=kLoop, calls=%fused_computation.1 | loop fusion | flops 4194304 | bytes 6291456 | tf_op jit(solution)/shard_map/convert_element_type | solution.py:1122
  222.0 3.5 add_convert_fusion.3
  226.3 6.2 %all-to-all-done.3.second = bf16[16,160,128]{2,1,0:T(8,128)(2,1)S(1)} async-done(((bf16[16,160,128]{2,1,0:T(8,128)(2,1)}), bf16[16,160,128]{2,1,0:T(8,128)(2,1)S(1)}, u32[]{:S(2)}, u32[]{:S(2)}) %all-to-all-start.3) | async-done | bytes 655392 | tf_op jit(solution)/shard_map/all_to_all | solution.py:1165
  233.4 4.8 %shard_map.127 = bf16[32,224,128]{2,1,0:T(8,128)(2,1)} custom-call(s32[1]{0:T(128)} %bitcast.9.scalars, bf16[16,160,128]{2,1,0:T(8,128)(2,1)} %copy-done.5, f32[1024,256]{1,0:T(8,128)} %get-tuple-element.102.qkv_g, f32[1024,256]{1,0:T(8,128)} %get-tuple-element.103.expand_g, f32[8,1024]{1,0:T(8,128)} %maximum_maximum_fusion.vector_g, ...), custom_call_target="tpu_custom_call" | custom-call | tf_op jit(solution)/shard_map/pallas_call | solution.py:1189
  238.2 11.0 %all-to-all-start.4 = ((bf16[32,224,128]{2,1,0:T(8,128)(2,1)}), bf16[32,224,128]{2,1,0:T(8,128)(2,1)S(1)}, u32[]{:S(2)}, u32[]{:S(2)}) async-start(bf16[32,224,128]{2,1,0:T(8,128)(2,1)} %shard_map.127), calls=%async_computation.4 | async-start | bytes 3670016 | tf_op jit(solution)/shard_map/all_to_all | solution.py:1196
  253.4 34.5 %collective-permute-done.4 = bf16[4,2,64,1024]{3,2,1,0:T(8,128)(2,1)} collective-permute-done((bf16[4,2,64,1024]{3,2,1,0:T(8,128)(2,1)}, bf16[4,2,64,1024]{3,2,1,0:T(8,128)(2,1)}, u32[]{:S(2)}, u32[]{:S(2)}) %collective-permute-start.4) | collective-permute-done | bytes 1048608 | tf_op jit(solution)/shard_map/ppermute | solution.py:1117
  295.4 14.2 %collective-permute-done.5 = bf16[2,2,64,1024]{3,2,1,0:T(8,128)(2,1)S(1)} collective-permute-done((bf16[2,2,64,1024]{3,2,1,0:T(8,128)(2,1)S(1)}, bf16[2,2,64,1024]{3,2,1,0:T(8,128)(2,1)S(1)}, u32[]{:S(2)}, u32[]{:S(2)}) %collective-permute-start.5) | collective-permute-done | bytes 524320 | tf_op jit(solution)/shard_map/ppermute | solution.py:1117
  311.7 11.6 %collective-permute-done.6 = bf16[1,2,64,1024]{3,2,1,0:T(8,128)(2,1)} collective-permute-done((bf16[1,2,64,1024]{3,2,1,0:T(8,128)(2,1)S(1)}, bf16[1,2,64,1024]{3,2,1,0:T(8,128)(2,1)}, u32[]{:S(2)}, u32[]{:S(2)}) %collective-permute-start.6) | collective-permute-done | bytes 262176 | tf_op jit(solution)/shard_map/ppermute | solution.py:1117
  324.5 10.2 %collective-permute-start.11 = (bf16[2,64,1024]{2,1,0:T(8,128)(2,1)S(1)}, bf16[2,64,1024]{2,1,0:T(8,128)(2,1)S(1)}, u32[]{:S(2)}, u32[]{:S(2)}) collective-permute-start(bf16[2,64,1024]{2,1,0:T(8,128)(2,1)S(1)} %get-tuple-element.122), channel_id=1, source_target_pairs={{0,16},{16,0},{1,17},{17,1},{2,18},{18,2},{3,19},{19,3},{4,20},{20... | collective-permute-start | bytes 786440 | tf_op jit(solution)/shard_map/ppermute | solution.py:1023
  336.2 5.1 %collective-permute-done.11 = bf16[2,64,1024]{2,1,0:T(8,128)(2,1)S(1)} collective-permute-done((bf16[2,64,1024]{2,1,0:T(8,128)(2,1)S(1)}, bf16[2,64,1024]{2,1,0:T(8,128)(2,1)S(1)}, u32[]{:S(2)}, u32[]{:S(2)}) %collective-permute-start.11) | collective-permute-done | bytes 262176 | tf_op jit(solution)/shard_map/ppermute | solution.py:1023
  343.9 8.2 %shard_map.128 = f32[3120,128]{1,0:T(8,128)} custom-call(s32[4]{0:T(128)} %add_add_fusion.1.scalars, bf16[32,224,128]{2,1,0:T(8,128)(2,1)} %copy-done), custom_call_target="tpu_custom_call" | custom-call | tf_op jit(solution)/shard_map/pallas_call | solution.py:1199
  (127 shorter events, 70.2 us)
Async XLA Ops:
  7.2 126.6 %all-gather.5.cloned.1.call-start = ((), (), s32[]{:S(2)}) async-start(), calls=%async_computation.5 | async-start | bytes 4456448 | tf_op jit(solution)/shard_map/all_gather | solution.py:1045
  8.5 9.3 %collective-permute-start = (bf16[2,64,1024]{2,1,0:T(8,128)(2,1)S(1)}, bf16[2,64,1024]{2,1,0:T(8,128)(2,1)S(1)}, u32[]{:S(2)}, u32[]{:S(2)}) collective-permute-start(bf16[2,64,1024]{2,1,0:T(8,128)(2,1)S(1)} %get-tuple-element.126), channel_id=1, source_target_pairs={{0,16},{16,0},{1,17},{17,1},{2,18},{18,2},{3,19},{19,3},{4,20},{20... | collective-permute-start | bytes 786440 | tf_op jit(solution)/shard_map/ppermute | solution.py:1023
  18.7 143.9 %all-gather.7.cloned.1.call-start = ((), (), s32[]{:S(2)}) async-start(), calls=%async_computation.6 | async-start | bytes 4456448 | tf_op jit(solution)/shard_map/all_gather | solution.py:1091
  18.8 7.9 %collective-permute-start.2 = (f32[4096]{0:T(1024)S(1)}, f32[4096]{0:T(1024)S(1)}, u32[]{:S(2)}, u32[]{:S(2)}) collective-permute-start(f32[4096]{0:T(1024)S(1)} %slice.144), channel_id=1, source_target_pairs={{1,0},{2,1},{3,2},{4,3},{5,4},{6,5},{7,6},{8,7},{9,8},{10,9},{11,1... | collective-permute-start | bytes 49160 | tf_op jit(solution)/shard_map/ppermute | solution.py:1062
  20.2 6.5 %collective-permute-start.1 = (f32[1024]{0:T(1024)S(1)}, f32[1024]{0:T(1024)S(1)}, u32[]{:S(2)}, u32[]{:S(2)}) collective-permute-start(f32[1024]{0:T(1024)S(1)} %slice.143), channel_id=1, source_target_pairs={{0,1},{1,2},{2,3},{3,4},{4,5},{5,6},{6,7},{7,8},{8,9},{9,10},{10,1... | collective-permute-start | bytes 12296 | tf_op jit(solution)/shard_map/ppermute | solution.py:1061
  36.2 69.8 %copy-start.18 = (s32[2,64]{1,0:T(2,128)S(1)}, s32[2,64]{1,0:T(2,128)}, u32[]{:S(2)}) copy-start(s32[2,64]{1,0:T(2,128)} %param.14) | copy-start | bytes 1540
  106.7 9.6 %all-to-all-start.1 = ((s32[32,1,128]{2,1,0:T(1,128)}), s32[32,1,128]{2,1,0:T(1,128)S(1)}, u32[]{:S(2)}, u32[]{:S(2)}) async-start(s32[32,1,128]{2,1,0:T(1,128)} %broadcast_in_dim.40), calls=%async_computation.1 | async-start | bytes 32768 | tf_op jit(solution)/shard_map/all_to_all | solution.py:1048
  116.3 44.1 %all-to-all-start.2 = ((bf16[16,160,128]{2,1,0:T(8,128)(2,1)}), bf16[16,160,128]{2,1,0:T(8,128)(2,1)}, u32[]{:S(2)}, u32[]{:S(2)}) async-start(bf16[16,160,128]{2,1,0:T(8,128)(2,1)} %get-tuple-element.74), calls=%async_computation.2 | async-start | bytes 1310720 | tf_op jit(solution)/shard_map/all_to_all | solution.py:1101
  207.6 6.4 %collective-permute-start.7 = (bf16[8,2,64,1024]{3,2,1,0:T(8,128)(2,1)}, bf16[8,2,64,1024]{3,2,1,0:T(8,128)(2,1)}, u32[]{:S(2)}, u32[]{:S(2)}) collective-permute-start(bf16[8,2,64,1024]{3,2,1,0:T(8,128)(2,1)} %get-tuple-element.100), channel_id=1, source_target_pairs={{0,8},{8,0},{1,9},{9,1},{2,10},{10,2},{3,11},{11,3},{4,12},{12,4},... | collective-permute-start | bytes 6291464 | tf_op jit(solution)/shard_map/ppermute | solution.py:1117
  207.7 12.9 %collective-permute-start.3 = (bf16[8,2,64,1024]{3,2,1,0:T(8,128)(2,1)}, bf16[8,2,64,1024]{3,2,1,0:T(8,128)(2,1)S(1)}, u32[]{:S(2)}, u32[]{:S(2)}) collective-permute-start(bf16[8,2,64,1024]{3,2,1,0:T(8,128)(2,1)} %get-tuple-element.87), channel_id=1, source_target_pairs={{0,8},{8,0},{1,9},{9,1},{2,10},{10,2},{3,11},{11,3},{4,12},{12,4},... | collective-permute-start | bytes 6291464 | tf_op jit(solution)/shard_map/ppermute | solution.py:1117
  208.4 24.1 %all-to-all-start.3 = ((bf16[16,160,128]{2,1,0:T(8,128)(2,1)}), bf16[16,160,128]{2,1,0:T(8,128)(2,1)S(1)}, u32[]{:S(2)}, u32[]{:S(2)}) async-start(bf16[16,160,128]{2,1,0:T(8,128)(2,1)} %shard_map.124), calls=%async_computation.3 | async-start | bytes 1310720 | tf_op jit(solution)/shard_map/all_to_all | solution.py:1165
  218.7 30.8 %collective-permute-start.8 = (bf16[4,2,64,1024]{3,2,1,0:T(8,128)(2,1)}, bf16[4,2,64,1024]{3,2,1,0:T(8,128)(2,1)}, u32[]{:S(2)}, u32[]{:S(2)}) collective-permute-start(bf16[4,2,64,1024]{3,2,1,0:T(8,128)(2,1)} %get-tuple-element.112), channel_id=1, source_target_pairs={{0,1},{1,0},{2,3},{3,2},{4,5},{5,4},{6,7},{7,6},{8,9},{9,8},{10,11... | collective-permute-start | bytes 3145736 | tf_op jit(solution)/shard_map/ppermute | solution.py:1117
  225.5 62.4 %collective-permute-start.4 = (bf16[4,2,64,1024]{3,2,1,0:T(8,128)(2,1)}, bf16[4,2,64,1024]{3,2,1,0:T(8,128)(2,1)}, u32[]{:S(2)}, u32[]{:S(2)}) collective-permute-start(bf16[4,2,64,1024]{3,2,1,0:T(8,128)(2,1)} %get-tuple-element.114), channel_id=1, source_target_pairs={{0,1},{1,0},{2,3},{3,2},{4,5},{5,4},{6,7},{7,6},{8,9},{9,8},{10,11... | collective-permute-start | bytes 3145736 | tf_op jit(solution)/shard_map/ppermute | solution.py:1117
  238.2 104.4 %all-to-all-start.4 = ((bf16[32,224,128]{2,1,0:T(8,128)(2,1)}), bf16[32,224,128]{2,1,0:T(8,128)(2,1)S(1)}, u32[]{:S(2)}, u32[]{:S(2)}) async-start(bf16[32,224,128]{2,1,0:T(8,128)(2,1)} %shard_map.127), calls=%async_computation.4 | async-start | bytes 3670016 | tf_op jit(solution)/shard_map/all_to_all | solution.py:1196
  251.4 42.0 %copy-start.8 = (bf16[2,2,64,1024]{3,2,1,0:T(8,128)(2,1)}, bf16[2,2,64,1024]{3,2,1,0:T(8,128)(2,1)S(1)}, u32[]{:S(2)}) copy-start(bf16[2,2,64,1024]{3,2,1,0:T(8,128)(2,1)S(1)} %get-tuple-element.115) | copy-start | bytes 1572868
  251.4 41.9 %collective-permute-start.9 = (bf16[2,2,64,1024]{3,2,1,0:T(8,128)(2,1)S(1)}, bf16[2,2,64,1024]{3,2,1,0:T(8,128)(2,1)S(1)}, u32[]{:S(2)}, u32[]{:S(2)}) collective-permute-start(bf16[2,2,64,1024]{3,2,1,0:T(8,128)(2,1)S(1)} %get-tuple-element.116), channel_id=1, source_target_pairs={{0,2},{2,0},{4,6},{6,4},{1,3},{3,1},{5,7},{7,5},{8,10},{10,8},{12,... | collective-permute-start | bytes 1572872 | tf_op jit(solution)/shard_map/ppermute | solution.py:1117
  289.4 20.2 %copy-start.9 = (bf16[2,2,64,1024]{3,2,1,0:T(8,128)(2,1)}, bf16[2,2,64,1024]{3,2,1,0:T(8,128)(2,1)S(1)}, u32[]{:S(2)}) copy-start(bf16[2,2,64,1024]{3,2,1,0:T(8,128)(2,1)S(1)} %get-tuple-element.117) | copy-start | bytes 1572868
  289.5 20.2 %collective-permute-start.5 = (bf16[2,2,64,1024]{3,2,1,0:T(8,128)(2,1)S(1)}, bf16[2,2,64,1024]{3,2,1,0:T(8,128)(2,1)S(1)}, u32[]{:S(2)}, u32[]{:S(2)}) collective-permute-start(bf16[2,2,64,1024]{3,2,1,0:T(8,128)(2,1)S(1)} %get-tuple-element.118), channel_id=1, source_target_pairs={{0,2},{2,0},{4,6},{6,4},{1,3},{3,1},{5,7},{7,5},{8,10},{10,8},{12,... | collective-permute-start | bytes 1572872 | tf_op jit(solution)/shard_map/ppermute | solution.py:1117
  293.4 17.2 %collective-permute-start.10 = (bf16[1,2,64,1024]{3,2,1,0:T(8,128)(2,1)S(1)}, bf16[1,2,64,1024]{3,2,1,0:T(8,128)(2,1)S(1)}, u32[]{:S(2)}, u32[]{:S(2)}) collective-permute-start(bf16[1,2,64,1024]{3,2,1,0:T(8,128)(2,1)S(1)} %add_convert_fusion.9), channel_id=1, source_target_pairs={{0,4},{4,0},{2,6},{6,2},{1,5},{5,1},{3,7},{7,3},{8,12},{12,8},{10,... | collective-permute-start | bytes 786440 | tf_op jit(solution)/shard_map/ppermute | solution.py:1117
  309.7 13.6 %collective-permute-start.6 = (bf16[1,2,64,1024]{3,2,1,0:T(8,128)(2,1)S(1)}, bf16[1,2,64,1024]{3,2,1,0:T(8,128)(2,1)}, u32[]{:S(2)}, u32[]{:S(2)}) collective-permute-start(bf16[1,2,64,1024]{3,2,1,0:T(8,128)(2,1)S(1)} %add_convert_fusion.12), channel_id=1, source_target_pairs={{0,4},{4,0},{2,6},{6,2},{1,5},{5,1},{3,7},{7,3},{8,12},{12,8},{10,... | collective-permute-start | bytes 786440 | tf_op jit(solution)/shard_map/ppermute | solution.py:1117
  324.5 16.7 %collective-permute-start.11 = (bf16[2,64,1024]{2,1,0:T(8,128)(2,1)S(1)}, bf16[2,64,1024]{2,1,0:T(8,128)(2,1)S(1)}, u32[]{:S(2)}, u32[]{:S(2)}) collective-permute-start(bf16[2,64,1024]{2,1,0:T(8,128)(2,1)S(1)} %get-tuple-element.122), channel_id=1, source_target_pairs={{0,16},{16,0},{1,17},{17,1},{2,18},{18,2},{3,19},{19,3},{4,20},{20... | collective-permute-start | bytes 786440 | tf_op jit(solution)/shard_map/ppermute | solution.py:1023
  343.9 20.1 %copy-start.11 = (f32[393632]{0:T(1024)S(1)}, f32[393632]{0:T(1024)}, u32[]{:S(2)}) copy-start(f32[393632]{0:T(1024)} %param.16) | copy-start | bytes 4723588
  353.1 6.6 %collective-permute-start.12 = (f32[4096]{0:T(1024)S(1)}, f32[4096]{0:T(1024)S(1)}, u32[]{:S(2)}, u32[]{:S(2)}) collective-permute-start(f32[4096]{0:T(1024)S(1)} %slice.206), channel_id=1, source_target_pairs={{0,1},{1,2},{2,3},{3,4},{4,5},{5,6},{6,7},{7,8},{8,9},{9,10},{10,1... | collective-permute-start | bytes 49160 | tf_op jit(solution)/shard_map/ppermute | solution.py:1203
  358.4 5.5 %collective-permute-start.13 = (f32[1024]{0:T(1024)S(1)}, f32[1024]{0:T(1024)S(1)}, u32[]{:S(2)}, u32[]{:S(2)}) collective-permute-start(f32[1024]{0:T(1024)S(1)} %slice_bitcast_fusion.4), channel_id=1, source_target_pairs={{1,0},{2,1},{3,2},{4,3},{5,4},{6,5},{7,6},{8,7},{9,8},{10,9},{11,1... | collective-permute-start | bytes 12296 | tf_op jit(solution)/shard_map/ppermute | solution.py:1204
  (16 other events, 120.9 us)
Sparse Core Ops, SparseCore 0:
  18.8 73.2 all-gather.4
  106.1 53.5 all-gather.6
